TPU v7x, 32 devices: a whole 2x2x4 slice. The times are simulated.
32 devices in a mesh: var: 4 (over z), lat: 2 (over y), lon: 4 (over x, core).
Axes of the slice: x: 2, y: 2, z: 4, core: 2. Of those that a mesh axis runs over, the one named last changes fastest.
Arguments:
- var_tokens: bfloat16 [128, 12, 96, 1024], P(('var', 'lon'), 'lat'), may hold values from -6 to 6
- var_query: float32 [16, 64], replicated, may hold values from -80 to 80
- agg_key: bfloat16 [1024, 1024], replicated, may hold values from -0.1875 to 0.1875
- agg_value: bfloat16 [1024, 1024], replicated, may hold values from -0.1875 to 0.1875
- agg_out: bfloat16 [1024, 1024], replicated, may hold values from -0.1875 to 0.1875
- norm_gain: float32 [1024], replicated, may hold values from 0.25 to 1.75
- nb_query: bfloat16 [1024, 1024], replicated, may hold values from -0.1875 to 0.1875
- nb_key: bfloat16 [1024, 1024], replicated, may hold values from -0.1875 to 0.1875
- nb_value: bfloat16 [1024, 1024], replicated, may hold values from -0.1875 to 0.1875
- nb_out: bfloat16 [1024, 1024], replicated, may hold values from -0.1875 to 0.1875
- pos_bias: float32 [16, 13, 13], replicated, may hold values from -120 to 120
- valid: int32 [12, 96], replicated, may hold values 0 or 1
Outputs:
- layer_out: bfloat16 [12, 96, 1024], P('lat', ('var', 'lon'))
Inputs may be any that keep to these rules, and one draw needn't show every extreme that they name: `valid`: a patch always attends to itself.
All inputs are finite; a program needn't handle non-finite values.
Results may differ from a plain program's by a relative error of at most 0.015.
Values may be sent and summed in bfloat16 or wider, within the bound.
No kernel may reach another device: no remote copies, remote signals or barrier semaphores. Data moves between devices by JAX's collectives and lax.ppermute only.
A program may use at most 128 MiB of HBM per device.

v0:
```python
import functools
import math

import jax
import jax.numpy as jnp
import numpy as np
from jax import lax
from jax.experimental import pallas as pl
from jax.experimental.pallas import tpu as pltpu
from jax.sharding import PartitionSpec as P

HALF = 6
EPS = 1e-05
LANES = 128
TILE_BLOCKS = 16
RADICES = (2, 2, 4)
CHUNKS = 2
QROWS = 48
MIB = 1 << 20
F32 = jnp.float32
BF16 = jnp.bfloat16


def dot(a, b):
    return jnp.dot(a, b, preferred_element_type=F32)


def dot_nt(a, b):
    return lax.dot_general(a, b, (((1,), (1,)), ((), ())), preferred_element_type=F32)


def split3(x):
    hi = x.astype(BF16)
    rest = x - hi.astype(F32)
    mid = rest.astype(BF16)
    low = (rest - mid.astype(F32)).astype(BF16)
    return hi.astype(F32), mid.astype(F32), low.astype(F32)


def lane_iota(shape):
    return lax.broadcasted_iota(jnp.int32, shape, len(shape) - 1)


def pack3(x, heads):
    hi, mid, low = split3(x)
    lane = lane_iota(x.shape)
    mid = pltpu.roll(mid, heads, 1)
    low = pltpu.roll(low, 2 * heads, 1)
    out = jnp.where(lane < heads, hi, jnp.where(lane < 2 * heads, mid, low))
    return jnp.where(lane < 3 * heads, out, 0.0)


def unpack3(x, heads):
    return x + pltpu.roll(x, LANES - heads, 1) + pltpu.roll(x, LANES - 2 * heads, 1)


def expander(heads, width):
    head_dim = width // heads
    row = lax.broadcasted_iota(jnp.int32, (LANES, width), 0)
    lane = lax.broadcasted_iota(jnp.int32, (LANES, width), 1)
    hit = jnp.zeros((LANES, width), F32)
    for piece in range(3):
        low = (row - piece * heads) * head_dim
        inside = (row >= piece * heads) & (row < (piece + 1) * heads)
        hit = jnp.where(inside & (lane >= low) & (lane < low + head_dim), 1.0, hit)
    return hit.astype(BF16)


def encode_stats(top, total, heads):
    return pack3(top, heads) + pltpu.roll(pack3(total, heads), 3 * heads, 1)


def fold_kernel(scale, query_ref, key_ref, out_ref):
    heads, head_dim = query_ref.shape
    width = key_ref.shape[0]
    query = query_ref[...] * scale
    wide = jnp.concatenate([query] * (width // head_dim), axis=1)
    row = lax.broadcasted_iota(jnp.int32, wide.shape, 0)
    lane = lax.broadcasted_iota(jnp.int32, wide.shape, 1)
    own = (lane >= row * head_dim) & (lane < (row + 1) * head_dim)
    pieces = jnp.concatenate(split3(jnp.where(own, wide, 0.0)), axis=0).astype(BF16)
    folded = dot_nt(pieces, key_ref[...])
    folded = folded[:heads] + folded[heads : 2 * heads] + folded[2 * heads :]
    parts = jnp.concatenate(
        list(split3(folded)) + [jnp.zeros((LANES - 3 * heads, width), F32)], axis=0
    )
    out_ref[...] = parts.T.astype(BF16)


def pool_kernel(heads, place_ref, token_ref, fold_ref, value_ref, keep_ref, send_ref):
    variables, _, columns, width = token_ref.shape
    tokens = token_ref[:, 0].reshape(variables * columns, width)
    score = unpack3(dot(tokens, fold_ref[...]), heads)
    score = score.reshape(variables, columns, LANES)
    top = jnp.max(score, axis=0)
    raised = jnp.exp(score - top[None])
    total = jnp.sum(raised, axis=0)
    share = pack3(raised.reshape(variables * columns, LANES), heads).astype(BF16)
    spread = expander(heads, width)
    step = 256
    pooled = []
    for start in range(0, width, step):
        rows = dot(tokens, value_ref[:, start : start + step])
        rows = rows * dot(share, spread[:, start : start + step])
        pooled.append(jnp.sum(rows.reshape(variables, columns, step), axis=0).astype(BF16))
    pooled.append(encode_stats(top, total, heads).astype(BF16))
    packed = jnp.concatenate(pooled, axis=1)
    source = lax.broadcasted_iota(jnp.int32, (columns, columns), 1)
    target = jnp.broadcast_to(place_ref[...], (columns, columns))
    chosen = jnp.where(source == target, 1.0, 0.0).astype(BF16)
    ordered = dot(chosen, packed).astype(BF16)
    half = columns // RADICES[0]
    keep_ref[0, 0] = ordered[:half]
    send_ref[0, 0] = ordered[half:]


def merge_body(parts, heads, width, last):
    stats = [unpack3(part[:, width:].astype(F32), heads) for part in parts]
    top = functools.reduce(jnp.maximum, stats)
    scales = [jnp.exp(stat - top) for stat in stats]
    totals = [pltpu.roll(stat, LANES - 3 * heads, 1) for stat in stats]
    total = sum(scale * amount for scale, amount in zip(scales, totals))
    lane = lane_iota(total.shape)
    total = jnp.where(lane < heads, total, 1.0)
    if last:
        scales = [scale / total for scale in scales]
    spread = expander(heads, width)
    merged = sum(
        dot(pack3(scale, heads).astype(BF16), spread) * part[:, :width].astype(F32)
        for scale, part in zip(scales, parts)
    ).astype(BF16)
    if last:
        return merged
    stat = encode_stats(top, total, heads).astype(BF16)
    return jnp.concatenate([merged, stat], axis=1)


def merge_kernel(heads, width, count, last, *refs):
    parts = [ref[...] for ref in refs[:count]]
    flat = [part.reshape(-1, part.shape[-1]) for part in parts]
    merged = merge_body(flat, heads, width, last)
    outs = refs[count:]
    if last:
        outs[0][...] = merged
        return
    if len(outs[0].shape) == 3:
        groups, size, _ = outs[0].shape
        merged = merged.reshape(groups, size * len(outs), merged.shape[-1])
        for at, out in enumerate(outs):
            out[...] = merged[:, at * size : (at + 1) * size]
    else:
        groups = parts[0].shape[0]
        size = outs[0].shape[0] // groups
        merged = merged.astype(F32)
        for group in range(groups):
            for at, out in enumerate(outs):
                low = (group * len(outs) + at) * size
                out[group * size : (group + 1) * size] = merged[low : low + size].astype(BF16)


def merge(parts, shapes, heads, width, last):
    rows = sum(math.prod(part.shape[:-1]) for part in parts)
    return pl.pallas_call(
        functools.partial(merge_kernel, heads, width, len(parts), last),
        out_shape=[jax.ShapeDtypeStruct(shape, BF16) for shape in shapes],
        compiler_params=pltpu.CompilerParams(vmem_limit_bytes=48 * MIB),
        cost_estimate=pl.CostEstimate(
            flops=rows * LANES * width * 2,
            bytes_accessed=rows * width * 4,
            transcendentals=rows * LANES,
        ),
        name="merge",
    )(*parts)


def bias_kernel(columns, side_ref, meta_ref, allowed_ref, table_ref, out_ref):
    heads, span2 = table_ref.shape
    span = 2 * HALF + 1
    keys = meta_ref.shape[1]
    hi, mid, low = split3(table_ref[...])
    pieces = jnp.concatenate([hi, mid, low], axis=0).astype(BF16)
    row_at = meta_ref[0:1] + meta_ref[1:2] * side_ref[0]
    column_at = meta_ref[2:3]
    allowed = allowed_ref[...] > 0
    out_ref[...] = jnp.zeros(out_ref.shape, F32)
    place = lax.broadcasted_iota(jnp.int32, (span2, keys), 0)
    for row in range(HALF):
        for column in range(columns):
            up = row_at - row + HALF
            across = column_at - column + HALF
            inside = (up >= 0) & (up < span) & (across >= 0) & (across < span)
            index = jnp.where(inside, up * span + across, -1)
            hot = jnp.where(place == index, 1.0, 0.0).astype(BF16)
            found = dot(pieces, hot)
            found = found[:heads] + found[heads : 2 * heads] + found[2 * heads :]
            center = index == HALF * span + HALF
            kept = (inside & allowed) | center
            out_ref[:, row * columns + column, :] = jnp.where(kept, found, -jnp.inf)


def attend_kernel(heads, count, *refs):
    blocks = refs[:count]
    gain_ref, bias_ref = refs[count : count + 2]
    sources = refs[count + 2 : count + 7]
    out_ref = refs[count + 7]
    window, mix, *held = refs[count + 8 : count + 15]
    sems = refs[count + 15]
    copies = [
        pltpu.make_async_copy(source, target, sems.at[at])
        for at, (source, target) in enumerate(zip(sources, held))
    ]
    for copy in copies:
        copy.start()
    w_agg, w_query, w_key, w_value, w_out = held
    size, width = blocks[0].shape
    scale = 1.0 / math.sqrt(width // heads)
    for at, block in enumerate(blocks):
        window[at * size : (at + 1) * size] = block[...]
    copies[0].wait()
    tokens = dot(window[...], w_agg[...]).astype(BF16)
    values = tokens.astype(F32)
    center = values - jnp.mean(values, axis=-1, keepdims=True)
    variance = jnp.mean(center * center, axis=-1, keepdims=True)
    normed = (center * lax.rsqrt(variance + EPS) * gain_ref[...]).astype(BF16)
    copies[1].wait()
    queries = dot(normed[:QROWS], w_query[...]).astype(BF16)
    copies[2].wait()
    keys = dot(normed, w_key[...]).astype(BF16)
    copies[3].wait()
    values = dot(normed, w_value[...]).astype(BF16)
    lane = lane_iota((QROWS, LANES))
    left = lane < LANES // 2
    for pair in range(heads // 2):
        at = slice(pair * LANES, (pair + 1) * LANES)
        query = queries[:, at]
        zero = jnp.zeros_like(query)
        both = jnp.concatenate([jnp.where(left, query, zero), jnp.where(left, zero, query)], axis=0)
        logit = dot_nt(both, keys[:, at]) * scale
        bias = bias_ref[2 * pair : 2 * pair + 2]
        logit = logit + bias.reshape(2 * QROWS, bias.shape[-1])
        raised = jnp.exp(logit - jnp.max(logit, axis=-1, keepdims=True))
        attn = (raised / jnp.sum(raised, axis=-1, keepdims=True)).astype(BF16)
        mixed = dot(attn, values[:, at])
        mix[:, at] = jnp.where(left, mixed[:QROWS], mixed[QROWS:]).astype(BF16)
    copies[4].wait()
    result = tokens[:QROWS].astype(F32) + dot(mix[...], w_out[...])
    out_ref[...] = result[:size].astype(BF16)


def on_device(
    sizes,
    var_tokens,
    var_query,
    agg_key,
    agg_value,
    agg_out,
    norm_gain,
    nb_query,
    nb_key,
    nb_value,
    nb_out,
    pos_bias,
    valid,
):
    heads, head_dim = var_query.shape
    width = agg_key.shape[0]
    local_vars, rows, total_columns, _ = var_tokens.shape
    n_var, n_lat, n_lon = sizes
    devices = n_var * n_lon
    columns = total_columns // devices
    tile = TILE_BLOCKS * columns
    tiles = devices // TILE_BLOCKS
    packed = width + LANES
    lat = lax.axis_index("lat")
    block = lax.axis_index("var") * n_lon + lax.axis_index("lon")

    digits = []
    stride = 1
    for radix in RADICES:
        digits.append((stride, radix))
        stride *= radix
    at = np.arange(tile) // columns
    wanted = jnp.zeros((tile,), jnp.int32)
    weight = TILE_BLOCKS
    for stride, radix in digits:
        weight //= radix
        relative = jnp.asarray((at // weight) % radix, jnp.int32)
        wanted = wanted + ((relative + block // stride) % radix) * stride
    wanted = wanted * columns + jnp.asarray(np.arange(tile) % columns, jnp.int32)
    place = jnp.broadcast_to(wanted[:, None], (tile, 1))
    high = (block // TILE_BLOCKS).astype(jnp.int32).reshape(1)

    folded = pl.pallas_call(
        functools.partial(fold_kernel, 1.0 / math.sqrt(head_dim)),
        out_shape=jax.ShapeDtypeStruct((width, LANES), BF16),
        compiler_params=pltpu.CompilerParams(vmem_limit_bytes=32 * MIB),
        name="fold",
    )(var_query, agg_key)

    half = tile // RADICES[0]
    per_chunk = rows // CHUNKS

    def pool(chunk):
        def kernel(high_ref, *refs):
            pool_kernel(heads, *refs)

        def out_map(r, t, high_ref):
            return (r, lax.rem(t + tiles - high_ref[0], tiles), 0, 0)

        shape = jax.ShapeDtypeStruct((per_chunk, tiles, half, packed), BF16)
        keep, send = pl.pallas_call(
            kernel,
            grid_spec=pltpu.PrefetchScalarGridSpec(
                num_scalar_prefetch=1,
                grid=(per_chunk, tiles),
                in_specs=[
                    pl.BlockSpec((tile, 1), lambda r, t, h: (0, 0)),
                    pl.BlockSpec(
                        (local_vars, 1, tile, width),
                        lambda r, t, h: (0, chunk * per_chunk + r, t, 0),
                    ),
                    pl.BlockSpec((width, LANES), lambda r, t, h: (0, 0)),
                    pl.BlockSpec((width, width), lambda r, t, h: (0, 0)),
                ],
                out_specs=[pl.BlockSpec((1, 1, half, packed), out_map)] * 2,
            ),
            out_shape=[shape, shape],
            compiler_params=pltpu.CompilerParams(vmem_limit_bytes=56 * MIB),
            cost_estimate=pl.CostEstimate(
                flops=3 * per_chunk * total_columns * local_vars * width * width,
                bytes_accessed=2 * per_chunk * total_columns * local_vars * width,
                transcendentals=per_chunk * total_columns * local_vars * LANES,
            ),
            name="pool",
        )(high, place, var_tokens, folded, agg_value)
        flat = (per_chunk * tiles, half, packed)
        return keep.reshape(flat), send.reshape(flat)

    def exchange(array, shift, stride, radix):
        def moved(i):
            digit = (i // stride) % radix
            return i + ((digit + shift) % radix - digit) * stride

        return lax.ppermute(array, ("var", "lon"), [(i, moved(i)) for i in range(devices)])

    stages = [(stride, radix) for stride, radix in digits]
    if tiles > 1:
        stages.append((TILE_BLOCKS, tiles))

    def reduce_scatter(keep, sends):
        groups = per_chunk * tiles
        size = half
        for number, (stride, radix) in enumerate(stages):
            got = [exchange(s, k + 1, stride, radix) for k, s in enumerate(sends)]
            parts = [keep] + got
            if number + 1 == len(stages):
                rows_left = math.prod(keep.shape[:-1])
                (out,) = merge(parts, [(rows_left, width)], heads, width, True)
                return out
            following = stages[number + 1][1]
            if number + 2 < len(stages) and number + 1 < len(RADICES):
                size //= following
                if size % 8 == 0:
                    shape = (groups, size, packed)
                else:
                    shape = (groups * size, packed)
                outs = merge(parts, [shape] * following, heads, width, False)
            elif number + 1 < len(RADICES):
                size //= following
                shape = (groups * size, packed)
                outs = merge(parts, [shape] * following, heads, width, False)
            else:
                (full,) = merge_whole(parts, heads, width)
                full = full.reshape(per_chunk, tiles, size, packed)
                outs = [full[:, k].reshape(per_chunk * size, packed) for k in range(tiles)]
            keep, sends = outs[0], list(outs[1:])

    def merge_whole(parts, heads, width):
        shape = (math.prod(parts[0].shape[:-1]), packed)
        parts = [part.reshape((1,) + shape) for part in parts]
        return merge(parts, [(1,) + shape], heads, width, False)

    chunks = []
    for chunk in range(CHUNKS):
        keep, send = pool(chunk)
        chunks.append(reduce_scatter(keep, [send]))
    pooled = jnp.concatenate(chunks, axis=0) if CHUNKS > 1 else chunks[0]

    places = [(dl, dx) for dx in (0, -1, 1) for dl in (0, 1)]

    def neighbour(array, dl, dx):
        pairs = []
        for i in range(n_var * n_lat * n_lon):
            v, l, o = i // (n_lat * n_lon), (i // n_lon) % n_lat, i % n_lon
            b = (v * n_lon + o + dx) % devices
            source = ((b // n_lon) * n_lat + (l + dl) % n_lat) * n_lon + b % n_lon
            pairs.append((source, i))
        return lax.ppermute(array, ("var", "lat", "lon"), pairs)

    window = [pooled] + [neighbour(pooled, dl, dx) for dl, dx in places[1:]]

    patch = rows * columns
    dl = np.repeat([p[0] for p in places], patch)
    dx = np.repeat([p[1] for p in places], patch)
    row = np.tile(np.repeat(np.arange(rows), columns), len(places))
    column = np.tile(np.arange(columns), len(places) * rows)
    meta = jnp.asarray(np.stack([row, dl, dx * columns + column]), jnp.int32)
    side = jnp.where(lat == 0, rows, -rows).astype(jnp.int32)
    row_ids = lat * rows + meta[0] + meta[1] * side
    column_ids = (block * columns + meta[2]) % total_columns
    allowed = jnp.take(valid.reshape(-1), row_ids * total_columns + column_ids)[None, :]
    keys = len(places) * patch
    bias = pl.pallas_call(
        functools.partial(bias_kernel, columns),
        in_specs=[
            pl.BlockSpec(memory_space=pltpu.SMEM),
            pl.BlockSpec(memory_space=pltpu.VMEM),
            pl.BlockSpec(memory_space=pltpu.VMEM),
            pl.BlockSpec(memory_space=pltpu.VMEM),
        ],
        out_shape=jax.ShapeDtypeStruct((heads, QROWS, keys), F32),
        name="bias",
    )(side.reshape(1), meta, allowed, pos_bias.reshape(heads, -1))

    vmem = pl.BlockSpec(memory_space=pltpu.VMEM)
    square = pltpu.VMEM((width, width), BF16)
    out = pl.pallas_call(
        functools.partial(attend_kernel, heads, len(window)),
        in_specs=[vmem] * (len(window) + 2) + [pl.BlockSpec(memory_space=pl.ANY)] * 5,
        out_specs=vmem,
        out_shape=jax.ShapeDtypeStruct((patch, width), BF16),
        scratch_shapes=[
            pltpu.VMEM((keys, width), BF16),
            pltpu.VMEM((QROWS, width), BF16),
            square,
            square,
            square,
            square,
            square,
            pltpu.SemaphoreType.DMA((5,)),
        ],
        compiler_params=pltpu.CompilerParams(vmem_limit_bytes=48 * MIB),
        name="attend",
    )(*window, norm_gain.reshape(1, width), bias, agg_out, nb_query, nb_key, nb_value, nb_out)
    return out.reshape(rows, columns, width)


def solution(mesh):
    sizes = (mesh.shape["var"], mesh.shape["lat"], mesh.shape["lon"])
    return jax.shard_map(
        functools.partial(on_device, sizes),
        mesh=mesh,
        in_specs=(P(("var", "lon"), "lat", None, None),) + (P(),) * 11,
        out_specs=P("lat", ("var", "lon"), None),
        check_vma=False,
    )
```

profile of v0, /device:TPU:0, one launch (start us, length us, event | category | flops | bytes accessed | tf_op | source)
XLA Modules:
  0.0 74.3 jit_solution(16089414615754300339)
XLA Ops:
  0.0 0.7 fusion.11
  0.7 0.7 copy.21.refs_0_
  1.4 1.6 %copy-done.1 = bf16[1024,1024]{1,0:T(8,128)(2,1)S(1)} copy-done((bf16[1024,1024]{1,0:T(8,128)(2,1)S(1)}, bf16[1024,1024]{1,0:T(8,128)(2,1)}, u32[]{:S(2)}) %copy-start.1) | copy-done | bytes 2097176
  3.0 0.7 copy-done.7
  3.7 0.8 %fold.1.refs_2_ = bf16[1024,128]{1,0:T(8,128)(2,1)S(1)} custom-call(f32[16,64]{1,0:T(8,128)S(1)} %copy-done.7, bf16[1024,1024]{1,0:T(8,128)(2,1)S(1)} %copy-done.1), custom_call_target="tpu_custom_call" | custom-call | tf_op jit(solution)/shard_map/fold/pallas_call | solution.py:293
  4.6 0.0 copy-start.6
  4.6 0.7 copy-done.6
  5.3 11.5 %pool.3 = (bf16[3,1,48,1152]{3,2,1,0:T(8,128)(2,1)}, bf16[3,1,48,1152]{3,2,1,0:T(8,128)(2,1)}) custom-call(s32[1]{0:T(128)} %bitcast.high_ref, s32[96,1]{1,0:T(8,128)} %copy.21.refs_0_, bf16[8,6,96,1024]{3,2,1,0:T(8,128)(2,1)} %refs_1_.3, bf16[1024,128]{1,0:T(8,128)(2,1)} %copy-done.6, bf16[1024,1024]{1,0:T(8,128)(2,1)} %refs_3_.3), custom_call_target="tpu_custom_call" | custom-call | flops 7247757312 | bytes 4718592 | tf_op jit(solution)/shard_map/pool/pallas_call | solution.py:311
  16.8 0.0 copy-start.13
  16.8 0.0 copy-start.10
  16.8 0.5 collective-permute-start.5
  17.4 11.5 %pool.2 = (bf16[3,1,48,1152]{3,2,1,0:T(8,128)(2,1)}, bf16[3,1,48,1152]{3,2,1,0:T(8,128)(2,1)}) custom-call(s32[1]{0:T(128)} %bitcast.high_ref, s32[96,1]{1,0:T(8,128)} %copy.21.refs_0_, bf16[8,6,96,1024]{3,2,1,0:T(8,128)(2,1)} %refs_1_.3, bf16[1024,128]{1,0:T(8,128)(2,1)} %copy-done.6, bf16[1024,1024]{1,0:T(8,128)(2,1)} %refs_3_.3), custom_call_target="tpu_custom_call" | custom-call | flops 7247757312 | bytes 4718592 | tf_op jit(solution)/shard_map/pool/pallas_call | solution.py:311
  28.9 0.1 collective-permute-start
  28.9 0.0 collective-permute-done.5.refs_1_
  28.9 0.0 copy-done.5
  29.0 0.5 merge.9
  29.5 3.0 %collective-permute-start.6 = (bf16[3,24,1152]{2,1,0:T(8,128)(2,1)S(1)}, bf16[3,24,1152]{2,1,0:T(8,128)(2,1)S(1)}, u32[]{:S(2)}, u32[]{:S(2)}) collective-permute-start(bf16[3,24,1152]{2,1,0:T(8,128)(2,1)S(1)} %get-tuple-element.32), channel_id=1, source_target_pairs={{0,2},{1,3},{2,0},{3,1},{8,10},{9,11},{10,8},{11,9},{16,18},{17,19... | collective-permute-start | bytes 497672 | tf_op jit(solution)/shard_map/ppermute | solution.py:344
  32.5 0.0 collective-permute-done.refs_1_
  32.5 1.0 %copy-done.4 = bf16[3,1,48,1152]{3,2,1,0:T(8,128)(2,1)S(1)} copy-done((bf16[3,1,48,1152]{3,2,1,0:T(8,128)(2,1)S(1)}, bf16[3,1,48,1152]{3,2,1,0:T(8,128)(2,1)}, u32[]{:S(2)}) %copy-start.4) | copy-done | bytes 331800
  33.5 0.5 merge.6
  34.0 0.9 %collective-permute-start.1 = (bf16[3,24,1152]{2,1,0:T(8,128)(2,1)S(1)}, bf16[3,24,1152]{2,1,0:T(8,128)(2,1)S(1)}, u32[]{:S(2)}, u32[]{:S(2)}) collective-permute-start(bf16[3,24,1152]{2,1,0:T(8,128)(2,1)S(1)} %get-tuple-element.24), channel_id=1, source_target_pairs={{0,2},{1,3},{2,0},{3,1},{8,10},{9,11},{10,8},{11,9},{16,18},{17,19... | collective-permute-start | bytes 497672 | tf_op jit(solution)/shard_map/ppermute | solution.py:344
  34.9 2.5 %collective-permute-done.6.refs_1_ = bf16[3,24,1152]{2,1,0:T(8,128)(2,1)S(1)} collective-permute-done((bf16[3,24,1152]{2,1,0:T(8,128)(2,1)S(1)}, bf16[3,24,1152]{2,1,0:T(8,128)(2,1)S(1)}, u32[]{:S(2)}, u32[]{:S(2)}) %collective-permute-start.6) | collective-permute-done | bytes 165920 | tf_op jit(solution)/shard_map/ppermute | solution.py:344
  37.4 0.4 merge.10
  37.8 2.1 %collective-permute-start.7 = (bf16[18,1152]{1,0:T(8,128)(2,1)S(1)}, bf16[18,1152]{1,0:T(8,128)(2,1)S(1)}, u32[]{:S(2)}, u32[]{:S(2)}) collective-permute-start(bf16[18,1152]{1,0:T(8,128)(2,1)S(1)} %get-tuple-element.34), channel_id=1, source_target_pairs={{0,8},{1,9},{2,10},{3,11},{8,16},{9,17},{10,18},{11,19},{16,24},{1... | collective-permute-start | bytes 124424 | tf_op jit(solution)/shard_map/ppermute | solution.py:344
  40.0 0.0 copy-done.11
  40.0 0.0 copy-done.12
  40.0 0.0 copy-done.13
  40.0 2.7 %collective-permute-start.8 = (bf16[18,1152]{1,0:T(8,128)(2,1)S(1)}, bf16[18,1152]{1,0:T(8,128)(2,1)S(1)}, u32[]{:S(2)}, u32[]{:S(2)}) collective-permute-start(bf16[18,1152]{1,0:T(8,128)(2,1)S(1)} %get-tuple-element.35), channel_id=1, source_target_pairs={{0,16},{1,17},{2,18},{3,19},{8,24},{9,25},{10,26},{11,27},{16,0},{... | collective-permute-start | bytes 124424 | tf_op jit(solution)/shard_map/ppermute | solution.py:344
  42.7 1.3 %collective-permute-start.9 = (bf16[18,1152]{1,0:T(8,128)(2,1)S(1)}, bf16[18,1152]{1,0:T(8,128)(2,1)S(1)}, u32[]{:S(2)}, u32[]{:S(2)}) collective-permute-start(bf16[18,1152]{1,0:T(8,128)(2,1)S(1)} %get-tuple-element.36), channel_id=1, source_target_pairs={{0,24},{1,25},{2,26},{3,27},{8,0},{9,1},{10,2},{11,3},{16,8},{17,9... | collective-permute-start | bytes 124424 | tf_op jit(solution)/shard_map/ppermute | solution.py:344
  44.0 0.0 collective-permute-done.1.refs_1_
  44.0 0.4 merge.7
  44.4 0.7 collective-permute-start.2
  45.2 0.3 collective-permute-start.3
  45.5 0.0 collective-permute-done.7.refs_1_
  45.5 2.8 %collective-permute-start.4 = (bf16[18,1152]{1,0:T(8,128)(2,1)S(1)}, bf16[18,1152]{1,0:T(8,128)(2,1)S(1)}, u32[]{:S(2)}, u32[]{:S(2)}) collective-permute-start(bf16[18,1152]{1,0:T(8,128)(2,1)S(1)} %get-tuple-element.28), channel_id=1, source_target_pairs={{0,24},{1,25},{2,26},{3,27},{8,0},{9,1},{10,2},{11,3},{16,8},{17,9... | collective-permute-start | bytes 124424 | tf_op jit(solution)/shard_map/ppermute | solution.py:344
  48.3 0.0 copy-done.10
  48.3 0.1 reshape.125
  48.4 1.7 %gather_fusion = s32[216]{0:T(256)S(1)} fusion(s32[1152]{0:T(1024)S(1)} %reshape.125, s32[1024]{0:T(1024)S(1)} %pad_clamp_fusion), kind=kCustom, calls=%fused_computation | custom fusion | bytes 2592 | tf_op jit(solution)/shard_map/jit(_take)/gather | solution.py:411
  50.1 0.0 collective-permute-done.8.refs_2_
  50.1 0.0 collective-permute-done.9.refs_3_
  50.1 0.4 merge.11
  50.6 0.0 collective-permute-done.2.refs_1_
  50.6 0.8 %collective-permute-done.3.refs_2_ = bf16[18,1152]{1,0:T(8,128)(2,1)S(1)} collective-permute-done((bf16[18,1152]{1,0:T(8,128)(2,1)S(1)}, bf16[18,1152]{1,0:T(8,128)(2,1)S(1)}, u32[]{:S(2)}, u32[]{:S(2)}) %collective-permute-start.3) | collective-permute-done | bytes 41504 | tf_op jit(solution)/shard_map/ppermute | solution.py:344
  51.4 0.0 collective-permute-done.4.refs_3_
  51.4 0.4 merge.8
  51.9 2.4 %collective-permute-start.14 = (bf16[36,1024]{1,0:T(8,128)(2,1)S(1)}, bf16[36,1024]{1,0:T(8,128)(2,1)S(1)}, u32[]{:S(2)}, u32[]{:S(2)}) collective-permute-start(bf16[36,1024]{1,0:T(8,128)(2,1)S(1)} %pad_maximum_fusion.refs_0_), channel_id=1, source_target_pairs={{5,0},{6,1},{7,2},{12,3},{1,4},{2,5},{3,6},{8,7},{13,8},{14,9},{15... | collective-permute-start | bytes 221192 | tf_op jit(solution)/shard_map/ppermute | solution.py:398
  54.3 2.7 %collective-permute-start.13 = (bf16[36,1024]{1,0:T(8,128)(2,1)S(1)}, bf16[36,1024]{1,0:T(8,128)(2,1)S(1)}, u32[]{:S(2)}, u32[]{:S(2)}) collective-permute-start(bf16[36,1024]{1,0:T(8,128)(2,1)S(1)} %pad_maximum_fusion.refs_0_), channel_id=1, source_target_pairs={{1,0},{2,1},{3,2},{8,3},{5,4},{6,5},{7,6},{12,7},{9,8},{10,9},{11,... | collective-permute-start | bytes 221192 | tf_op jit(solution)/shard_map/ppermute | solution.py:398
  57.0 0.0 collective-permute-start.12
  57.0 0.0 collective-permute-start.11
  57.0 0.5 collective-permute-start.10
  57.5 0.6 and_select_fusion.1.allowed_ref
  58.1 0.7 reshape.126.table_ref
  58.8 2.8 %bias.1.refs_7_ = f32[16,48,216]{2,1,0:T(8,128)} custom-call(s32[1]{0:T(128)} %bitcast.7.side_ref, s32[3,216]{1,0:T(4,128)} %constant.130.clone.meta_ref, s32[1,216]{1,0:T(1,128)} %and_select_fusion.1.allowed_ref, f32[16,169]{1,0:T(8,128)} %reshape.126.table_ref), custom_call_target="tpu_custom_call" | custom-call | tf_op jit(solution)/shard_map/bias/pallas_call | solution.py:413
  61.6 0.0 collective-permute-done.14.refs_5_
  61.6 0.0 collective-permute-done.13.refs_4_
  61.6 2.8 %collective-permute-done.12.refs_3_ = bf16[36,1024]{1,0:T(8,128)(2,1)S(1)} collective-permute-done((bf16[36,1024]{1,0:T(8,128)(2,1)S(1)}, bf16[36,1024]{1,0:T(8,128)(2,1)S(1)}, u32[]{:S(2)}, u32[]{:S(2)}) %collective-permute-start.12) | collective-permute-done | bytes 73760 | tf_op jit(solution)/shard_map/ppermute | solution.py:398
  64.4 0.0 collective-permute-done.11.refs_2_
  64.4 0.0 collective-permute-done.10.refs_1_
  64.5 0.0 copy-done.8
  64.5 0.0 copy-start
  64.5 1.1 %copy-done = f32[16,48,216]{2,1,0:T(8,128)S(1)} copy-done((f32[16,48,216]{2,1,0:T(8,128)S(1)}, f32[16,48,216]{2,1,0:T(8,128)}, u32[]{:S(2)}) %copy-start) | copy-done | bytes 663576
  65.6 1.6 %copy-done.3 = bf16[1024,1024]{1,0:T(8,128)(2,1)S(1)} copy-done((bf16[1024,1024]{1,0:T(8,128)(2,1)S(1)}, bf16[1024,1024]{1,0:T(8,128)(2,1)}, u32[]{:S(2)}) %copy-start.3) | copy-done | bytes 2097176
  67.2 6.4 %attend.1 = bf16[36,1024]{1,0:T(8,128)(2,1)S(1)} custom-call(bf16[36,1024]{1,0:T(8,128)(2,1)S(1)} %pad_maximum_fusion.refs_0_, bf16[36,1024]{1,0:T(8,128)(2,1)S(1)} %collective-permute-done.10.refs_1_, bf16[36,1024]{1,0:T(8,128)(2,1)S(1)} %collective-permute-done.11.refs_2_, bf16[36,1024]{1,0:T(8,128)(2,1)S(1)} %collective-permute-done.12.refs_3_, ...), custom_call_target="tpu_custom_call" | custom-call | tf_op jit(solution)/shard_map/attend/pallas_call | solution.py:427
  73.6 0.7 reshape.127
  (16 shorter events, 0.1 us)
Async XLA Ops:
  1.4 1.6 %copy-start.1 = (bf16[1024,1024]{1,0:T(8,128)(2,1)S(1)}, bf16[1024,1024]{1,0:T(8,128)(2,1)}, u32[]{:S(2)}) copy-start(bf16[1024,1024]{1,0:T(8,128)(2,1)} %key_ref.1) | copy-start | bytes 6291460
  3.0 0.7 copy-start.7
  4.6 0.7 copy-start.6
  16.8 12.1 %copy-start.5 = (bf16[3,1,48,1152]{3,2,1,0:T(8,128)(2,1)S(1)}, bf16[3,1,48,1152]{3,2,1,0:T(8,128)(2,1)}, u32[]{:S(2)}) copy-start(bf16[3,1,48,1152]{3,2,1,0:T(8,128)(2,1)} %get-tuple-element.29) | copy-start | bytes 995332
  16.8 23.2 %copy-start.11 = (s32[1,216]{1,0:T(1,128)S(1)}, s32[1,216]{1,0:T(1,128)}, u32[]{:S(2)}) copy-start(s32[1,216]{1,0:T(1,128)} %constant.134) | copy-start | bytes 2596
  16.8 23.2 %copy-start.12 = (s32[1,216]{1,0:T(1,128)S(1)}, s32[1,216]{1,0:T(1,128)}, u32[]{:S(2)}) copy-start(s32[1,216]{1,0:T(1,128)} %constant.133) | copy-start | bytes 2596
  16.8 23.1 %copy-start.13 = (s32[1,216]{1,0:T(1,128)S(1)}, s32[1,216]{1,0:T(1,128)}, u32[]{:S(2)}) copy-start(s32[1,216]{1,0:T(1,128)} %constant.132) | copy-start | bytes 2596
  16.8 31.5 %copy-start.10 = (s32[12,96]{1,0:T(8,128)S(1)}, s32[12,96]{1,0:T(8,128)}, u32[]{:S(2)}) copy-start(s32[12,96]{1,0:T(8,128)} %param.28) | copy-start | bytes 13828
  16.8 12.1 %collective-permute-start.5 = (bf16[3,48,1152]{2,1,0:T(8,128)(2,1)}, bf16[3,48,1152]{2,1,0:T(8,128)(2,1)S(1)}, u32[]{:S(2)}, u32[]{:S(2)}) collective-permute-start(bf16[3,48,1152]{2,1,0:T(8,128)(2,1)} %bitcast.25), channel_id=1, source_target_pairs={{0,1},{1,0},{2,3},{3,2},{8,9},{9,8},{10,11},{11,10},{16,17},{17,16... | collective-permute-start | bytes 995336 | tf_op jit(solution)/shard_map/ppermute | solution.py:344
  28.9 29.2 %copy-start.9 = (f32[16,13,13]{2,0,1:T(8,128)S(1)}, f32[16,13,13]{2,0,1:T(8,128)}, u32[]{:S(2)}) copy-start(f32[16,13,13]{2,0,1:T(8,128)} %param.27) | copy-start | bytes 32452
  28.9 3.6 %collective-permute-start = (bf16[3,48,1152]{2,1,0:T(8,128)(2,1)}, bf16[3,48,1152]{2,1,0:T(8,128)(2,1)S(1)}, u32[]{:S(2)}, u32[]{:S(2)}) collective-permute-start(bf16[3,48,1152]{2,1,0:T(8,128)(2,1)} %bitcast.24), channel_id=1, source_target_pairs={{0,1},{1,0},{2,3},{3,2},{8,9},{9,8},{10,11},{11,10},{16,17},{17,16... | collective-permute-start | bytes 995336 | tf_op jit(solution)/shard_map/ppermute | solution.py:344
  29.5 7.9 %collective-permute-start.6 = (bf16[3,24,1152]{2,1,0:T(8,128)(2,1)S(1)}, bf16[3,24,1152]{2,1,0:T(8,128)(2,1)S(1)}, u32[]{:S(2)}, u32[]{:S(2)}) collective-permute-start(bf16[3,24,1152]{2,1,0:T(8,128)(2,1)S(1)} %get-tuple-element.32), channel_id=1, source_target_pairs={{0,2},{1,3},{2,0},{3,1},{8,10},{9,11},{10,8},{11,9},{16,18},{17,19... | collective-permute-start | bytes 497672 | tf_op jit(solution)/shard_map/ppermute | solution.py:344
  32.5 1.0 %copy-start.4 = (bf16[3,1,48,1152]{3,2,1,0:T(8,128)(2,1)S(1)}, bf16[3,1,48,1152]{3,2,1,0:T(8,128)(2,1)}, u32[]{:S(2)}) copy-start(bf16[3,1,48,1152]{3,2,1,0:T(8,128)(2,1)} %get-tuple-element.21) | copy-start | bytes 995332
  33.5 31.0 %copy-start.2 = (bf16[1024,1024]{1,0:T(8,128)(2,1)S(1)}, bf16[1024,1024]{1,0:T(8,128)(2,1)}, u32[]{:S(2)}) copy-start(bf16[1024,1024]{1,0:T(8,128)(2,1)} %refs_8_.1) | copy-start | bytes 6291460
  33.5 31.0 %copy-start.8 = (f32[1024]{0:T(1024)S(1)}, f32[1024]{0:T(1024)}, u32[]{:S(2)}) copy-start(f32[1024]{0:T(1024)} %param.22) | copy-start | bytes 12292
  34.0 10.0 %collective-permute-start.1 = (bf16[3,24,1152]{2,1,0:T(8,128)(2,1)S(1)}, bf16[3,24,1152]{2,1,0:T(8,128)(2,1)S(1)}, u32[]{:S(2)}, u32[]{:S(2)}) collective-permute-start(bf16[3,24,1152]{2,1,0:T(8,128)(2,1)S(1)} %get-tuple-element.24), channel_id=1, source_target_pairs={{0,2},{1,3},{2,0},{3,1},{8,10},{9,11},{10,8},{11,9},{16,18},{17,19... | collective-permute-start | bytes 497672 | tf_op jit(solution)/shard_map/ppermute | solution.py:344
  37.8 7.7 %collective-permute-start.7 = (bf16[18,1152]{1,0:T(8,128)(2,1)S(1)}, bf16[18,1152]{1,0:T(8,128)(2,1)S(1)}, u32[]{:S(2)}, u32[]{:S(2)}) collective-permute-start(bf16[18,1152]{1,0:T(8,128)(2,1)S(1)} %get-tuple-element.34), channel_id=1, source_target_pairs={{0,8},{1,9},{2,10},{3,11},{8,16},{9,17},{10,18},{11,19},{16,24},{1... | collective-permute-start | bytes 124424 | tf_op jit(solution)/shard_map/ppermute | solution.py:344
  40.0 10.1 %collective-permute-start.8 = (bf16[18,1152]{1,0:T(8,128)(2,1)S(1)}, bf16[18,1152]{1,0:T(8,128)(2,1)S(1)}, u32[]{:S(2)}, u32[]{:S(2)}) collective-permute-start(bf16[18,1152]{1,0:T(8,128)(2,1)S(1)} %get-tuple-element.35), channel_id=1, source_target_pairs={{0,16},{1,17},{2,18},{3,19},{8,24},{9,25},{10,26},{11,27},{16,0},{... | collective-permute-start | bytes 124424 | tf_op jit(solution)/shard_map/ppermute | solution.py:344
  42.7 7.5 %collective-permute-start.9 = (bf16[18,1152]{1,0:T(8,128)(2,1)S(1)}, bf16[18,1152]{1,0:T(8,128)(2,1)S(1)}, u32[]{:S(2)}, u32[]{:S(2)}) collective-permute-start(bf16[18,1152]{1,0:T(8,128)(2,1)S(1)} %get-tuple-element.36), channel_id=1, source_target_pairs={{0,24},{1,25},{2,26},{3,27},{8,0},{9,1},{10,2},{11,3},{16,8},{17,9... | collective-permute-start | bytes 124424 | tf_op jit(solution)/shard_map/ppermute | solution.py:344
  44.4 6.2 %collective-permute-start.2 = (bf16[18,1152]{1,0:T(8,128)(2,1)S(1)}, bf16[18,1152]{1,0:T(8,128)(2,1)S(1)}, u32[]{:S(2)}, u32[]{:S(2)}) collective-permute-start(bf16[18,1152]{1,0:T(8,128)(2,1)S(1)} %get-tuple-element.26), channel_id=1, source_target_pairs={{0,8},{1,9},{2,10},{3,11},{8,16},{9,17},{10,18},{11,19},{16,24},{1... | collective-permute-start | bytes 124424 | tf_op jit(solution)/shard_map/ppermute | solution.py:344
  45.2 6.2 %collective-permute-start.3 = (bf16[18,1152]{1,0:T(8,128)(2,1)S(1)}, bf16[18,1152]{1,0:T(8,128)(2,1)S(1)}, u32[]{:S(2)}, u32[]{:S(2)}) collective-permute-start(bf16[18,1152]{1,0:T(8,128)(2,1)S(1)} %get-tuple-element.27), channel_id=1, source_target_pairs={{0,16},{1,17},{2,18},{3,19},{8,24},{9,25},{10,26},{11,27},{16,0},{... | collective-permute-start | bytes 124424 | tf_op jit(solution)/shard_map/ppermute | solution.py:344
  45.5 5.9 %collective-permute-start.4 = (bf16[18,1152]{1,0:T(8,128)(2,1)S(1)}, bf16[18,1152]{1,0:T(8,128)(2,1)S(1)}, u32[]{:S(2)}, u32[]{:S(2)}) collective-permute-start(bf16[18,1152]{1,0:T(8,128)(2,1)S(1)} %get-tuple-element.28), channel_id=1, source_target_pairs={{0,24},{1,25},{2,26},{3,27},{8,0},{9,1},{10,2},{11,3},{16,8},{17,9... | collective-permute-start | bytes 124424 | tf_op jit(solution)/shard_map/ppermute | solution.py:344
  51.9 9.7 %collective-permute-start.14 = (bf16[36,1024]{1,0:T(8,128)(2,1)S(1)}, bf16[36,1024]{1,0:T(8,128)(2,1)S(1)}, u32[]{:S(2)}, u32[]{:S(2)}) collective-permute-start(bf16[36,1024]{1,0:T(8,128)(2,1)S(1)} %pad_maximum_fusion.refs_0_), channel_id=1, source_target_pairs={{5,0},{6,1},{7,2},{12,3},{1,4},{2,5},{3,6},{8,7},{13,8},{14,9},{15... | collective-permute-start | bytes 221192 | tf_op jit(solution)/shard_map/ppermute | solution.py:398
  54.3 7.3 %collective-permute-start.13 = (bf16[36,1024]{1,0:T(8,128)(2,1)S(1)}, bf16[36,1024]{1,0:T(8,128)(2,1)S(1)}, u32[]{:S(2)}, u32[]{:S(2)}) collective-permute-start(bf16[36,1024]{1,0:T(8,128)(2,1)S(1)} %pad_maximum_fusion.refs_0_), channel_id=1, source_target_pairs={{1,0},{2,1},{3,2},{8,3},{5,4},{6,5},{7,6},{12,7},{9,8},{10,9},{11,... | collective-permute-start | bytes 221192 | tf_op jit(solution)/shard_map/ppermute | solution.py:398
  57.0 7.5 %collective-permute-start.12 = (bf16[36,1024]{1,0:T(8,128)(2,1)S(1)}, bf16[36,1024]{1,0:T(8,128)(2,1)S(1)}, u32[]{:S(2)}, u32[]{:S(2)}) collective-permute-start(bf16[36,1024]{1,0:T(8,128)(2,1)S(1)} %pad_maximum_fusion.refs_0_), channel_id=1, source_target_pairs={{31,0},{4,1},{5,2},{6,3},{27,4},{0,5},{1,6},{2,7},{7,8},{12,9},{13... | collective-permute-start | bytes 221192 | tf_op jit(solution)/shard_map/ppermute | solution.py:398
  57.0 7.5 %collective-permute-start.11 = (bf16[36,1024]{1,0:T(8,128)(2,1)S(1)}, bf16[36,1024]{1,0:T(8,128)(2,1)S(1)}, u32[]{:S(2)}, u32[]{:S(2)}) collective-permute-start(bf16[36,1024]{1,0:T(8,128)(2,1)S(1)} %pad_maximum_fusion.refs_0_), channel_id=1, source_target_pairs={{27,0},{0,1},{1,2},{2,3},{31,4},{4,5},{5,6},{6,7},{3,8},{8,9},{9,1... | collective-permute-start | bytes 221192 | tf_op jit(solution)/shard_map/ppermute | solution.py:398
  57.0 7.5 %collective-permute-start.10 = (bf16[36,1024]{1,0:T(8,128)(2,1)S(1)}, bf16[36,1024]{1,0:T(8,128)(2,1)S(1)}, u32[]{:S(2)}, u32[]{:S(2)}) collective-permute-start(bf16[36,1024]{1,0:T(8,128)(2,1)S(1)} %pad_maximum_fusion.refs_0_), channel_id=1, source_target_pairs={{4,0},{5,1},{6,2},{7,3},{0,4},{1,5},{2,6},{3,7},{12,8},{13,9},{14,... | collective-permute-start | bytes 221192 | tf_op jit(solution)/shard_map/ppermute | solution.py:398
  64.5 1.1 %copy-start = (f32[16,48,216]{2,1,0:T(8,128)S(1)}, f32[16,48,216]{2,1,0:T(8,128)}, u32[]{:S(2)}) copy-start(f32[16,48,216]{2,1,0:T(8,128)} %bias.1.refs_7_) | copy-start | bytes 1990660
  65.6 1.6 %copy-start.3 = (bf16[1024,1024]{1,0:T(8,128)(2,1)S(1)}, bf16[1024,1024]{1,0:T(8,128)(2,1)}, u32[]{:S(2)}) copy-start(bf16[1024,1024]{1,0:T(8,128)(2,1)} %refs_9_.1) | copy-start | bytes 6291460
where the time goes:
time: 74.6 us; the launch traced here: 74.3 us
  Pallas kernels  35.8 us (48%)
  starting transfers between devices  20.2 us (27%)
  local copies, waits for them, and re-layouts  10.6 us (14%)
  waiting for transfers between devices  6.14 us (8%)
  other arithmetic  1.36 us (2%)
    pallas_call x2, Pallas kernels, pool(): pl.pallas_call(kernel, grid_spec=pltpu.PrefetchScalarGridSpec(num_scalar_...  23 us
    ppermute x10, starting transfers between devices, exchange(): lax.ppermute(array, ('var', 'lon'), [(i, moved(i)) for i in range(devices)])  14.5 us
    unnamed x29, local copies, waits for them, and re-layouts  6.75 us
    pallas_call x1, Pallas kernels, on_device(): pl.pallas_call(functools.partial(attend_kernel, heads, len(window)), in_s...  6.41 us
    ppermute x5, starting transfers between devices, neighbour(): return lax.ppermute(array, ('var', 'lat', 'lon'), pairs)  5.62 us
    ppermute x10, waiting for transfers between devices, exchange(): lax.ppermute(array, ('var', 'lon'), [(i, moved(i)) for i in range(devices)])  3.3 us
    ppermute x5, waiting for transfers between devices, neighbour(): return lax.ppermute(array, ('var', 'lat', 'lon'), pairs)  2.84 us
    pallas_call x1, Pallas kernels, on_device(): pl.pallas_call(functools.partial(bias_kernel, columns), in_specs=[pl.Bloc...  2.76 us
  transfers between devices with their start and end apart: 15, of which 3 were waited for; matrix products, arithmetic and copies ran while one was open for 4% of the time, Pallas kernels for 22%

commit v1 on v0

v1 whole, which is shorter than its diff:
```python
import functools
import math

import jax
import jax.numpy as jnp
import numpy as np
from jax import lax
from jax.experimental import pallas as pl
from jax.experimental.pallas import tpu as pltpu
from jax.sharding import PartitionSpec as P

HALF = 6
EPS = 1e-05
LANES = 128
TILE_BLOCKS = 16
RADICES = (2, 2, 4)
QROWS = 48
MIB = 1 << 20
POOL_VMEM = 24 * MIB
MERGE_VMEM = 12 * MIB
F32 = jnp.float32
BF16 = jnp.bfloat16


def dot(a, b):
    return jnp.dot(a, b, preferred_element_type=F32)


def dot_nt(a, b):
    return lax.dot_general(a, b, (((1,), (1,)), ((), ())), preferred_element_type=F32)


def split3(x):
    hi = x.astype(BF16)
    rest = x - hi.astype(F32)
    mid = rest.astype(BF16)
    low = (rest - mid.astype(F32)).astype(BF16)
    return hi.astype(F32), mid.astype(F32), low.astype(F32)


def lane_iota(shape):
    return lax.broadcasted_iota(jnp.int32, shape, len(shape) - 1)


def pack3(x, heads):
    hi, mid, low = split3(x)
    lane = lane_iota(x.shape)
    mid = pltpu.roll(mid, heads, 1)
    low = pltpu.roll(low, 2 * heads, 1)
    out = jnp.where(lane < heads, hi, jnp.where(lane < 2 * heads, mid, low))
    return jnp.where(lane < 3 * heads, out, 0.0)


def unpack3(x, heads):
    return x + pltpu.roll(x, LANES - heads, 1) + pltpu.roll(x, LANES - 2 * heads, 1)


def expander(heads, width):
    head_dim = width // heads
    row = lax.broadcasted_iota(jnp.int32, (LANES, width), 0)
    lane = lax.broadcasted_iota(jnp.int32, (LANES, width), 1)
    hit = jnp.zeros((LANES, width), F32)
    for piece in range(3):
        low = (row - piece * heads) * head_dim
        inside = (row >= piece * heads) & (row < (piece + 1) * heads)
        hit = jnp.where(inside & (lane >= low) & (lane < low + head_dim), 1.0, hit)
    return hit.astype(BF16)


def encode_stats(top, total, heads):
    return pack3(top, heads) + pltpu.roll(pack3(total, heads), 3 * heads, 1)


def fold(query, key, heads, head_dim):
    width = key.shape[0]
    wide = jnp.concatenate([query] * (width // head_dim), axis=1)
    row = lax.broadcasted_iota(jnp.int32, wide.shape, 0)
    lane = lax.broadcasted_iota(jnp.int32, wide.shape, 1)
    own = (lane >= row * head_dim) & (lane < (row + 1) * head_dim)
    pieces = jnp.concatenate(split3(jnp.where(own, wide, 0.0)), axis=0).astype(BF16)
    folded = dot_nt(pieces, key)
    folded = folded[:heads] + folded[heads : 2 * heads] + folded[2 * heads :]
    parts = jnp.concatenate(
        list(split3(folded)) + [jnp.zeros((LANES - 3 * heads, width), F32)], axis=0
    )
    return parts.T.astype(BF16)


def column_order(block, tile, columns):
    shape = (tile, tile)
    target = lax.broadcasted_iota(jnp.int32, shape, 0)
    source = lax.broadcasted_iota(jnp.int32, shape, 1)
    group = jnp.zeros(shape, jnp.int32)
    for at in range(1, TILE_BLOCKS):
        group = group + jnp.where(target >= at * columns, 1, 0)
    wanted = jnp.zeros(shape, jnp.int32)
    weight, stride = TILE_BLOCKS, 1
    for radix in RADICES:
        weight //= radix
        bits, low = weight.bit_length() - 1, stride.bit_length() - 1
        digit = ((group >> bits) + (block >> low)) & (radix - 1)
        wanted = wanted + digit * stride
        stride *= radix
    wanted = wanted * columns + target - group * columns
    return jnp.where(source == wanted, 1.0, 0.0).astype(BF16)


def pool_kernel(heads, head_dim, first, count, tiles, columns, lead, *refs):
    block_ref, token_ref, value_ref = refs[:3]
    if lead:
        query_ref, key_ref, keep_ref, send_ref, fold_ref = refs[3:8]
        slots, held, sems, held_key = refs[8:]
    else:
        fold_ref, keep_ref, send_ref = refs[3:6]
        slots, held, sems = refs[6:]
    _, variables, tile, width = slots.shape
    steps = count * tiles
    block = block_ref[0]
    high = block // TILE_BLOCKS

    def fetch(step):
        row = first + step // tiles
        start = pl.multiple_of((step % tiles) * tile, tile)
        return pltpu.make_async_copy(
            token_ref.at[:, row, pl.ds(start, tile), :],
            slots.at[step % 2],
            sems.at[step % 2],
        )

    values = pltpu.make_async_copy(value_ref, held, sems.at[2])
    if lead:
        key = pltpu.make_async_copy(key_ref, held_key, sems.at[3])
        key.start()
    fetch(0).start()
    values.start()
    order = column_order(block, tile, columns)
    half = tile // RADICES[0]
    lane = lane_iota((variables * tile, LANES))
    if lead:
        key.wait()
        query = query_ref[...] * (1.0 / math.sqrt(head_dim))
        fold_ref[...] = fold(query, held_key[...], heads, head_dim)

    def body(step, _):
        @pl.when(step + 1 < steps)
        def _():
            fetch(step + 1).start()

        fetch(step).wait()
        tokens = slots[step % 2].reshape(variables * tile, width)
        score = unpack3(dot(tokens, fold_ref[...]), heads)
        score = score.reshape(variables, tile, LANES)
        top = jnp.max(score, axis=0)
        raised = jnp.exp(score - top[None])
        total = jnp.sum(raised, axis=0)
        share = raised.reshape(variables * tile, LANES)

        @pl.when(step == 0)
        def _():
            values.wait()

        pooled = []
        wide = 256
        for start in range(0, width, wide):
            rows = dot(tokens, held[:, start : start + wide])
            for low in range(0, wide, LANES):
                head = (start + low) // head_dim
                index = head + jnp.where(lane >= head_dim, 1, 0)
                spread = jnp.take_along_axis(share, index, axis=1)
                part = rows[:, low : low + LANES] * spread
                pooled.append(jnp.sum(part.reshape(variables, tile, LANES), axis=0).astype(BF16))
        pooled.append(encode_stats(top, total, heads).astype(BF16))
        ordered = dot(order, jnp.concatenate(pooled, axis=1)).astype(BF16)
        place = (step // tiles) * tiles + (step % tiles + tiles - high) % tiles
        keep_ref[place] = ordered[:half]
        send_ref[place] = ordered[half:]
        return 0

    lax.fori_loop(0, steps, body, 0)


def merge_body(parts, heads, width, last):
    stats = [unpack3(part[:, width:].astype(F32), heads) for part in parts]
    top = functools.reduce(jnp.maximum, stats)
    scales = [jnp.exp(stat - top) for stat in stats]
    totals = [pltpu.roll(stat, LANES - 3 * heads, 1) for stat in stats]
    total = sum(scale * amount for scale, amount in zip(scales, totals))
    lane = lane_iota(total.shape)
    total = jnp.where(lane < heads, total, 1.0)
    if last:
        scales = [scale / total for scale in scales]
    spread = expander(heads, width)
    merged = sum(
        dot(pack3(scale, heads).astype(BF16), spread) * part[:, :width].astype(F32)
        for scale, part in zip(scales, parts)
    ).astype(BF16)
    if last:
        return merged
    stat = encode_stats(top, total, heads).astype(BF16)
    return jnp.concatenate([merged, stat], axis=1)


def merge_kernel(heads, width, counts, last, *refs):
    outs = refs[sum(counts) :]
    at = 0
    merged, groups = [], 0
    for count in counts:
        parts = [ref[...] for ref in refs[at : at + count]]
        at += count
        groups += parts[0].shape[0]
        flat = [part.reshape(-1, part.shape[-1]) for part in parts]
        merged.append(merge_body(flat, heads, width, last))
    if last:
        for out, rows in zip(outs, merged):
            out[...] = rows
        return
    size = math.prod(outs[0].shape[:-1]) // groups
    place = 0
    for rows in merged:
        rows = rows.astype(F32)
        for low in range(0, rows.shape[0], size * len(outs)):
            for k, out in enumerate(outs):
                piece = rows[low + k * size : low + (k + 1) * size].astype(BF16)
                if len(out.shape) == 3:
                    out[place] = piece
                else:
                    out[place * size : (place + 1) * size] = piece
            place += 1


def merge(groups, shapes, heads, width, last):
    parts = [part for group in groups for part in group]
    rows = sum(math.prod(part.shape[:-1]) for part in parts)
    return pl.pallas_call(
        functools.partial(merge_kernel, heads, width, [len(group) for group in groups], last),
        out_shape=[jax.ShapeDtypeStruct(shape, BF16) for shape in shapes],
        compiler_params=pltpu.CompilerParams(vmem_limit_bytes=MERGE_VMEM),
        cost_estimate=pl.CostEstimate(
            flops=rows * LANES * width * 2,
            bytes_accessed=rows * width * 4,
            transcendentals=rows * LANES,
        ),
        name="merge",
    )(*parts)


def bias_kernel(rows, columns, where_ref, meta_ref, valid_ref, table_ref, out_ref):
    span, heads, _ = table_ref.shape
    pitch = 16
    n_rows, n_columns = valid_ref.shape
    keys = meta_ref.shape[1]
    lat, block = where_ref[0], where_ref[1]
    side = rows - 2 * rows * lat
    row_at = meta_ref[0:1] + meta_ref[1:2] * side
    column_at = meta_ref[2:3]

    far = column_at + block * columns
    far = jnp.where(far < 0, far + n_columns, far)
    far = jnp.where(far >= n_columns, far - n_columns, far)
    hot = lax.broadcasted_iota(jnp.int32, (n_columns, keys), 0) == far
    seen = dot(valid_ref[...].astype(F32).astype(BF16), jnp.where(hot, 1.0, 0.0).astype(BF16))
    mine = lax.broadcasted_iota(jnp.int32, (n_rows, keys), 0) == row_at + lat * rows
    allowed = jnp.sum(jnp.where(mine, seen, 0.0), axis=0, keepdims=True) > 0.5

    flat = [table_ref[up] for up in range(span)]
    gap = jnp.zeros((heads, pitch - span), F32)
    flat = jnp.concatenate([piece for up in flat for piece in (up, gap)], axis=1)
    pieces = jnp.concatenate(split3(flat), axis=0).astype(BF16)
    out_ref[...] = jnp.zeros(out_ref.shape, F32)
    place = lax.broadcasted_iota(jnp.int32, (span * pitch, keys), 0)
    for row in range(rows):
        for column in range(columns):
            up = row_at - row + HALF
            across = column_at - column + HALF
            inside = (up >= 0) & (up < span) & (across >= 0) & (across < span)
            index = jnp.where(inside, up * pitch + across, -1)
            found = dot(pieces, jnp.where(place == index, 1.0, 0.0).astype(BF16))
            found = found[:heads] + found[heads : 2 * heads] + found[2 * heads :]
            kept = (inside & allowed) | (index == HALF * pitch + HALF)
            out_ref[:, row * columns + column, :] = jnp.where(kept, found, -jnp.inf)


def attend_kernel(heads, count, *refs):
    blocks = refs[:count]
    gain_ref, bias_ref, w_agg, w_query, w_key, w_value, w_out, out_ref = refs[count : count + 8]
    window, mix = refs[count + 8 :]
    width = window.shape[1]
    scale = 1.0 / math.sqrt(width // heads)
    at = 0
    for block in blocks:
        size = block.shape[0]
        window[at : at + size] = block[...]
        at += size
    tokens = dot(window[...], w_agg[...]).astype(BF16)
    values = tokens.astype(F32)
    center = values - jnp.mean(values, axis=-1, keepdims=True)
    variance = jnp.mean(center * center, axis=-1, keepdims=True)
    normed = (center * lax.rsqrt(variance + EPS) * gain_ref[...]).astype(BF16)
    queries = dot(normed[:QROWS], w_query[...]).astype(BF16)
    keys = dot(normed, w_key[...]).astype(BF16)
    values = dot(normed, w_value[...]).astype(BF16)
    lane = lane_iota((QROWS, LANES))
    left = lane < LANES // 2
    for pair in range(heads // 2):
        at = slice(pair * LANES, (pair + 1) * LANES)
        query = queries[:, at]
        zero = jnp.zeros_like(query)
        both = jnp.concatenate([jnp.where(left, query, zero), jnp.where(left, zero, query)], axis=0)
        logit = dot_nt(both, keys[:, at]) * scale
        bias = bias_ref[2 * pair : 2 * pair + 2]
        logit = logit + bias.reshape(2 * QROWS, bias.shape[-1])
        raised = jnp.exp(logit - jnp.max(logit, axis=-1, keepdims=True))
        attn = (raised / jnp.sum(raised, axis=-1, keepdims=True)).astype(BF16)
        mixed = dot(attn, values[:, at])
        mix[:, at] = jnp.where(left, mixed[:QROWS], mixed[QROWS:]).astype(BF16)
    result = tokens[:QROWS].astype(F32) + dot(mix[...], w_out[...])
    rows, columns, _ = out_ref.shape
    for row in range(rows):
        out_ref[row] = result[row * columns : (row + 1) * columns].astype(BF16)


def split_before(stages, number):
    return math.prod(radix for _, radix in stages[1 : min(number + 1, len(RADICES))])


def on_device(
    sizes,
    var_tokens,
    var_query,
    agg_key,
    agg_value,
    agg_out,
    norm_gain,
    nb_query,
    nb_key,
    nb_value,
    nb_out,
    pos_bias,
    valid,
):
    heads, head_dim = var_query.shape
    width = agg_key.shape[0]
    local_vars, rows, total_columns, _ = var_tokens.shape
    n_var, n_lat, n_lon = sizes
    devices = n_var * n_lon
    columns = total_columns // devices
    tile = TILE_BLOCKS * columns
    tiles = devices // TILE_BLOCKS
    packed = width + LANES
    half = tile // RADICES[0]
    lat = lax.axis_index("lat")
    block = lax.axis_index("var") * n_lon + lax.axis_index("lon")
    where = jnp.stack([lat, block]).astype(jnp.int32)
    block = where[1:]
    smem = pl.BlockSpec(memory_space=pltpu.SMEM)
    vmem = pl.BlockSpec(memory_space=pltpu.VMEM)
    anywhere = pl.BlockSpec(memory_space=pl.ANY)

    def pool(first, count, folded):
        lead = folded is None
        shape = jax.ShapeDtypeStruct((count * tiles, half, packed), BF16)
        outs = [shape, shape] + [jax.ShapeDtypeStruct((width, LANES), BF16)] * lead
        extra = (var_query, agg_key) if lead else (folded,)
        square = pltpu.VMEM((width, width), BF16)
        patches = count * total_columns * local_vars
        return pl.pallas_call(
            functools.partial(
                pool_kernel, heads, head_dim, first, count, tiles, columns, lead
            ),
            in_specs=[smem, anywhere, anywhere] + ([vmem, anywhere] if lead else [vmem]),
            out_specs=[vmem] * len(outs),
            out_shape=outs,
            scratch_shapes=[
                pltpu.VMEM((2, local_vars, tile, width), BF16),
                square,
                pltpu.SemaphoreType.DMA((4,)),
            ]
            + [square] * lead,
            compiler_params=pltpu.CompilerParams(vmem_limit_bytes=POOL_VMEM),
            cost_estimate=pl.CostEstimate(
                flops=3 * patches * width * width,
                bytes_accessed=2 * patches * width,
                transcendentals=patches * LANES,
            ),
            name="pool",
        )(block, var_tokens, agg_value, *extra)

    def exchange(array, shift, stride, radix):
        def moved(i):
            digit = (i // stride) % radix
            return i + ((digit + shift) % radix - digit) * stride

        return lax.ppermute(array, ("var", "lon"), [(i, moved(i)) for i in range(devices)])

    stages, stride = [], 1
    for radix in RADICES:
        stages.append((stride, radix))
        stride *= radix
    if tiles > 1:
        stages.append((TILE_BLOCKS, tiles))

    def swap(sends, number):
        stride, radix = stages[number]
        return [exchange(send, k + 1, stride, radix) for k, send in enumerate(sends)]

    def next_split(groups, number, places, size):
        if number + 1 == len(stages):
            rows_left = sum(math.prod(group[0].shape[:-1]) for group in groups)
            return merge(groups, [(rows_left, width)], heads, width, True)
        radix = stages[number + 1][1]
        if number + 1 < len(RADICES):
            size //= radix
            shape = (places, size, packed) if size % 8 == 0 else (places * size, packed)
            return merge(groups, [shape] * radix, heads, width, False)
        (full,) = merge(groups, [(places * size, packed)], heads, width, False)
        full = full.reshape(places // tiles, tiles, size, packed)
        return [full[:, k].reshape(places // tiles * size, packed) for k in range(tiles)]

    barrier = lax.optimization_barrier
    lead_rows = rows - 2
    keep_a, send_a, folded = pool(0, lead_rows, None)
    got_a = swap([send_a], 0)
    keep_b, send_b = pool(lead_rows, 1, folded)
    size = half
    parts_a = next_split([[keep_a] + got_a], 0, lead_rows * tiles, size)
    got_b = swap([send_b], 0)
    parts_a, folded = barrier((parts_a, folded))
    got_a = swap(parts_a[1:], 1)
    keep_c, send_c = pool(lead_rows + 1, 1, folded)
    got_c = swap([send_c], 0)
    keep_a = parts_a[0]
    keep_b = [[keep_b] + got_b, [keep_c] + got_c]

    places = [(dl, dx) for dx in (0, -1, 1) for dl in (0, 1)]
    patch = rows * columns
    dl = np.repeat([p[0] for p in places], patch)
    dx = np.repeat([p[1] for p in places], patch)
    row = np.tile(np.repeat(np.arange(rows), columns), len(places))
    column = np.tile(np.arange(columns), len(places) * rows)
    meta = jnp.asarray(np.stack([row, dl, dx * columns + column]), jnp.int32)
    keys = len(places) * patch
    bias = pl.pallas_call(
        functools.partial(bias_kernel, rows, columns),
        in_specs=[smem, vmem, vmem, vmem],
        out_specs=vmem,
        out_shape=jax.ShapeDtypeStruct((heads, QROWS, keys), F32),
        compiler_params=pltpu.CompilerParams(vmem_limit_bytes=MERGE_VMEM),
        cost_estimate=pl.CostEstimate(
            flops=patch * 256 * keys * 48 * 8, bytes_accessed=heads * keys * 400, transcendentals=0
        ),
        name="bias",
    )(where, meta, valid, jnp.transpose(pos_bias, (1, 0, 2)))

    for number in range(1, len(stages)):
        parts_a = next_split(
            [[keep_a] + got_a], number, lead_rows * tiles, half // split_before(stages, number)
        )
        if number + 1 < len(stages):
            keep_a, got_a = parts_a[0], swap(parts_a[1:], number + 1)
        parts_b = next_split(keep_b, number - 1, 2 * tiles, half // split_before(stages, number - 1))
        got = swap(parts_b[1:], number)
        if number == 1:
            got, bias = barrier((got, bias))
        keep_b = [[parts_b[0]] + got]
    pooled_a = parts_a[0]
    (pooled_b,) = next_split(keep_b, len(stages) - 1, 2 * tiles, columns)
    pooled = jnp.concatenate([pooled_a, pooled_b], axis=0)

    def neighbour(array, dl, dx):
        pairs = []
        for i in range(n_var * n_lat * n_lon):
            v, l, o = i // (n_lat * n_lon), (i // n_lon) % n_lat, i % n_lon
            b = (v * n_lon + o + dx) % devices
            source = ((b // n_lon) * n_lat + (l + dl) % n_lat) * n_lon + b % n_lon
            pairs.append((source, i))
        return lax.ppermute(array, ("var", "lat", "lon"), pairs)

    window = [pooled] + [neighbour(pooled, dl, dx) for dl, dx in places[1:]]

    return pl.pallas_call(
        functools.partial(attend_kernel, heads, len(window)),
        in_specs=[vmem] * (len(window) + 7),
        out_specs=vmem,
        out_shape=jax.ShapeDtypeStruct((rows, columns, width), BF16),
        scratch_shapes=[pltpu.VMEM((keys, width), BF16), pltpu.VMEM((QROWS, width), BF16)],
        compiler_params=pltpu.CompilerParams(vmem_limit_bytes=MERGE_VMEM),
        name="attend",
    )(*window, norm_gain.reshape(1, width), bias, agg_out, nb_query, nb_key, nb_value, nb_out)


def solution(mesh):
    sizes = (mesh.shape["var"], mesh.shape["lat"], mesh.shape["lon"])
    return jax.shard_map(
        functools.partial(on_device, sizes),
        mesh=mesh,
        in_specs=(P(("var", "lon"), "lat", None, None),) + (P(),) * 11,
        out_specs=P("lat", ("var", "lon"), None),
        check_vma=False,
    )
```

time: 74.6 us -> 75.2 us (level)
  Pallas kernels: 35.8 us -> 29.5 us
  waiting for transfers between devices: 6.14 us -> 11.8 us
  starting transfers between devices: 20.2 us -> 22.4 us
  other arithmetic: 1.36 us -> 0.08 us
    pallas_call x10, Pallas kernels: 29.4 us -> 23.5 us  [the longest x3 18.8 us: pool(): pl.pallas_call(functools.partial(pool_kernel, heads, head_dim, first, cou...]
    ppermute x10 -> x11, waiting for transfers between devices: 3.3 us -> 8.6 us  [exchange(): lax.ppermute(array, ('var', 'lon'), [(i, moved(i)) for i in range(devices)])]
    unnamed x29 -> x26, local copies, waits for them, and re-layouts: 6.75 us -> 10.8 us
    ppermute x5, starting transfers between devices: 5.62 us -> 7.6 us  [neighbour(): return lax.ppermute(array, ('var', 'lat', 'lon'), pairs)]
    gather x1 -> x0, local copies, waits for them, and re-layouts: 1.72 us -> none  [on_device(): jnp.take(valid.reshape(-1), row_ids * total_columns + column_ids)[None, :]]
    reshape x3 -> x0, local copies, waits for them, and re-layouts: 1.45 us -> none  [the longest x1 0.71 us: on_device(): pos_bias.reshape(heads, -1)]
    ppermute x10 -> x11, starting transfers between devices: 14.5 us -> 14.8 us  [exchange(): lax.ppermute(array, ('var', 'lon'), [(i, moved(i)) for i in range(devices)])]
  transfers between devices with their start and end apart: 15 -> 16, of which waited for: 3 -> 6; matrix products, arithmetic and copies ran while one was open for 4% -> 0% of each run, Pallas kernels for 22% -> 14%
where the time goes in v1:
time: 75.2 us; the launch traced here: 74.8 us
  Pallas kernels  29.5 us (39%)
  starting transfers between devices  22.4 us (30%)
  waiting for transfers between devices  11.8 us (16%)
  local copies, waits for them, and re-layouts  10.8 us (14%)
    pallas_call x3, Pallas kernels, pool(): pl.pallas_call(functools.partial(pool_kernel, heads, head_dim, first, cou...  18.8 us
    ppermute x11, starting transfers between devices, exchange(): lax.ppermute(array, ('var', 'lon'), [(i, moved(i)) for i in range(devices)])  14.8 us
    unnamed x26, local copies, waits for them, and re-layouts  10.8 us
    ppermute x11, waiting for transfers between devices, exchange(): lax.ppermute(array, ('var', 'lon'), [(i, moved(i)) for i in range(devices)])  8.6 us
    ppermute x5, starting transfers between devices, neighbour(): return lax.ppermute(array, ('var', 'lat', 'lon'), pairs)  7.6 us
    pallas_call x1, Pallas kernels, on_device(): pl.pallas_call(functools.partial(attend_kernel, heads, len(window)), in_s...  6.02 us
    ppermute x5, waiting for transfers between devices, neighbour(): return lax.ppermute(array, ('var', 'lat', 'lon'), pairs)  3.25 us
    pallas_call x6, Pallas kernels, merge(): pl.pallas_call(functools.partial(merge_kernel, heads, width, [len(group)...  2.79 us
  transfers between devices with their start and end apart: 16, of which 6 were waited for; matrix products, arithmetic and copies ran while one was open for 0% of the time, Pallas kernels for 14%

profile of v1, /device:TPU:0, one launch (start us, length us, event | category | flops | bytes accessed | tf_op | source)
XLA Modules:
  0.0 74.8 jit_solution(5737122159391070310)
XLA Ops:
  0.0 3.7 %copy-done = bf16[8,6,96,1024]{3,2,1,0:T(8,128)(2,1)S(1)} copy-done((bf16[8,6,96,1024]{3,2,1,0:T(8,128)(2,1)S(1)}, bf16[8,6,96,1024]{3,2,1,0:T(8,128)(2,1)}, u32[]{:S(2)}) %copy-start) | copy-done | bytes 9437208
  3.7 1.6 %copy-done.1 = bf16[1024,1024]{1,0:T(8,128)(2,1)S(1)} copy-done((bf16[1024,1024]{1,0:T(8,128)(2,1)S(1)}, bf16[1024,1024]{1,0:T(8,128)(2,1)}, u32[]{:S(2)}) %copy-start.1) | copy-done | bytes 2097176
  5.3 1.6 %copy-done.8 = bf16[1024,1024]{1,0:T(8,128)(2,1)S(1)} copy-done((bf16[1024,1024]{1,0:T(8,128)(2,1)S(1)}, bf16[1024,1024]{1,0:T(8,128)(2,1)}, u32[]{:S(2)}) %copy-start.8) | copy-done | bytes 2097176
  6.9 0.7 copy-done.10
  7.6 12.6 %pool.3 = (bf16[4,48,1152]{2,1,0:T(8,128)(2,1)S(1)}, bf16[4,48,1152]{2,1,0:T(8,128)(2,1)S(1)}, bf16[1024,128]{1,0:T(8,128)(2,1)S(1)}) custom-call(s32[1]{0:T(128)} %bitcast.refs_0_, bf16[8,6,96,1024]{3,2,1,0:T(8,128)(2,1)S(1)} %copy-done, bf16[1024,1024]{1,0:T(8,128)(2,1)S(1)} %copy-done.1, f32[16,64]{1,0:T(8,128)S(1)} %copy-done.10, ...), custom_call_target="tpu_custom_call" | custom-call | flops 9663676416 | bytes 6291456 | tf_op jit(solution)/shard_map/pool/pallas_call | solution.py:366
  20.2 0.5 collective-permute-start
  20.7 3.1 %pool.4 = (bf16[1,48,1152]{2,1,0:T(8,128)(2,1)S(1)}, bf16[1,48,1152]{2,1,0:T(8,128)(2,1)S(1)}) custom-call(s32[1]{0:T(128)} %bitcast.refs_0_, bf16[8,6,96,1024]{3,2,1,0:T(8,128)(2,1)S(1)} %copy-done, bf16[1024,1024]{1,0:T(8,128)(2,1)S(1)} %copy-done.1, bf16[1024,128]{1,0:T(8,128)(2,1)S(1)} %get-tuple-element.42.refs_3_), custom_call_target="tpu_custom_call" | custom-call | flops 2415919104 | bytes 1572864 | tf_op jit(solution)/shard_map/pool/pallas_call | solution.py:366
  23.8 0.1 collective-permute-start.5
  23.9 0.0 collective-permute-done.refs_1_
  23.9 0.6 merge.6
  24.6 0.0 copy-start.9
  24.6 0.0 copy-start.11
  24.6 0.0 copy-start.12
  24.6 0.0 copy-start.4
  24.6 3.1 %pool.5 = (bf16[1,48,1152]{2,1,0:T(8,128)(2,1)S(1)}, bf16[1,48,1152]{2,1,0:T(8,128)(2,1)S(1)}) custom-call(s32[1]{0:T(128)} %bitcast.refs_0_, bf16[8,6,96,1024]{3,2,1,0:T(8,128)(2,1)S(1)} %copy-done, bf16[1024,1024]{1,0:T(8,128)(2,1)S(1)} %copy-done.1, bf16[1024,128]{1,0:T(8,128)(2,1)S(1)} %get-tuple-element.42.refs_3_), custom_call_target="tpu_custom_call" | custom-call | flops 2415919104 | bytes 1572864 | tf_op jit(solution)/shard_map/pool/pallas_call | solution.py:366
  27.7 0.5 collective-permute-start.6
  28.2 2.6 %collective-permute-start.1 = (bf16[4,24,1152]{2,1,0:T(8,128)(2,1)S(1)}, bf16[4,24,1152]{2,1,0:T(8,128)(2,1)S(1)}, u32[]{:S(2)}, u32[]{:S(2)}) collective-permute-start(bf16[4,24,1152]{2,1,0:T(8,128)(2,1)S(1)} %get-tuple-element.35), channel_id=1, source_target_pairs={{0,2},{1,3},{2,0},{3,1},{8,10},{9,11},{10,8},{11,9},{16,18},{17,19... | collective-permute-start | bytes 663560 | tf_op jit(solution)/shard_map/ppermute | solution.py:393
  30.8 0.0 collective-permute-done.5.refs_1_
  30.8 0.0 collective-permute-done.6.refs_3_
  30.8 0.5 merge.9
  31.3 0.0 copy-start.2
  31.3 0.0 copy-start.7
  31.3 1.3 %collective-permute-start.7 = (bf16[2,24,1152]{2,1,0:T(8,128)(2,1)S(1)}, bf16[2,24,1152]{2,1,0:T(8,128)(2,1)S(1)}, u32[]{:S(2)}, u32[]{:S(2)}) collective-permute-start(bf16[2,24,1152]{2,1,0:T(8,128)(2,1)S(1)} %get-tuple-element.46), channel_id=1, source_target_pairs={{0,2},{1,3},{2,0},{3,1},{8,10},{9,11},{10,8},{11,9},{16,18},{17,19... | collective-permute-start | bytes 331784 | tf_op jit(solution)/shard_map/ppermute | solution.py:393
  32.6 0.1 pad_add_fusion.where_ref
  32.7 0.0 copy-done.9
  32.7 0.0 copy-done.11
  32.7 0.0 copy-done.12
  32.7 1.9 %bias.1.refs_7_ = f32[16,48,216]{2,1,0:T(8,128)S(1)} custom-call(s32[2]{0:T(128)S(1)} %pad_add_fusion.where_ref, s32[3,216]{1,0:T(4,128)S(1)} %copy-done.12, s32[12,96]{1,0:T(8,128)S(1)} %copy-done.11, f32[13,16,13]{2,1,0:T(8,128)S(1)} %bitcast.5), custom_call_target="tpu_custom_call" | custom-call | flops 764411904 | bytes 1382400 | tf_op jit(solution)/shard_map/bias/pallas_call | solution.py:442
  34.6 4.5 %collective-permute-done.7.refs_1_ = bf16[2,24,1152]{2,1,0:T(8,128)(2,1)S(1)} collective-permute-done((bf16[2,24,1152]{2,1,0:T(8,128)(2,1)S(1)}, bf16[2,24,1152]{2,1,0:T(8,128)(2,1)S(1)}, u32[]{:S(2)}, u32[]{:S(2)}) %collective-permute-start.7) | collective-permute-done | bytes 110624 | tf_op jit(solution)/shard_map/ppermute | solution.py:393
  39.2 0.4 merge.10
  39.5 3.9 %collective-permute-start.10 = (bf16[12,1152]{1,0:T(8,128)(2,1)S(1)}, bf16[12,1152]{1,0:T(8,128)(2,1)S(1)}, u32[]{:S(2)}, u32[]{:S(2)}) collective-permute-start(bf16[12,1152]{1,0:T(8,128)(2,1)S(1)} %get-tuple-element.51), channel_id=1, source_target_pairs={{0,24},{1,25},{2,26},{3,27},{8,0},{9,1},{10,2},{11,3},{16,8},{17,9... | collective-permute-start | bytes 82952 | tf_op jit(solution)/shard_map/ppermute | solution.py:393
  43.5 0.0 collective-permute-done.1.refs_1_
  43.5 0.4 merge.7
  43.9 0.1 collective-permute-start.2
  44.0 1.0 %collective-permute-start.3 = (bf16[24,1152]{1,0:T(8,128)(2,1)S(1)}, bf16[24,1152]{1,0:T(8,128)(2,1)S(1)}, u32[]{:S(2)}, u32[]{:S(2)}) collective-permute-start(bf16[24,1152]{1,0:T(8,128)(2,1)S(1)} %get-tuple-element.38), channel_id=1, source_target_pairs={{0,16},{1,17},{2,18},{3,19},{8,24},{9,25},{10,26},{11,27},{16,0},{... | collective-permute-start | bytes 165896 | tf_op jit(solution)/shard_map/ppermute | solution.py:393
  45.0 2.8 %collective-permute-start.4 = (bf16[24,1152]{1,0:T(8,128)(2,1)S(1)}, bf16[24,1152]{1,0:T(8,128)(2,1)S(1)}, u32[]{:S(2)}, u32[]{:S(2)}) collective-permute-start(bf16[24,1152]{1,0:T(8,128)(2,1)S(1)} %get-tuple-element.39), channel_id=1, source_target_pairs={{0,24},{1,25},{2,26},{3,27},{8,0},{9,1},{10,2},{11,3},{16,8},{17,9... | collective-permute-start | bytes 165896 | tf_op jit(solution)/shard_map/ppermute | solution.py:393
  47.8 0.6 collective-permute-start.8
  48.4 0.0 collective-permute-done.10.refs_3_
  48.4 1.5 %collective-permute-start.9 = (bf16[12,1152]{1,0:T(8,128)(2,1)S(1)}, bf16[12,1152]{1,0:T(8,128)(2,1)S(1)}, u32[]{:S(2)}, u32[]{:S(2)}) collective-permute-start(bf16[12,1152]{1,0:T(8,128)(2,1)S(1)} %get-tuple-element.50), channel_id=1, source_target_pairs={{0,16},{1,17},{2,18},{3,19},{8,24},{9,25},{10,26},{11,27},{16,0},{... | collective-permute-start | bytes 82952 | tf_op jit(solution)/shard_map/ppermute | solution.py:393
  49.8 3.8 %collective-permute-done.8.refs_1_ = bf16[12,1152]{1,0:T(8,128)(2,1)S(1)} collective-permute-done((bf16[12,1152]{1,0:T(8,128)(2,1)S(1)}, bf16[12,1152]{1,0:T(8,128)(2,1)S(1)}, u32[]{:S(2)}, u32[]{:S(2)}) %collective-permute-start.8) | collective-permute-done | bytes 27680 | tf_op jit(solution)/shard_map/ppermute | solution.py:393
  53.7 0.2 collective-permute-done.9.refs_2_
  53.9 0.4 merge.11
  54.3 0.0 collective-permute-done.2.refs_1_
  54.3 0.0 collective-permute-done.3.refs_2_
  54.3 0.0 collective-permute-done.4.refs_3_
  54.3 0.4 merge.8
  54.8 1.6 %collective-permute-start.11 = (bf16[36,1024]{1,0:T(8,128)(2,1)S(1)}, bf16[36,1024]{1,0:T(8,128)(2,1)S(1)}, u32[]{:S(2)}, u32[]{:S(2)}) collective-permute-start(bf16[36,1024]{1,0:T(8,128)(2,1)S(1)} %pad_maximum_fusion.refs_0_), channel_id=1, source_target_pairs={{4,0},{5,1},{6,2},{7,3},{0,4},{1,5},{2,6},{3,7},{12,8},{13,9},{14,... | collective-permute-start | bytes 221192 | tf_op jit(solution)/shard_map/ppermute | solution.py:476
  56.3 0.0 collective-permute-start.12
  56.3 1.7 %collective-permute-start.13 = (bf16[36,1024]{1,0:T(8,128)(2,1)S(1)}, bf16[36,1024]{1,0:T(8,128)(2,1)S(1)}, u32[]{:S(2)}, u32[]{:S(2)}) collective-permute-start(bf16[36,1024]{1,0:T(8,128)(2,1)S(1)} %pad_maximum_fusion.refs_0_), channel_id=1, source_target_pairs={{31,0},{4,1},{5,2},{6,3},{27,4},{0,5},{1,6},{2,7},{7,8},{12,9},{13... | collective-permute-start | bytes 221192 | tf_op jit(solution)/shard_map/ppermute | solution.py:476
  58.1 2.7 %collective-permute-start.14 = (bf16[36,1024]{1,0:T(8,128)(2,1)S(1)}, bf16[36,1024]{1,0:T(8,128)(2,1)S(1)}, u32[]{:S(2)}, u32[]{:S(2)}) collective-permute-start(bf16[36,1024]{1,0:T(8,128)(2,1)S(1)} %pad_maximum_fusion.refs_0_), channel_id=1, source_target_pairs={{1,0},{2,1},{3,2},{8,3},{5,4},{6,5},{7,6},{12,7},{9,8},{10,9},{11,... | collective-permute-start | bytes 221192 | tf_op jit(solution)/shard_map/ppermute | solution.py:476
  60.8 1.6 %collective-permute-start.15 = (bf16[36,1024]{1,0:T(8,128)(2,1)S(1)}, bf16[36,1024]{1,0:T(8,128)(2,1)S(1)}, u32[]{:S(2)}, u32[]{:S(2)}) collective-permute-start(bf16[36,1024]{1,0:T(8,128)(2,1)S(1)} %pad_maximum_fusion.refs_0_), channel_id=1, source_target_pairs={{5,0},{6,1},{7,2},{12,3},{1,4},{2,5},{3,6},{8,7},{13,8},{14,9},{15... | collective-permute-start | bytes 221192 | tf_op jit(solution)/shard_map/ppermute | solution.py:476
  62.4 0.0 collective-permute-done.11.refs_1_
  62.4 0.6 collective-permute-done.12.refs_2_
  62.9 0.9 %collective-permute-done.13.refs_3_ = bf16[36,1024]{1,0:T(8,128)(2,1)S(1)} collective-permute-done((bf16[36,1024]{1,0:T(8,128)(2,1)S(1)}, bf16[36,1024]{1,0:T(8,128)(2,1)S(1)}, u32[]{:S(2)}, u32[]{:S(2)}) %collective-permute-start.13) | collective-permute-done | bytes 73760 | tf_op jit(solution)/shard_map/ppermute | solution.py:476
  63.9 0.0 collective-permute-done.14.refs_4_
  63.9 1.7 %collective-permute-done.15.refs_5_ = bf16[36,1024]{1,0:T(8,128)(2,1)S(1)} collective-permute-done((bf16[36,1024]{1,0:T(8,128)(2,1)S(1)}, bf16[36,1024]{1,0:T(8,128)(2,1)S(1)}, u32[]{:S(2)}, u32[]{:S(2)}) %collective-permute-start.15) | collective-permute-done | bytes 73760 | tf_op jit(solution)/shard_map/ppermute | solution.py:476
  65.6 0.0 copy-done.4
  65.6 0.0 copy-done.3
  65.6 0.0 copy-done.2
  65.6 0.0 copy-done.7
  65.6 0.0 copy-start.5
  65.6 1.6 %copy-done.5 = bf16[1024,1024]{1,0:T(8,128)(2,1)S(1)} copy-done((bf16[1024,1024]{1,0:T(8,128)(2,1)S(1)}, bf16[1024,1024]{1,0:T(8,128)(2,1)}, u32[]{:S(2)}) %copy-start.5) | copy-done | bytes 2097176
  67.2 1.6 %copy-done.6 = bf16[1024,1024]{1,0:T(8,128)(2,1)S(1)} copy-done((bf16[1024,1024]{1,0:T(8,128)(2,1)S(1)}, bf16[1024,1024]{1,0:T(8,128)(2,1)}, u32[]{:S(2)}) %copy-start.6) | copy-done | bytes 2097176
  68.8 6.0 %attend.1 = bf16[6,6,1024]{2,1,0:T(8,128)(2,1)} custom-call(bf16[36,1024]{1,0:T(8,128)(2,1)S(1)} %pad_maximum_fusion.refs_0_, bf16[36,1024]{1,0:T(8,128)(2,1)S(1)} %collective-permute-done.11.refs_1_, bf16[36,1024]{1,0:T(8,128)(2,1)S(1)} %collective-permute-done.12.refs_2_, bf16[36,1024]{1,0:T(8,128)(2,1)S(1)} %collective-permute-done.13.refs_3_, ...), custom_call_target="tpu_custom_call" | custom-call | tf_op jit(solution)/shard_map/attend/pallas_call | solution.py:480
  (7 shorter events, 0.0 us)
Async XLA Ops:
  0.0 3.7 %copy-start = (bf16[8,6,96,1024]{3,2,1,0:T(8,128)(2,1)S(1)}, bf16[8,6,96,1024]{3,2,1,0:T(8,128)(2,1)}, u32[]{:S(2)}) copy-start(bf16[8,6,96,1024]{3,2,1,0:T(8,128)(2,1)} %refs_1_.5) | copy-start | bytes 28311556
  3.7 1.6 %copy-start.1 = (bf16[1024,1024]{1,0:T(8,128)(2,1)S(1)}, bf16[1024,1024]{1,0:T(8,128)(2,1)}, u32[]{:S(2)}) copy-start(bf16[1024,1024]{1,0:T(8,128)(2,1)} %refs_2_.5) | copy-start | bytes 6291460
  5.3 1.6 %copy-start.8 = (bf16[1024,1024]{1,0:T(8,128)(2,1)S(1)}, bf16[1024,1024]{1,0:T(8,128)(2,1)}, u32[]{:S(2)}) copy-start(bf16[1024,1024]{1,0:T(8,128)(2,1)} %refs_4_.1) | copy-start | bytes 6291460
  6.9 0.7 copy-start.10
  20.2 3.7 %collective-permute-start = (bf16[4,48,1152]{2,1,0:T(8,128)(2,1)S(1)}, bf16[4,48,1152]{2,1,0:T(8,128)(2,1)S(1)}, u32[]{:S(2)}, u32[]{:S(2)}) collective-permute-start(bf16[4,48,1152]{2,1,0:T(8,128)(2,1)S(1)} %get-tuple-element.30), channel_id=1, source_target_pairs={{0,1},{1,0},{2,3},{3,2},{8,9},{9,8},{10,11},{11,10},{16,17},{17,16... | collective-permute-start | bytes 1327112 | tf_op jit(solution)/shard_map/ppermute | solution.py:393
  23.8 7.0 %collective-permute-start.5 = (bf16[1,48,1152]{2,1,0:T(8,128)(2,1)S(1)}, bf16[1,48,1152]{2,1,0:T(8,128)(2,1)S(1)}, u32[]{:S(2)}, u32[]{:S(2)}) collective-permute-start(bf16[1,48,1152]{2,1,0:T(8,128)(2,1)S(1)} %get-tuple-element.41), channel_id=1, source_target_pairs={{0,1},{1,0},{2,3},{3,2},{8,9},{9,8},{10,11},{11,10},{16,17},{17,16... | collective-permute-start | bytes 331784 | tf_op jit(solution)/shard_map/ppermute | solution.py:393
  24.6 8.1 %copy-start.9 = (f32[16,13,13]{2,0,1:T(8,128)S(1)}, f32[16,13,13]{2,0,1:T(8,128)}, u32[]{:S(2)}) copy-start(f32[16,13,13]{2,0,1:T(8,128)} %param.23) | copy-start | bytes 32452
  24.6 8.1 %copy-start.11 = (s32[12,96]{1,0:T(8,128)S(1)}, s32[12,96]{1,0:T(8,128)}, u32[]{:S(2)}) copy-start(s32[12,96]{1,0:T(8,128)} %valid_ref.1) | copy-start | bytes 13828
  24.6 8.1 %copy-start.12 = (s32[3,216]{1,0:T(4,128)S(1)}, s32[3,216]{1,0:T(4,128)}, u32[]{:S(2)}) copy-start(s32[3,216]{1,0:T(4,128)} %constant.16.clone.meta_ref) | copy-start | bytes 7780
  24.6 41.0 %copy-start.4 = (bf16[1024,1024]{1,0:T(8,128)(2,1)S(1)}, bf16[1024,1024]{1,0:T(8,128)(2,1)}, u32[]{:S(2)}) copy-start(bf16[1024,1024]{1,0:T(8,128)(2,1)} %refs_10_.1) | copy-start | bytes 6291460
  27.7 3.1 %collective-permute-start.6 = (bf16[1,48,1152]{2,1,0:T(8,128)(2,1)S(1)}, bf16[1,48,1152]{2,1,0:T(8,128)(2,1)S(1)}, u32[]{:S(2)}, u32[]{:S(2)}) collective-permute-start(bf16[1,48,1152]{2,1,0:T(8,128)(2,1)S(1)} %get-tuple-element.44), channel_id=1, source_target_pairs={{0,1},{1,0},{2,3},{3,2},{8,9},{9,8},{10,11},{11,10},{16,17},{17,16... | collective-permute-start | bytes 331784 | tf_op jit(solution)/shard_map/ppermute | solution.py:393
  28.2 15.3 %collective-permute-start.1 = (bf16[4,24,1152]{2,1,0:T(8,128)(2,1)S(1)}, bf16[4,24,1152]{2,1,0:T(8,128)(2,1)S(1)}, u32[]{:S(2)}, u32[]{:S(2)}) collective-permute-start(bf16[4,24,1152]{2,1,0:T(8,128)(2,1)S(1)} %get-tuple-element.35), channel_id=1, source_target_pairs={{0,2},{1,3},{2,0},{3,1},{8,10},{9,11},{10,8},{11,9},{16,18},{17,19... | collective-permute-start | bytes 663560 | tf_op jit(solution)/shard_map/ppermute | solution.py:393
  30.8 34.8 %copy-start.3 = (bf16[1024,1024]{1,0:T(8,128)(2,1)S(1)}, bf16[1024,1024]{1,0:T(8,128)(2,1)}, u32[]{:S(2)}) copy-start(bf16[1024,1024]{1,0:T(8,128)(2,1)} %refs_9_.1) | copy-start | bytes 6291460
  31.3 34.3 %copy-start.2 = (bf16[1024,1024]{1,0:T(8,128)(2,1)S(1)}, bf16[1024,1024]{1,0:T(8,128)(2,1)}, u32[]{:S(2)}) copy-start(bf16[1024,1024]{1,0:T(8,128)(2,1)} %refs_8_.1) | copy-start | bytes 6291460
  31.3 34.3 %copy-start.7 = (f32[1024]{0:T(1024)S(1)}, f32[1024]{0:T(1024)}, u32[]{:S(2)}) copy-start(f32[1024]{0:T(1024)} %param.18) | copy-start | bytes 12292
  31.3 7.9 %collective-permute-start.7 = (bf16[2,24,1152]{2,1,0:T(8,128)(2,1)S(1)}, bf16[2,24,1152]{2,1,0:T(8,128)(2,1)S(1)}, u32[]{:S(2)}, u32[]{:S(2)}) collective-permute-start(bf16[2,24,1152]{2,1,0:T(8,128)(2,1)S(1)} %get-tuple-element.46), channel_id=1, source_target_pairs={{0,2},{1,3},{2,0},{3,1},{8,10},{9,11},{10,8},{11,9},{16,18},{17,19... | collective-permute-start | bytes 331784 | tf_op jit(solution)/shard_map/ppermute | solution.py:393
  39.5 8.8 %collective-permute-start.10 = (bf16[12,1152]{1,0:T(8,128)(2,1)S(1)}, bf16[12,1152]{1,0:T(8,128)(2,1)S(1)}, u32[]{:S(2)}, u32[]{:S(2)}) collective-permute-start(bf16[12,1152]{1,0:T(8,128)(2,1)S(1)} %get-tuple-element.51), channel_id=1, source_target_pairs={{0,24},{1,25},{2,26},{3,27},{8,0},{9,1},{10,2},{11,3},{16,8},{17,9... | collective-permute-start | bytes 82952 | tf_op jit(solution)/shard_map/ppermute | solution.py:393
  43.9 10.4 %collective-permute-start.2 = (bf16[24,1152]{1,0:T(8,128)(2,1)S(1)}, bf16[24,1152]{1,0:T(8,128)(2,1)S(1)}, u32[]{:S(2)}, u32[]{:S(2)}) collective-permute-start(bf16[24,1152]{1,0:T(8,128)(2,1)S(1)} %get-tuple-element.37), channel_id=1, source_target_pairs={{0,8},{1,9},{2,10},{3,11},{8,16},{9,17},{10,18},{11,19},{16,24},{1... | collective-permute-start | bytes 165896 | tf_op jit(solution)/shard_map/ppermute | solution.py:393
  44.0 10.3 %collective-permute-start.3 = (bf16[24,1152]{1,0:T(8,128)(2,1)S(1)}, bf16[24,1152]{1,0:T(8,128)(2,1)S(1)}, u32[]{:S(2)}, u32[]{:S(2)}) collective-permute-start(bf16[24,1152]{1,0:T(8,128)(2,1)S(1)} %get-tuple-element.38), channel_id=1, source_target_pairs={{0,16},{1,17},{2,18},{3,19},{8,24},{9,25},{10,26},{11,27},{16,0},{... | collective-permute-start | bytes 165896 | tf_op jit(solution)/shard_map/ppermute | solution.py:393
  45.0 9.3 %collective-permute-start.4 = (bf16[24,1152]{1,0:T(8,128)(2,1)S(1)}, bf16[24,1152]{1,0:T(8,128)(2,1)S(1)}, u32[]{:S(2)}, u32[]{:S(2)}) collective-permute-start(bf16[24,1152]{1,0:T(8,128)(2,1)S(1)} %get-tuple-element.39), channel_id=1, source_target_pairs={{0,24},{1,25},{2,26},{3,27},{8,0},{9,1},{10,2},{11,3},{16,8},{17,9... | collective-permute-start | bytes 165896 | tf_op jit(solution)/shard_map/ppermute | solution.py:393
  47.8 5.9 %collective-permute-start.8 = (bf16[12,1152]{1,0:T(8,128)(2,1)S(1)}, bf16[12,1152]{1,0:T(8,128)(2,1)S(1)}, u32[]{:S(2)}, u32[]{:S(2)}) collective-permute-start(bf16[12,1152]{1,0:T(8,128)(2,1)S(1)} %get-tuple-element.49), channel_id=1, source_target_pairs={{0,8},{1,9},{2,10},{3,11},{8,16},{9,17},{10,18},{11,19},{16,24},{1... | collective-permute-start | bytes 82952 | tf_op jit(solution)/shard_map/ppermute | solution.py:393
  48.4 5.5 %collective-permute-start.9 = (bf16[12,1152]{1,0:T(8,128)(2,1)S(1)}, bf16[12,1152]{1,0:T(8,128)(2,1)S(1)}, u32[]{:S(2)}, u32[]{:S(2)}) collective-permute-start(bf16[12,1152]{1,0:T(8,128)(2,1)S(1)} %get-tuple-element.50), channel_id=1, source_target_pairs={{0,16},{1,17},{2,18},{3,19},{8,24},{9,25},{10,26},{11,27},{16,0},{... | collective-permute-start | bytes 82952 | tf_op jit(solution)/shard_map/ppermute | solution.py:393
  54.8 7.6 %collective-permute-start.11 = (bf16[36,1024]{1,0:T(8,128)(2,1)S(1)}, bf16[36,1024]{1,0:T(8,128)(2,1)S(1)}, u32[]{:S(2)}, u32[]{:S(2)}) collective-permute-start(bf16[36,1024]{1,0:T(8,128)(2,1)S(1)} %pad_maximum_fusion.refs_0_), channel_id=1, source_target_pairs={{4,0},{5,1},{6,2},{7,3},{0,4},{1,5},{2,6},{3,7},{12,8},{13,9},{14,... | collective-permute-start | bytes 221192 | tf_op jit(solution)/shard_map/ppermute | solution.py:476
  56.3 6.6 %collective-permute-start.12 = (bf16[36,1024]{1,0:T(8,128)(2,1)S(1)}, bf16[36,1024]{1,0:T(8,128)(2,1)S(1)}, u32[]{:S(2)}, u32[]{:S(2)}) collective-permute-start(bf16[36,1024]{1,0:T(8,128)(2,1)S(1)} %pad_maximum_fusion.refs_0_), channel_id=1, source_target_pairs={{27,0},{0,1},{1,2},{2,3},{31,4},{4,5},{5,6},{6,7},{3,8},{8,9},{9,1... | collective-permute-start | bytes 221192 | tf_op jit(solution)/shard_map/ppermute | solution.py:476
  56.3 7.5 %collective-permute-start.13 = (bf16[36,1024]{1,0:T(8,128)(2,1)S(1)}, bf16[36,1024]{1,0:T(8,128)(2,1)S(1)}, u32[]{:S(2)}, u32[]{:S(2)}) collective-permute-start(bf16[36,1024]{1,0:T(8,128)(2,1)S(1)} %pad_maximum_fusion.refs_0_), channel_id=1, source_target_pairs={{31,0},{4,1},{5,2},{6,3},{27,4},{0,5},{1,6},{2,7},{7,8},{12,9},{13... | collective-permute-start | bytes 221192 | tf_op jit(solution)/shard_map/ppermute | solution.py:476
  58.1 5.8 %collective-permute-start.14 = (bf16[36,1024]{1,0:T(8,128)(2,1)S(1)}, bf16[36,1024]{1,0:T(8,128)(2,1)S(1)}, u32[]{:S(2)}, u32[]{:S(2)}) collective-permute-start(bf16[36,1024]{1,0:T(8,128)(2,1)S(1)} %pad_maximum_fusion.refs_0_), channel_id=1, source_target_pairs={{1,0},{2,1},{3,2},{8,3},{5,4},{6,5},{7,6},{12,7},{9,8},{10,9},{11,... | collective-permute-start | bytes 221192 | tf_op jit(solution)/shard_map/ppermute | solution.py:476
  60.8 4.8 %collective-permute-start.15 = (bf16[36,1024]{1,0:T(8,128)(2,1)S(1)}, bf16[36,1024]{1,0:T(8,128)(2,1)S(1)}, u32[]{:S(2)}, u32[]{:S(2)}) collective-permute-start(bf16[36,1024]{1,0:T(8,128)(2,1)S(1)} %pad_maximum_fusion.refs_0_), channel_id=1, source_target_pairs={{5,0},{6,1},{7,2},{12,3},{1,4},{2,5},{3,6},{8,7},{13,8},{14,9},{15... | collective-permute-start | bytes 221192 | tf_op jit(solution)/shard_map/ppermute | solution.py:476
  65.6 1.6 %copy-start.5 = (bf16[1024,1024]{1,0:T(8,128)(2,1)S(1)}, bf16[1024,1024]{1,0:T(8,128)(2,1)}, u32[]{:S(2)}) copy-start(bf16[1024,1024]{1,0:T(8,128)(2,1)} %refs_11_.1) | copy-start | bytes 6291460
  67.2 1.6 %copy-start.6 = (bf16[1024,1024]{1,0:T(8,128)(2,1)S(1)}, bf16[1024,1024]{1,0:T(8,128)(2,1)}, u32[]{:S(2)}) copy-start(bf16[1024,1024]{1,0:T(8,128)(2,1)} %refs_12_.1) | copy-start | bytes 6291460

commit v2 on v1

--- a/solution.py
+++ b/solution.py
@@ -16,8 +16,9 @@
 RADICES = (2, 2, 4)
 QROWS = 48
 MIB = 1 << 20
-POOL_VMEM = 24 * MIB
+POOL_VMEM = 60 * MIB
 MERGE_VMEM = 12 * MIB
+STAGE_VMEM = 42 * MIB
 F32 = jnp.float32
 BF16 = jnp.bfloat16
 
@@ -244,7 +245,13 @@
     )(*parts)
 
 
-def bias_kernel(rows, columns, where_ref, meta_ref, valid_ref, table_ref, out_ref):
+def bias_kernel(rows, columns, where_ref, meta_ref, valid_ref, table_ref, *refs):
+    out_ref, sems = refs[5], refs[11]
+    copies = [
+        pltpu.make_async_copy(refs[at], refs[6 + at], sems.at[at]) for at in range(5)
+    ]
+    for copy in copies:
+        copy.start()
     span, heads, _ = table_ref.shape
     pitch = 16
     n_rows, n_columns = valid_ref.shape
@@ -278,6 +285,8 @@
             found = found[:heads] + found[heads : 2 * heads] + found[2 * heads :]
             kept = (inside & allowed) | (index == HALF * pitch + HALF)
             out_ref[:, row * columns + column, :] = jnp.where(kept, found, -jnp.inf)
+    for copy in copies:
+        copy.wait()
 
 
 def attend_kernel(heads, count, *refs):
@@ -354,7 +363,7 @@
     block = where[1:]
     smem = pl.BlockSpec(memory_space=pltpu.SMEM)
     vmem = pl.BlockSpec(memory_space=pltpu.VMEM)
-    anywhere = pl.BlockSpec(memory_space=pl.ANY)
+    hbm = pl.BlockSpec(memory_space=pltpu.HBM)
 
     def pool(first, count, folded):
         lead = folded is None
@@ -362,12 +371,11 @@
         outs = [shape, shape] + [jax.ShapeDtypeStruct((width, LANES), BF16)] * lead
         extra = (var_query, agg_key) if lead else (folded,)
         square = pltpu.VMEM((width, width), BF16)
-        patches = count * total_columns * local_vars
         return pl.pallas_call(
             functools.partial(
                 pool_kernel, heads, head_dim, first, count, tiles, columns, lead
             ),
-            in_specs=[smem, anywhere, anywhere] + ([vmem, anywhere] if lead else [vmem]),
+            in_specs=[smem, hbm, hbm] + ([vmem, hbm] if lead else [vmem]),
             out_specs=[vmem] * len(outs),
             out_shape=outs,
             scratch_shapes=[
@@ -378,9 +386,9 @@
             + [square] * lead,
             compiler_params=pltpu.CompilerParams(vmem_limit_bytes=POOL_VMEM),
             cost_estimate=pl.CostEstimate(
-                flops=3 * patches * width * width,
-                bytes_accessed=2 * patches * width,
-                transcendentals=patches * LANES,
+                flops=3 * count * total_columns * local_vars * width * width,
+                bytes_accessed=2 * count * total_columns * local_vars * width,
+                transcendentals=0,
             ),
             name="pool",
         )(block, var_tokens, agg_value, *extra)
@@ -439,28 +447,32 @@
     column = np.tile(np.arange(columns), len(places) * rows)
     meta = jnp.asarray(np.stack([row, dl, dx * columns + column]), jnp.int32)
     keys = len(places) * patch
-    bias = pl.pallas_call(
+    weights = (agg_out, nb_query, nb_key, nb_value, nb_out)
+    bias, *weights = pl.pallas_call(
         functools.partial(bias_kernel, rows, columns),
-        in_specs=[smem, vmem, vmem, vmem],
-        out_specs=vmem,
-        out_shape=jax.ShapeDtypeStruct((heads, QROWS, keys), F32),
-        compiler_params=pltpu.CompilerParams(vmem_limit_bytes=MERGE_VMEM),
+        in_specs=[smem, vmem, vmem, vmem] + [hbm] * 5,
+        out_specs=[vmem] * 6,
+        out_shape=[jax.ShapeDtypeStruct((heads, QROWS, keys), F32)]
+        + [jax.ShapeDtypeStruct(weight.shape, weight.dtype) for weight in weights],
+        scratch_shapes=[pltpu.SemaphoreType.DMA((5,))],
+        compiler_params=pltpu.CompilerParams(vmem_limit_bytes=STAGE_VMEM),
         cost_estimate=pl.CostEstimate(
-            flops=patch * 256 * keys * 48 * 8, bytes_accessed=heads * keys * 400, transcendentals=0
+            flops=1000, bytes_accessed=1000, transcendentals=0
         ),
         name="bias",
-    )(where, meta, valid, jnp.transpose(pos_bias, (1, 0, 2)))
+    )(where, meta, valid, jnp.transpose(pos_bias, (1, 0, 2)), *weights)
 
     for number in range(1, len(stages)):
         parts_a = next_split(
             [[keep_a] + got_a], number, lead_rows * tiles, half // split_before(stages, number)
         )
+        parts_b = next_split(keep_b, number - 1, 2 * tiles, half // split_before(stages, number - 1))
+        parts_a, parts_b = barrier((parts_a, parts_b))
         if number + 1 < len(stages):
             keep_a, got_a = parts_a[0], swap(parts_a[1:], number + 1)
-        parts_b = next_split(keep_b, number - 1, 2 * tiles, half // split_before(stages, number - 1))
         got = swap(parts_b[1:], number)
         if number == 1:
-            got, bias = barrier((got, bias))
+            got, bias, weights = barrier((got, bias, weights))
         keep_b = [[parts_b[0]] + got]
     pooled_a = parts_a[0]
     (pooled_b,) = next_split(keep_b, len(stages) - 1, 2 * tiles, columns)
@@ -482,10 +494,13 @@
         in_specs=[vmem] * (len(window) + 7),
         out_specs=vmem,
         out_shape=jax.ShapeDtypeStruct((rows, columns, width), BF16),
-        scratch_shapes=[pltpu.VMEM((keys, width), BF16), pltpu.VMEM((QROWS, width), BF16)],
+        scratch_shapes=[
+            pltpu.VMEM((keys, width), BF16),
+            pltpu.VMEM((QROWS, width), BF16),
+        ],
         compiler_params=pltpu.CompilerParams(vmem_limit_bytes=MERGE_VMEM),
         name="attend",
-    )(*window, norm_gain.reshape(1, width), bias, agg_out, nb_query, nb_key, nb_value, nb_out)
+    )(*window, norm_gain.reshape(1, width), bias, *weights)
 
 
 def solution(mesh):

time: 75.2 us -> 72.4 us (0.963)
  Pallas kernels: 29.5 us -> 40.3 us
  local copies, waits for them, and re-layouts: 10.8 us -> 0.93 us
  starting transfers between devices: 22.4 us -> 19.5 us
    unnamed x26 -> x14, local copies, waits for them, and re-layouts: 10.8 us -> 0.93 us
    pallas_call x3, Pallas kernels: 18.8 us -> 26.9 us  [pool(): pl.pallas_call(functools.partial(pool_kernel, heads, head_dim, first, cou...]
    ppermute x11, waiting for transfers between devices: 8.6 us -> 4.23 us  [exchange(): lax.ppermute(array, ('var', 'lon'), [(i, moved(i)) for i in range(devices)])]
    ppermute x5, waiting for transfers between devices: 3.25 us -> 6.96 us  [neighbour(): return lax.ppermute(array, ('var', 'lat', 'lon'), pairs)]
    pallas_call x1, Pallas kernels: 1.94 us -> 4.68 us  [on_device(): pl.pallas_call(functools.partial(bias_kernel, rows, columns), in_specs=[s...]
    ppermute x5, starting transfers between devices: 7.6 us -> 5.76 us  [neighbour(): return lax.ppermute(array, ('var', 'lat', 'lon'), pairs)]
    ppermute x11, starting transfers between devices: 14.8 us -> 13.7 us  [exchange(): lax.ppermute(array, ('var', 'lon'), [(i, moved(i)) for i in range(devices)])]
  transfers between devices with their start and end apart: 16 -> 16, of which waited for: 6 -> 5; matrix products, arithmetic and copies ran while one was open for 0% -> 0% of each run, Pallas kernels for 14% -> 25%
where the time goes in v2:
time: 72.4 us; the launch traced here: 72.2 us
  Pallas kernels  40.3 us (56%)
  starting transfers between devices  19.5 us (27%)
  waiting for transfers between devices  11.2 us (15%)
  local copies, waits for them, and re-layouts  0.93 us (1%)
    pallas_call x3, Pallas kernels, pool(): pl.pallas_call(functools.partial(pool_kernel, heads, head_dim, first, cou...  26.9 us
    ppermute x11, starting transfers between devices, exchange(): lax.ppermute(array, ('var', 'lon'), [(i, moved(i)) for i in range(devices)])  13.7 us
    ppermute x5, waiting for transfers between devices, neighbour(): return lax.ppermute(array, ('var', 'lat', 'lon'), pairs)  6.96 us
    pallas_call x1, Pallas kernels, on_device(): pl.pallas_call(functools.partial(attend_kernel, heads, len(window)), in_s...  6.03 us
    ppermute x5, starting transfers between devices, neighbour(): return lax.ppermute(array, ('var', 'lat', 'lon'), pairs)  5.76 us
    pallas_call x1, Pallas kernels, on_device(): pl.pallas_call(functools.partial(bias_kernel, rows, columns), in_specs=[s...  4.68 us
    ppermute x11, waiting for transfers between devices, exchange(): lax.ppermute(array, ('var', 'lon'), [(i, moved(i)) for i in range(devices)])  4.23 us
    pallas_call x6, Pallas kernels, merge(): pl.pallas_call(functools.partial(merge_kernel, heads, width, [len(group)...  2.77 us
  transfers between devices with their start and end apart: 16, of which 5 were waited for; matrix products, arithmetic and copies ran while one was open for 0% of the time, Pallas kernels for 25%

profile of v2, /device:TPU:0, one launch (start us, length us, event | category | flops | bytes accessed | tf_op | source)
XLA Modules:
  0.0 72.2 jit_solution(5827173087078021898)
XLA Ops:
  0.0 15.2 %pool.3 = (bf16[4,48,1152]{2,1,0:T(8,128)(2,1)}, bf16[4,48,1152]{2,1,0:T(8,128)(2,1)}, bf16[1024,128]{1,0:T(8,128)(2,1)}) custom-call(s32[1]{0:T(128)} %bitcast.refs_0_, bf16[8,6,96,1024]{3,2,1,0:T(8,128)(2,1)} %refs_1_.6, bf16[1024,1024]{1,0:T(8,128)(2,1)} %refs_2_.6, f32[16,64]{1,0:T(8,128)} %refs_3_.2, bf16[1024,1024]{1,0:T(8,128)(2,1)} %refs_4_.2), custom_call_target="tpu_custom_call" | custom-call | flops 9663676416 | bytes 6291456 | tf_op jit(solution)/shard_map/pool/pallas_call | solution.py:374
  15.2 0.5 collective-permute-start
  15.7 0.0 copy-start
  15.7 5.9 %pool.4 = (bf16[1,48,1152]{2,1,0:T(8,128)(2,1)}, bf16[1,48,1152]{2,1,0:T(8,128)(2,1)}) custom-call(s32[1]{0:T(128)} %bitcast.refs_0_, bf16[8,6,96,1024]{3,2,1,0:T(8,128)(2,1)} %refs_1_.6, bf16[1024,1024]{1,0:T(8,128)(2,1)} %refs_2_.6, bf16[1024,128]{1,0:T(8,128)(2,1)} %get-tuple-element.64.refs_3_), custom_call_target="tpu_custom_call" | custom-call | flops 2415919104 | bytes 1572864 | tf_op jit(solution)/shard_map/pool/pallas_call | solution.py:374
  21.6 0.1 collective-permute-start.2
  21.7 0.0 collective-permute-done.refs_1_
  21.7 0.0 copy-done
  21.7 0.6 merge.6
  22.4 0.0 copy-start.1
  22.4 0.0 copy-start.3
  22.4 0.0 copy-start.4
  22.4 0.0 copy-start.5
  22.4 3.0 %collective-permute-start.1 = (bf16[4,24,1152]{2,1,0:T(8,128)(2,1)S(1)}, bf16[4,24,1152]{2,1,0:T(8,128)(2,1)S(1)}, u32[]{:S(2)}, u32[]{:S(2)}) collective-permute-start(bf16[4,24,1152]{2,1,0:T(8,128)(2,1)S(1)} %get-tuple-element.57), channel_id=1, source_target_pairs={{0,2},{1,3},{2,0},{3,1},{8,10},{9,11},{10,8},{11,9},{16,18},{17,19... | collective-permute-start | bytes 663560 | tf_op jit(solution)/shard_map/ppermute | solution.py:401
  25.4 5.8 %pool.5 = (bf16[1,48,1152]{2,1,0:T(8,128)(2,1)}, bf16[1,48,1152]{2,1,0:T(8,128)(2,1)}) custom-call(s32[1]{0:T(128)} %bitcast.refs_0_, bf16[8,6,96,1024]{3,2,1,0:T(8,128)(2,1)} %refs_1_.6, bf16[1024,1024]{1,0:T(8,128)(2,1)} %refs_2_.6, bf16[1024,128]{1,0:T(8,128)(2,1)} %get-tuple-element.64.refs_3_), custom_call_target="tpu_custom_call" | custom-call | flops 2415919104 | bytes 1572864 | tf_op jit(solution)/shard_map/pool/pallas_call | solution.py:374
  31.2 0.1 collective-permute-start.3
  31.3 0.0 collective-permute-done.2.refs_1_
  31.3 1.5 %collective-permute-done.3.refs_3_ = bf16[1,48,1152]{2,1,0:T(8,128)(2,1)S(1)} collective-permute-done((bf16[1,48,1152]{2,1,0:T(8,128)(2,1)}, bf16[1,48,1152]{2,1,0:T(8,128)(2,1)S(1)}, u32[]{:S(2)}, u32[]{:S(2)}) %collective-permute-start.3) | collective-permute-done | bytes 110624 | tf_op jit(solution)/shard_map/ppermute | solution.py:401
  32.8 0.0 copy-done.1
  32.8 0.0 copy-start.2
  32.8 0.9 %copy-done.2 = bf16[1,48,1152]{2,1,0:T(8,128)(2,1)S(1)} copy-done((bf16[1,48,1152]{2,1,0:T(8,128)(2,1)S(1)}, bf16[1,48,1152]{2,1,0:T(8,128)(2,1)}, u32[]{:S(2)}) %copy-start.2) | copy-done | bytes 110616
  33.7 0.5 merge.8
  34.2 0.0 collective-permute-done.1.refs_1_
  34.2 0.4 merge.7
  34.7 1.6 %collective-permute-start.4 = (bf16[24,1152]{1,0:T(8,128)(2,1)S(1)}, bf16[24,1152]{1,0:T(8,128)(2,1)S(1)}, u32[]{:S(2)}, u32[]{:S(2)}) collective-permute-start(bf16[24,1152]{1,0:T(8,128)(2,1)S(1)} %get-tuple-element.70), channel_id=1, source_target_pairs={{0,8},{1,9},{2,10},{3,11},{8,16},{9,17},{10,18},{11,19},{16,24},{1... | collective-permute-start | bytes 165896 | tf_op jit(solution)/shard_map/ppermute | solution.py:401
  36.3 2.6 %collective-permute-start.5 = (bf16[24,1152]{1,0:T(8,128)(2,1)S(1)}, bf16[24,1152]{1,0:T(8,128)(2,1)S(1)}, u32[]{:S(2)}, u32[]{:S(2)}) collective-permute-start(bf16[24,1152]{1,0:T(8,128)(2,1)S(1)} %get-tuple-element.71), channel_id=1, source_target_pairs={{0,16},{1,17},{2,18},{3,19},{8,24},{9,25},{10,26},{11,27},{16,0},{... | collective-permute-start | bytes 165896 | tf_op jit(solution)/shard_map/ppermute | solution.py:401
  38.9 1.3 %collective-permute-start.6 = (bf16[24,1152]{1,0:T(8,128)(2,1)S(1)}, bf16[24,1152]{1,0:T(8,128)(2,1)S(1)}, u32[]{:S(2)}, u32[]{:S(2)}) collective-permute-start(bf16[24,1152]{1,0:T(8,128)(2,1)S(1)} %get-tuple-element.72), channel_id=1, source_target_pairs={{0,24},{1,25},{2,26},{3,27},{8,0},{9,1},{10,2},{11,3},{16,8},{17,9... | collective-permute-start | bytes 165896 | tf_op jit(solution)/shard_map/ppermute | solution.py:401
  40.2 0.5 collective-permute-start.7
  40.8 0.1 pad_add_fusion.where_ref
  40.9 0.0 copy-done.3
  40.9 0.0 copy-done.4
  40.9 0.0 copy-done.5
  40.9 0.0 copy-start.6
  40.9 4.7 %bias.1 = (f32[16,48,216]{2,1,0:T(8,128)S(1)}, bf16[1024,1024]{1,0:T(8,128)(2,1)S(1)}, bf16[1024,1024]{1,0:T(8,128)(2,1)S(1)}, bf16[1024,1024]{1,0:T(8,128)(2,1)...) custom-call(s32[2]{0:T(128)S(1)} %pad_add_fusion.where_ref, s32[3,216]{1,0:T(4,128)S(1)} %copy-done.5, ...), custom_call_target="tpu_custom_call" | custom-call | flops 1000 | bytes 1000 | tf_op jit(solution)/shard_map/bias/pallas_call | solution.py:451
  45.6 0.0 collective-permute-done.4.refs_1_
  45.6 0.0 collective-permute-done.5.refs_2_
  45.6 0.0 collective-permute-done.6.refs_3_
  45.6 0.4 merge.9
  46.0 0.0 collective-permute-done.7.refs_1_
  46.0 0.4 merge.10
  46.4 0.7 %collective-permute-start.8 = (bf16[12,1152]{1,0:T(8,128)(2,1)S(1)}, bf16[12,1152]{1,0:T(8,128)(2,1)S(1)}, u32[]{:S(2)}, u32[]{:S(2)}) collective-permute-start(bf16[12,1152]{1,0:T(8,128)(2,1)S(1)} %get-tuple-element.88), channel_id=1, source_target_pairs={{0,8},{1,9},{2,10},{3,11},{8,16},{9,17},{10,18},{11,19},{16,24},{1... | collective-permute-start | bytes 82952 | tf_op jit(solution)/shard_map/ppermute | solution.py:401
  47.1 0.5 collective-permute-start.9
  47.6 2.7 %collective-permute-start.10 = (bf16[12,1152]{1,0:T(8,128)(2,1)S(1)}, bf16[12,1152]{1,0:T(8,128)(2,1)S(1)}, u32[]{:S(2)}, u32[]{:S(2)}) collective-permute-start(bf16[12,1152]{1,0:T(8,128)(2,1)S(1)} %get-tuple-element.90), channel_id=1, source_target_pairs={{0,24},{1,25},{2,26},{3,27},{8,0},{9,1},{10,2},{11,3},{16,8},{17,9... | collective-permute-start | bytes 82952 | tf_op jit(solution)/shard_map/ppermute | solution.py:401
  50.3 2.0 %collective-permute-done.8.refs_1_ = bf16[12,1152]{1,0:T(8,128)(2,1)S(1)} collective-permute-done((bf16[12,1152]{1,0:T(8,128)(2,1)S(1)}, bf16[12,1152]{1,0:T(8,128)(2,1)S(1)}, u32[]{:S(2)}, u32[]{:S(2)}) %collective-permute-start.8) | collective-permute-done | bytes 27680 | tf_op jit(solution)/shard_map/ppermute | solution.py:401
  52.3 0.7 collective-permute-done.9.refs_2_
  53.0 0.0 collective-permute-done.10.refs_3_
  53.0 0.4 merge.11
  53.4 2.2 %collective-permute-start.15 = (bf16[36,1024]{1,0:T(8,128)(2,1)S(1)}, bf16[36,1024]{1,0:T(8,128)(2,1)S(1)}, u32[]{:S(2)}, u32[]{:S(2)}) collective-permute-start(bf16[36,1024]{1,0:T(8,128)(2,1)S(1)} %pad_maximum_fusion.refs_0_), channel_id=1, source_target_pairs={{5,0},{6,1},{7,2},{12,3},{1,4},{2,5},{3,6},{8,7},{13,8},{14,9},{15... | collective-permute-start | bytes 221192 | tf_op jit(solution)/shard_map/ppermute | solution.py:488
  55.6 3.1 %collective-permute-start.14 = (bf16[36,1024]{1,0:T(8,128)(2,1)S(1)}, bf16[36,1024]{1,0:T(8,128)(2,1)S(1)}, u32[]{:S(2)}, u32[]{:S(2)}) collective-permute-start(bf16[36,1024]{1,0:T(8,128)(2,1)S(1)} %pad_maximum_fusion.refs_0_), channel_id=1, source_target_pairs={{1,0},{2,1},{3,2},{8,3},{5,4},{6,5},{7,6},{12,7},{9,8},{10,9},{11,... | collective-permute-start | bytes 221192 | tf_op jit(solution)/shard_map/ppermute | solution.py:488
  58.7 0.0 collective-permute-start.13
  58.7 0.0 collective-permute-start.12
  58.7 0.5 collective-permute-start.11
  59.2 0.0 collective-permute-done.15.refs_5_
  59.2 1.6 %collective-permute-done.14.refs_4_ = bf16[36,1024]{1,0:T(8,128)(2,1)S(1)} collective-permute-done((bf16[36,1024]{1,0:T(8,128)(2,1)S(1)}, bf16[36,1024]{1,0:T(8,128)(2,1)S(1)}, u32[]{:S(2)}, u32[]{:S(2)}) %collective-permute-start.14) | collective-permute-done | bytes 73760 | tf_op jit(solution)/shard_map/ppermute | solution.py:488
  60.8 5.4 %collective-permute-done.13.refs_3_ = bf16[36,1024]{1,0:T(8,128)(2,1)S(1)} collective-permute-done((bf16[36,1024]{1,0:T(8,128)(2,1)S(1)}, bf16[36,1024]{1,0:T(8,128)(2,1)S(1)}, u32[]{:S(2)}, u32[]{:S(2)}) %collective-permute-start.13) | collective-permute-done | bytes 73760 | tf_op jit(solution)/shard_map/ppermute | solution.py:488
  66.2 0.0 collective-permute-done.12.refs_2_
  66.2 0.0 collective-permute-done.11.refs_1_
  66.2 0.0 copy-done.6
  66.2 6.0 %attend.1 = bf16[6,6,1024]{2,1,0:T(8,128)(2,1)} custom-call(bf16[36,1024]{1,0:T(8,128)(2,1)S(1)} %pad_maximum_fusion.refs_0_, bf16[36,1024]{1,0:T(8,128)(2,1)S(1)} %collective-permute-done.11.refs_1_, bf16[36,1024]{1,0:T(8,128)(2,1)S(1)} %collective-permute-done.12.refs_2_, bf16[36,1024]{1,0:T(8,128)(2,1)S(1)} %collective-permute-done.13.refs_3_, ...), custom_call_target="tpu_custom_call" | custom-call | tf_op jit(solution)/shard_map/attend/pallas_call | solution.py:492
  (1 shorter events, 0.0 us)
Async XLA Ops:
  15.2 6.5 %collective-permute-start = (bf16[4,48,1152]{2,1,0:T(8,128)(2,1)}, bf16[4,48,1152]{2,1,0:T(8,128)(2,1)S(1)}, u32[]{:S(2)}, u32[]{:S(2)}) collective-permute-start(bf16[4,48,1152]{2,1,0:T(8,128)(2,1)} %get-tuple-element.52), channel_id=1, source_target_pairs={{0,1},{1,0},{2,3},{3,2},{8,9},{9,8},{10,11},{11,10},{16,17},{17,16... | collective-permute-start | bytes 1327112 | tf_op jit(solution)/shard_map/ppermute | solution.py:401
  15.7 6.0 %copy-start = (bf16[4,48,1152]{2,1,0:T(8,128)(2,1)S(1)}, bf16[4,48,1152]{2,1,0:T(8,128)(2,1)}, u32[]{:S(2)}) copy-start(bf16[4,48,1152]{2,1,0:T(8,128)(2,1)} %get-tuple-element.51.refs_0_) | copy-start | bytes 1327108
  21.6 9.7 %collective-permute-start.2 = (bf16[1,48,1152]{2,1,0:T(8,128)(2,1)}, bf16[1,48,1152]{2,1,0:T(8,128)(2,1)S(1)}, u32[]{:S(2)}, u32[]{:S(2)}) collective-permute-start(bf16[1,48,1152]{2,1,0:T(8,128)(2,1)} %get-tuple-element.63), channel_id=1, source_target_pairs={{0,1},{1,0},{2,3},{3,2},{8,9},{9,8},{10,11},{11,10},{16,17},{17,16... | collective-permute-start | bytes 331784 | tf_op jit(solution)/shard_map/ppermute | solution.py:401
  22.4 10.5 %copy-start.1 = (bf16[1,48,1152]{2,1,0:T(8,128)(2,1)S(1)}, bf16[1,48,1152]{2,1,0:T(8,128)(2,1)}, u32[]{:S(2)}) copy-start(bf16[1,48,1152]{2,1,0:T(8,128)(2,1)} %get-tuple-element.62.refs_0_) | copy-start | bytes 331780
  22.4 18.5 %copy-start.3 = (f32[16,13,13]{2,0,1:T(8,128)S(1)}, f32[16,13,13]{2,0,1:T(8,128)}, u32[]{:S(2)}) copy-start(f32[16,13,13]{2,0,1:T(8,128)} %param.23) | copy-start | bytes 32452
  22.4 18.5 %copy-start.4 = (s32[12,96]{1,0:T(8,128)S(1)}, s32[12,96]{1,0:T(8,128)}, u32[]{:S(2)}) copy-start(s32[12,96]{1,0:T(8,128)} %valid_ref.1) | copy-start | bytes 13828
  22.4 18.5 %copy-start.5 = (s32[3,216]{1,0:T(4,128)S(1)}, s32[3,216]{1,0:T(4,128)}, u32[]{:S(2)}) copy-start(s32[3,216]{1,0:T(4,128)} %constant.16.clone.meta_ref) | copy-start | bytes 7780
  22.4 11.8 %collective-permute-start.1 = (bf16[4,24,1152]{2,1,0:T(8,128)(2,1)S(1)}, bf16[4,24,1152]{2,1,0:T(8,128)(2,1)S(1)}, u32[]{:S(2)}, u32[]{:S(2)}) collective-permute-start(bf16[4,24,1152]{2,1,0:T(8,128)(2,1)S(1)} %get-tuple-element.57), channel_id=1, source_target_pairs={{0,2},{1,3},{2,0},{3,1},{8,10},{9,11},{10,8},{11,9},{16,18},{17,19... | collective-permute-start | bytes 663560 | tf_op jit(solution)/shard_map/ppermute | solution.py:401
  31.2 1.6 %collective-permute-start.3 = (bf16[1,48,1152]{2,1,0:T(8,128)(2,1)}, bf16[1,48,1152]{2,1,0:T(8,128)(2,1)S(1)}, u32[]{:S(2)}, u32[]{:S(2)}) collective-permute-start(bf16[1,48,1152]{2,1,0:T(8,128)(2,1)} %get-tuple-element.66), channel_id=1, source_target_pairs={{0,1},{1,0},{2,3},{3,2},{8,9},{9,8},{10,11},{11,10},{16,17},{17,16... | collective-permute-start | bytes 331784 | tf_op jit(solution)/shard_map/ppermute | solution.py:401
  32.8 0.9 %copy-start.2 = (bf16[1,48,1152]{2,1,0:T(8,128)(2,1)S(1)}, bf16[1,48,1152]{2,1,0:T(8,128)(2,1)}, u32[]{:S(2)}) copy-start(bf16[1,48,1152]{2,1,0:T(8,128)(2,1)} %get-tuple-element.65.refs_2_) | copy-start | bytes 331780
  34.7 10.9 %collective-permute-start.4 = (bf16[24,1152]{1,0:T(8,128)(2,1)S(1)}, bf16[24,1152]{1,0:T(8,128)(2,1)S(1)}, u32[]{:S(2)}, u32[]{:S(2)}) collective-permute-start(bf16[24,1152]{1,0:T(8,128)(2,1)S(1)} %get-tuple-element.70), channel_id=1, source_target_pairs={{0,8},{1,9},{2,10},{3,11},{8,16},{9,17},{10,18},{11,19},{16,24},{1... | collective-permute-start | bytes 165896 | tf_op jit(solution)/shard_map/ppermute | solution.py:401
  36.3 9.3 %collective-permute-start.5 = (bf16[24,1152]{1,0:T(8,128)(2,1)S(1)}, bf16[24,1152]{1,0:T(8,128)(2,1)S(1)}, u32[]{:S(2)}, u32[]{:S(2)}) collective-permute-start(bf16[24,1152]{1,0:T(8,128)(2,1)S(1)} %get-tuple-element.71), channel_id=1, source_target_pairs={{0,16},{1,17},{2,18},{3,19},{8,24},{9,25},{10,26},{11,27},{16,0},{... | collective-permute-start | bytes 165896 | tf_op jit(solution)/shard_map/ppermute | solution.py:401
  38.9 6.7 %collective-permute-start.6 = (bf16[24,1152]{1,0:T(8,128)(2,1)S(1)}, bf16[24,1152]{1,0:T(8,128)(2,1)S(1)}, u32[]{:S(2)}, u32[]{:S(2)}) collective-permute-start(bf16[24,1152]{1,0:T(8,128)(2,1)S(1)} %get-tuple-element.72), channel_id=1, source_target_pairs={{0,24},{1,25},{2,26},{3,27},{8,0},{9,1},{10,2},{11,3},{16,8},{17,9... | collective-permute-start | bytes 165896 | tf_op jit(solution)/shard_map/ppermute | solution.py:401
  40.2 5.8 %collective-permute-start.7 = (bf16[2,24,1152]{2,1,0:T(8,128)(2,1)S(1)}, bf16[2,24,1152]{2,1,0:T(8,128)(2,1)S(1)}, u32[]{:S(2)}, u32[]{:S(2)}) collective-permute-start(bf16[2,24,1152]{2,1,0:T(8,128)(2,1)S(1)} %get-tuple-element.74), channel_id=1, source_target_pairs={{0,2},{1,3},{2,0},{3,1},{8,10},{9,11},{10,8},{11,9},{16,18},{17,19... | collective-permute-start | bytes 331784 | tf_op jit(solution)/shard_map/ppermute | solution.py:401
  40.9 25.3 %copy-start.6 = (f32[1024]{0:T(1024)S(1)}, f32[1024]{0:T(1024)}, u32[]{:S(2)}) copy-start(f32[1024]{0:T(1024)} %param.18) | copy-start | bytes 12292
  46.4 5.9 %collective-permute-start.8 = (bf16[12,1152]{1,0:T(8,128)(2,1)S(1)}, bf16[12,1152]{1,0:T(8,128)(2,1)S(1)}, u32[]{:S(2)}, u32[]{:S(2)}) collective-permute-start(bf16[12,1152]{1,0:T(8,128)(2,1)S(1)} %get-tuple-element.88), channel_id=1, source_target_pairs={{0,8},{1,9},{2,10},{3,11},{8,16},{9,17},{10,18},{11,19},{16,24},{1... | collective-permute-start | bytes 82952 | tf_op jit(solution)/shard_map/ppermute | solution.py:401
  47.1 5.9 %collective-permute-start.9 = (bf16[12,1152]{1,0:T(8,128)(2,1)S(1)}, bf16[12,1152]{1,0:T(8,128)(2,1)S(1)}, u32[]{:S(2)}, u32[]{:S(2)}) collective-permute-start(bf16[12,1152]{1,0:T(8,128)(2,1)S(1)} %get-tuple-element.89), channel_id=1, source_target_pairs={{0,16},{1,17},{2,18},{3,19},{8,24},{9,25},{10,26},{11,27},{16,0},{... | collective-permute-start | bytes 82952 | tf_op jit(solution)/shard_map/ppermute | solution.py:401
  47.6 5.4 %collective-permute-start.10 = (bf16[12,1152]{1,0:T(8,128)(2,1)S(1)}, bf16[12,1152]{1,0:T(8,128)(2,1)S(1)}, u32[]{:S(2)}, u32[]{:S(2)}) collective-permute-start(bf16[12,1152]{1,0:T(8,128)(2,1)S(1)} %get-tuple-element.90), channel_id=1, source_target_pairs={{0,24},{1,25},{2,26},{3,27},{8,0},{9,1},{10,2},{11,3},{16,8},{17,9... | collective-permute-start | bytes 82952 | tf_op jit(solution)/shard_map/ppermute | solution.py:401
  53.4 5.8 %collective-permute-start.15 = (bf16[36,1024]{1,0:T(8,128)(2,1)S(1)}, bf16[36,1024]{1,0:T(8,128)(2,1)S(1)}, u32[]{:S(2)}, u32[]{:S(2)}) collective-permute-start(bf16[36,1024]{1,0:T(8,128)(2,1)S(1)} %pad_maximum_fusion.refs_0_), channel_id=1, source_target_pairs={{5,0},{6,1},{7,2},{12,3},{1,4},{2,5},{3,6},{8,7},{13,8},{14,9},{15... | collective-permute-start | bytes 221192 | tf_op jit(solution)/shard_map/ppermute | solution.py:488
  55.6 5.1 %collective-permute-start.14 = (bf16[36,1024]{1,0:T(8,128)(2,1)S(1)}, bf16[36,1024]{1,0:T(8,128)(2,1)S(1)}, u32[]{:S(2)}, u32[]{:S(2)}) collective-permute-start(bf16[36,1024]{1,0:T(8,128)(2,1)S(1)} %pad_maximum_fusion.refs_0_), channel_id=1, source_target_pairs={{1,0},{2,1},{3,2},{8,3},{5,4},{6,5},{7,6},{12,7},{9,8},{10,9},{11,... | collective-permute-start | bytes 221192 | tf_op jit(solution)/shard_map/ppermute | solution.py:488
  58.7 7.5 %collective-permute-start.13 = (bf16[36,1024]{1,0:T(8,128)(2,1)S(1)}, bf16[36,1024]{1,0:T(8,128)(2,1)S(1)}, u32[]{:S(2)}, u32[]{:S(2)}) collective-permute-start(bf16[36,1024]{1,0:T(8,128)(2,1)S(1)} %pad_maximum_fusion.refs_0_), channel_id=1, source_target_pairs={{31,0},{4,1},{5,2},{6,3},{27,4},{0,5},{1,6},{2,7},{7,8},{12,9},{13... | collective-permute-start | bytes 221192 | tf_op jit(solution)/shard_map/ppermute | solution.py:488
  58.7 7.5 %collective-permute-start.12 = (bf16[36,1024]{1,0:T(8,128)(2,1)S(1)}, bf16[36,1024]{1,0:T(8,128)(2,1)S(1)}, u32[]{:S(2)}, u32[]{:S(2)}) collective-permute-start(bf16[36,1024]{1,0:T(8,128)(2,1)S(1)} %pad_maximum_fusion.refs_0_), channel_id=1, source_target_pairs={{27,0},{0,1},{1,2},{2,3},{31,4},{4,5},{5,6},{6,7},{3,8},{8,9},{9,1... | collective-permute-start | bytes 221192 | tf_op jit(solution)/shard_map/ppermute | solution.py:488
  58.7 7.5 %collective-permute-start.11 = (bf16[36,1024]{1,0:T(8,128)(2,1)S(1)}, bf16[36,1024]{1,0:T(8,128)(2,1)S(1)}, u32[]{:S(2)}, u32[]{:S(2)}) collective-permute-start(bf16[36,1024]{1,0:T(8,128)(2,1)S(1)} %pad_maximum_fusion.refs_0_), channel_id=1, source_target_pairs={{4,0},{5,1},{6,2},{7,3},{0,4},{1,5},{2,6},{3,7},{12,8},{13,9},{14,... | collective-permute-start | bytes 221192 | tf_op jit(solution)/shard_map/ppermute | solution.py:488

commit v3 on v2

--- a/solution.py
+++ b/solution.py
@@ -16,7 +16,9 @@
 RADICES = (2, 2, 4)
 QROWS = 48
 MIB = 1 << 20
-POOL_VMEM = 60 * MIB
+PRE_VMEM = 50 * MIB
+LEAD_VMEM = 40 * MIB
+POOL_VMEM = 30 * MIB
 MERGE_VMEM = 12 * MIB
 STAGE_VMEM = 42 * MIB
 F32 = jnp.float32
@@ -106,78 +108,123 @@
     return jnp.where(source == wanted, 1.0, 0.0).astype(BF16)
 
 
-def pool_kernel(heads, head_dim, first, count, tiles, columns, lead, *refs):
-    block_ref, token_ref, value_ref = refs[:3]
-    if lead:
-        query_ref, key_ref, keep_ref, send_ref, fold_ref = refs[3:8]
-        slots, held, sems, held_key = refs[8:]
-    else:
-        fold_ref, keep_ref, send_ref = refs[3:6]
-        slots, held, sems = refs[6:]
-    _, variables, tile, width = slots.shape
+def pool_rows(heads, head_dim, block, order, tokens, fold_ref, values, keep_ref, send_ref, place):
+    variables, tile, width = tokens.shape
+    half = tile // RADICES[0]
+    lane = lane_iota((variables * tile, LANES))
+    flat = tokens.reshape(variables * tile, width)
+    score = unpack3(dot(flat, fold_ref[...]), heads)
+    score = score.reshape(variables, tile, LANES)
+    top = jnp.max(score, axis=0)
+    raised = jnp.exp(score - top[None])
+    total = jnp.sum(raised, axis=0)
+    share = raised.reshape(variables * tile, LANES)
+    pooled = []
+    wide = 256
+    for start in range(0, width, wide):
+        rows = dot(flat, values(start, wide))
+        for low in range(0, wide, LANES):
+            index = (start + low) // head_dim + jnp.where(lane >= head_dim, 1, 0)
+            spread = jnp.take_along_axis(share, index, axis=1)
+            part = rows[:, low : low + LANES] * spread
+            pooled.append(jnp.sum(part.reshape(variables, tile, LANES), axis=0).astype(BF16))
+    pooled.append(encode_stats(top, total, heads).astype(BF16))
+    ordered = dot(order, jnp.concatenate(pooled, axis=1)).astype(BF16)
+    keep_ref[place] = ordered[:half]
+    send_ref[place] = ordered[half:]
+
+
+def pre_kernel(heads, head_dim, token_ref, value_ref, query_ref, key_ref, *refs):
+    fold_ref, held, first_ref, query, held_key, sems = refs
+    tile = first_ref.shape[1]
+    copies = [
+        pltpu.make_async_copy(query_ref, query, sems.at[0]),
+        pltpu.make_async_copy(key_ref, held_key, sems.at[1]),
+        pltpu.make_async_copy(token_ref.at[:, 0, pl.ds(0, tile), :], first_ref, sems.at[2]),
+        pltpu.make_async_copy(value_ref, held, sems.at[3]),
+    ]
+    for copy in copies:
+        copy.start()
+    for copy in copies[:2]:
+        copy.wait()
+    scaled = query[...] * (1.0 / math.sqrt(head_dim))
+    fold_ref[...] = fold(scaled, held_key[...], heads, head_dim)
+    for copy in copies[2:]:
+        copy.wait()
+
+
+def lead_kernel(heads, head_dim, count, tiles, columns, *refs):
+    block_ref, token_ref, first_ref, held, fold_ref = refs[:5]
+    keep_ref, send_ref, rest_ref, slots, sems = refs[5:]
+    tile = slots.shape[2]
     steps = count * tiles
     block = block_ref[0]
     high = block // TILE_BLOCKS
 
     def fetch(step):
-        row = first + step // tiles
         start = pl.multiple_of((step % tiles) * tile, tile)
         return pltpu.make_async_copy(
-            token_ref.at[:, row, pl.ds(start, tile), :],
+            token_ref.at[:, step // tiles, pl.ds(start, tile), :],
             slots.at[step % 2],
             sems.at[step % 2],
         )
 
-    values = pltpu.make_async_copy(value_ref, held, sems.at[2])
-    if lead:
-        key = pltpu.make_async_copy(key_ref, held_key, sems.at[3])
-        key.start()
-    fetch(0).start()
-    values.start()
+    later = rest_ref.shape[1]
+    rest = pltpu.make_async_copy(token_ref.at[:, pl.ds(count, later)], rest_ref, sems.at[2])
+    fetch(1).start()
     order = column_order(block, tile, columns)
-    half = tile // RADICES[0]
-    lane = lane_iota((variables * tile, LANES))
-    if lead:
-        key.wait()
-        query = query_ref[...] * (1.0 / math.sqrt(head_dim))
-        fold_ref[...] = fold(query, held_key[...], heads, head_dim)
+
+    def work(step, tokens):
+        pool_rows(
+            heads,
+            head_dim,
+            block,
+            order,
+            tokens,
+            fold_ref,
+            lambda start, wide: held[:, start : start + wide],
+            keep_ref,
+            send_ref,
+            (step // tiles) * tiles + (step % tiles + tiles - high) % tiles,
+        )
+
+    work(0, first_ref[...])
+    fetch(2).start()
+    rest.start()
 
     def body(step, _):
-        @pl.when(step + 1 < steps)
+        fetch(step).wait()
+        work(step, slots[step % 2])
+
+        @pl.when(step + 2 < steps)
         def _():
-            fetch(step + 1).start()
-
-        fetch(step).wait()
-        tokens = slots[step % 2].reshape(variables * tile, width)
-        score = unpack3(dot(tokens, fold_ref[...]), heads)
-        score = score.reshape(variables, tile, LANES)
-        top = jnp.max(score, axis=0)
-        raised = jnp.exp(score - top[None])
-        total = jnp.sum(raised, axis=0)
-        share = raised.reshape(variables * tile, LANES)
-
-        @pl.when(step == 0)
-        def _():
-            values.wait()
-
-        pooled = []
-        wide = 256
-        for start in range(0, width, wide):
-            rows = dot(tokens, held[:, start : start + wide])
-            for low in range(0, wide, LANES):
-                head = (start + low) // head_dim
-                index = head + jnp.where(lane >= head_dim, 1, 0)
-                spread = jnp.take_along_axis(share, index, axis=1)
-                part = rows[:, low : low + LANES] * spread
-                pooled.append(jnp.sum(part.reshape(variables, tile, LANES), axis=0).astype(BF16))
-        pooled.append(encode_stats(top, total, heads).astype(BF16))
-        ordered = dot(order, jnp.concatenate(pooled, axis=1)).astype(BF16)
-        place = (step // tiles) * tiles + (step % tiles + tiles - high) % tiles
-        keep_ref[place] = ordered[:half]
-        send_ref[place] = ordered[half:]
+            fetch(step + 2).start()
+
         return 0
 
-    lax.fori_loop(0, steps, body, 0)
+    lax.fori_loop(1, steps, body, 0)
+    rest.wait()
+
+
+def pool_kernel(heads, head_dim, row, tiles, columns, *refs):
+    block_ref, rest_ref, held, fold_ref, keep_ref, send_ref = refs
+    block = block_ref[0]
+    high = block // TILE_BLOCKS
+    tile = rest_ref.shape[2] // tiles
+    order = column_order(block, tile, columns)
+    for step in range(tiles):
+        pool_rows(
+            heads,
+            head_dim,
+            block,
+            order,
+            rest_ref[:, row, step * tile : (step + 1) * tile],
+            fold_ref,
+            lambda start, wide: held[:, start : start + wide],
+            keep_ref,
+            send_ref,
+            (step + tiles - high) % tiles,
+        )
 
 
 def merge_body(parts, heads, width, last):
@@ -245,10 +292,13 @@
     )(*parts)
 
 
-def bias_kernel(rows, columns, where_ref, meta_ref, valid_ref, table_ref, *refs):
-    out_ref, sems = refs[5], refs[11]
+def stage_kernel(rows, columns, count, *refs):
+    where_ref, meta_ref, valid_ref, table_ref = refs[:4]
+    sources, out_ref = refs[4 : 4 + count], refs[4 + count]
+    targets, sems = refs[5 + count : 5 + 2 * count], refs[5 + 2 * count]
     copies = [
-        pltpu.make_async_copy(refs[at], refs[6 + at], sems.at[at]) for at in range(5)
+        pltpu.make_async_copy(source, target, sems.at[at])
+        for at, (source, target) in enumerate(zip(sources, targets))
     ]
     for copy in copies:
         copy.start()
@@ -307,21 +357,24 @@
     normed = (center * lax.rsqrt(variance + EPS) * gain_ref[...]).astype(BF16)
     queries = dot(normed[:QROWS], w_query[...]).astype(BF16)
     keys = dot(normed, w_key[...]).astype(BF16)
-    values = dot(normed, w_value[...]).astype(BF16)
-    lane = lane_iota((QROWS, LANES))
-    left = lane < LANES // 2
-    for pair in range(heads // 2):
-        at = slice(pair * LANES, (pair + 1) * LANES)
+    left = lane_iota((QROWS, LANES)) < LANES // 2
+    pairs = [slice(at, at + LANES) for at in range(0, width, LANES)]
+    logits = []
+    for at in pairs:
         query = queries[:, at]
         zero = jnp.zeros_like(query)
         both = jnp.concatenate([jnp.where(left, query, zero), jnp.where(left, zero, query)], axis=0)
-        logit = dot_nt(both, keys[:, at]) * scale
+        logits.append(dot_nt(both, keys[:, at]))
+    values = dot(normed, w_value[...]).astype(BF16)
+    shares = []
+    for pair, logit in enumerate(logits):
         bias = bias_ref[2 * pair : 2 * pair + 2]
-        logit = logit + bias.reshape(2 * QROWS, bias.shape[-1])
+        logit = logit * scale + bias.reshape(2 * QROWS, bias.shape[-1])
         raised = jnp.exp(logit - jnp.max(logit, axis=-1, keepdims=True))
-        attn = (raised / jnp.sum(raised, axis=-1, keepdims=True)).astype(BF16)
-        mixed = dot(attn, values[:, at])
-        mix[:, at] = jnp.where(left, mixed[:QROWS], mixed[QROWS:]).astype(BF16)
+        shares.append((raised / jnp.sum(raised, axis=-1, keepdims=True)).astype(BF16))
+    mixed = [dot(share, values[:, at]) for share, at in zip(shares, pairs)]
+    for at, rows in zip(pairs, mixed):
+        mix[:, at] = jnp.where(left, rows[:QROWS], rows[QROWS:]).astype(BF16)
     result = tokens[:QROWS].astype(F32) + dot(mix[...], w_out[...])
     rows, columns, _ = out_ref.shape
     for row in range(rows):
@@ -365,33 +418,57 @@
     vmem = pl.BlockSpec(memory_space=pltpu.VMEM)
     hbm = pl.BlockSpec(memory_space=pltpu.HBM)
 
-    def pool(first, count, folded):
-        lead = folded is None
-        shape = jax.ShapeDtypeStruct((count * tiles, half, packed), BF16)
-        outs = [shape, shape] + [jax.ShapeDtypeStruct((width, LANES), BF16)] * lead
-        extra = (var_query, agg_key) if lead else (folded,)
-        square = pltpu.VMEM((width, width), BF16)
-        return pl.pallas_call(
-            functools.partial(
-                pool_kernel, heads, head_dim, first, count, tiles, columns, lead
-            ),
-            in_specs=[smem, hbm, hbm] + ([vmem, hbm] if lead else [vmem]),
-            out_specs=[vmem] * len(outs),
-            out_shape=outs,
+    weight = jax.ShapeDtypeStruct((width, width), BF16)
+    lead_rows = rows - 2
+
+    def pool_cost(count):
+        work = count * total_columns * local_vars * width
+        return pl.CostEstimate(flops=3 * work * width, bytes_accessed=2 * work, transcendentals=0)
+
+    def lead_pool():
+        folded = jax.ShapeDtypeStruct((width, LANES), BF16)
+        first = jax.ShapeDtypeStruct((local_vars, tile, width), BF16)
+        folded, held, first = pl.pallas_call(
+            functools.partial(pre_kernel, heads, head_dim),
+            in_specs=[hbm] * 4,
+            out_specs=[vmem] * 3,
+            out_shape=[folded, weight, first],
+            scratch_shapes=[
+                pltpu.VMEM(var_query.shape, F32),
+                pltpu.VMEM((width, width), BF16),
+                pltpu.SemaphoreType.DMA((4,)),
+            ],
+            compiler_params=pltpu.CompilerParams(vmem_limit_bytes=PRE_VMEM),
+            name="pre",
+        )(var_tokens, agg_value, var_query, agg_key)
+        shape = jax.ShapeDtypeStruct((lead_rows * tiles, half, packed), BF16)
+        later = (local_vars, rows - lead_rows, total_columns, width)
+        keep, send, rest = pl.pallas_call(
+            functools.partial(lead_kernel, heads, head_dim, lead_rows, tiles, columns),
+            in_specs=[smem, hbm, vmem, vmem, vmem],
+            out_specs=[vmem] * 3,
+            out_shape=[shape, shape, jax.ShapeDtypeStruct(later, BF16)],
             scratch_shapes=[
                 pltpu.VMEM((2, local_vars, tile, width), BF16),
-                square,
-                pltpu.SemaphoreType.DMA((4,)),
-            ]
-            + [square] * lead,
+                pltpu.SemaphoreType.DMA((3,)),
+            ],
+            compiler_params=pltpu.CompilerParams(vmem_limit_bytes=LEAD_VMEM),
+            cost_estimate=pool_cost(lead_rows),
+            name="lead",
+        )(block, var_tokens, first, held, folded)
+        return keep, send, folded, held, rest
+
+    def pool(row, rest, held, folded):
+        shape = jax.ShapeDtypeStruct((tiles, half, packed), BF16)
+        return pl.pallas_call(
+            functools.partial(pool_kernel, heads, head_dim, row, tiles, columns),
+            in_specs=[smem] + [vmem] * 3,
+            out_specs=[vmem] * 2,
+            out_shape=[shape] * 2,
             compiler_params=pltpu.CompilerParams(vmem_limit_bytes=POOL_VMEM),
-            cost_estimate=pl.CostEstimate(
-                flops=3 * count * total_columns * local_vars * width * width,
-                bytes_accessed=2 * count * total_columns * local_vars * width,
-                transcendentals=0,
-            ),
+            cost_estimate=pool_cost(1),
             name="pool",
-        )(block, var_tokens, agg_value, *extra)
+        )(block, rest, held, folded)
 
     def exchange(array, shift, stride, radix):
         def moved(i):
@@ -425,16 +502,14 @@
         return [full[:, k].reshape(places // tiles * size, packed) for k in range(tiles)]
 
     barrier = lax.optimization_barrier
-    lead_rows = rows - 2
-    keep_a, send_a, folded = pool(0, lead_rows, None)
+    keep_a, send_a, folded, held, rest = lead_pool()
     got_a = swap([send_a], 0)
-    keep_b, send_b = pool(lead_rows, 1, folded)
-    size = half
-    parts_a = next_split([[keep_a] + got_a], 0, lead_rows * tiles, size)
+    keep_b, send_b = pool(0, rest, held, folded)
+    parts_a = next_split([[keep_a] + got_a], 0, lead_rows * tiles, half)
     got_b = swap([send_b], 0)
     parts_a, folded = barrier((parts_a, folded))
     got_a = swap(parts_a[1:], 1)
-    keep_c, send_c = pool(lead_rows + 1, 1, folded)
+    keep_c, send_c = pool(1, rest, held, folded)
     got_c = swap([send_c], 0)
     keep_a = parts_a[0]
     keep_b = [[keep_b] + got_b, [keep_c] + got_c]
@@ -447,33 +522,17 @@
     column = np.tile(np.arange(columns), len(places) * rows)
     meta = jnp.asarray(np.stack([row, dl, dx * columns + column]), jnp.int32)
     keys = len(places) * patch
-    weights = (agg_out, nb_query, nb_key, nb_value, nb_out)
-    bias, *weights = pl.pallas_call(
-        functools.partial(bias_kernel, rows, columns),
-        in_specs=[smem, vmem, vmem, vmem] + [hbm] * 5,
-        out_specs=[vmem] * 6,
-        out_shape=[jax.ShapeDtypeStruct((heads, QROWS, keys), F32)]
-        + [jax.ShapeDtypeStruct(weight.shape, weight.dtype) for weight in weights],
-        scratch_shapes=[pltpu.SemaphoreType.DMA((5,))],
-        compiler_params=pltpu.CompilerParams(vmem_limit_bytes=STAGE_VMEM),
-        cost_estimate=pl.CostEstimate(
-            flops=1000, bytes_accessed=1000, transcendentals=0
-        ),
-        name="bias",
-    )(where, meta, valid, jnp.transpose(pos_bias, (1, 0, 2)), *weights)
-
     for number in range(1, len(stages)):
-        parts_a = next_split(
-            [[keep_a] + got_a], number, lead_rows * tiles, half // split_before(stages, number)
-        )
-        parts_b = next_split(keep_b, number - 1, 2 * tiles, half // split_before(stages, number - 1))
-        parts_a, parts_b = barrier((parts_a, parts_b))
+        split_b, split_a = split_before(stages, number - 1), split_before(stages, number)
+        parts_b = next_split(keep_b, number - 1, 2 * tiles, half // split_b)
+        if number > 1:
+            got_a, _ = barrier((got_a, parts_b))
+        parts_a = next_split([[keep_a] + got_a], number, lead_rows * tiles, half // split_a)
+        if number == 1:
+            parts_a, parts_b = barrier((parts_a, parts_b))
         if number + 1 < len(stages):
             keep_a, got_a = parts_a[0], swap(parts_a[1:], number + 1)
-        got = swap(parts_b[1:], number)
-        if number == 1:
-            got, bias, weights = barrier((got, bias, weights))
-        keep_b = [[parts_b[0]] + got]
+        keep_b = [[parts_b[0]] + swap(parts_b[1:], number)]
     pooled_a = parts_a[0]
     (pooled_b,) = next_split(keep_b, len(stages) - 1, 2 * tiles, columns)
     pooled = jnp.concatenate([pooled_a, pooled_b], axis=0)
@@ -487,6 +546,20 @@
             pairs.append((source, i))
         return lax.ppermute(array, ("var", "lat", "lon"), pairs)
 
+    weights = (agg_out, nb_query, nb_key, nb_value, nb_out)
+    pooled, where = barrier((pooled, where))
+    bias, *weights = pl.pallas_call(
+        functools.partial(stage_kernel, rows, columns, len(weights)),
+        in_specs=[smem, vmem, vmem, vmem] + [hbm] * len(weights),
+        out_specs=[vmem] * (1 + len(weights)),
+        out_shape=[jax.ShapeDtypeStruct((heads, QROWS, keys), F32)] + [weight] * len(weights),
+        scratch_shapes=[pltpu.SemaphoreType.DMA((len(weights),))],
+        compiler_params=pltpu.CompilerParams(vmem_limit_bytes=STAGE_VMEM),
+        cost_estimate=pl.CostEstimate(
+            flops=1000, bytes_accessed=10 * width * width, transcendentals=0
+        ),
+        name="stage",
+    )(where, meta, valid, jnp.transpose(pos_bias, (1, 0, 2)), *weights)
     window = [pooled] + [neighbour(pooled, dl, dx) for dl, dx in places[1:]]
 
     return pl.pallas_call(

time: 72.4 us -> 58.1 us (0.80)
  Pallas kernels: 40.3 us -> 29.7 us
  waiting for transfers between devices: 11.2 us -> 6.87 us
  starting transfers between devices: 19.5 us -> 20.3 us
    pallas_call x4 -> x5, Pallas kernels: 31.5 us -> 23.1 us  [the longest x1 10.8 us: lead_pool(): pl.pallas_call(functools.partial(lead_kernel, heads, head_dim, lead_rows,...]
    ppermute x5, waiting for transfers between devices: 6.96 us -> 2.24 us  [neighbour(): return lax.ppermute(array, ('var', 'lat', 'lon'), pairs)]
    pallas_call x1, Pallas kernels: 6.03 us -> 3.82 us  [on_device(): pl.pallas_call(functools.partial(attend_kernel, heads, len(window)), in_s...]
    ppermute x11, starting transfers between devices: 13.7 us -> 14.9 us  [exchange(): lax.ppermute(array, ('var', 'lon'), [(i, moved(i)) for i in range(devices)])]
  transfers between devices with their start and end apart: 16 -> 16, of which waited for: 5 -> 5; matrix products, arithmetic and copies ran while one was open for 0% -> 0% of each run, Pallas kernels for 25% -> 20%
where the time goes in v3:
time: 58.1 us; the launch traced here: 57.8 us
  Pallas kernels  29.7 us (51%)
  starting transfers between devices  20.3 us (35%)
  waiting for transfers between devices  6.87 us (12%)
  local copies, waits for them, and re-layouts  0.72 us (1%)
    ppermute x11, starting transfers between devices, exchange(): lax.ppermute(array, ('var', 'lon'), [(i, moved(i)) for i in range(devices)])  14.9 us
    pallas_call x1, Pallas kernels, lead_pool(): pl.pallas_call(functools.partial(lead_kernel, heads, head_dim, lead_rows,...  10.8 us
    ppermute x5, starting transfers between devices, neighbour(): return lax.ppermute(array, ('var', 'lat', 'lon'), pairs)  5.34 us
    pallas_call x2, Pallas kernels, pool(): pl.pallas_call(functools.partial(pool_kernel, heads, head_dim, row, tiles...  4.9 us
    pallas_call x1, Pallas kernels, on_device(): pl.pallas_call(functools.partial(stage_kernel, rows, columns, len(weights...  4.68 us
    ppermute x11, waiting for transfers between devices, exchange(): lax.ppermute(array, ('var', 'lon'), [(i, moved(i)) for i in range(devices)])  4.63 us
    pallas_call x1, Pallas kernels, on_device(): pl.pallas_call(functools.partial(attend_kernel, heads, len(window)), in_s...  3.82 us
    pallas_call x6, Pallas kernels, merge(): pl.pallas_call(functools.partial(merge_kernel, heads, width, [len(group)...  2.79 us
  transfers between devices with their start and end apart: 16, of which 5 were waited for; matrix products, arithmetic and copies ran while one was open for 0% of the time, Pallas kernels for 20%

profile of v3, /device:TPU:0, one launch (start us, length us, event | category | flops | bytes accessed | tf_op | source)
XLA Modules:
  0.0 57.8 jit_solution(1844870525519573377)
XLA Ops:
  0.0 0.0 copy-start.1
  0.0 0.7 %copy-done.1 = f32[16,64]{1,0:T(8,128)S(1)} copy-done((f32[16,64]{1,0:T(8,128)S(1)}, f32[16,64]{1,0:T(8,128)}, u32[]{:S(2)}) %copy-start.1) | copy-done | bytes 4120
  0.7 2.7 %pre.1 = (bf16[1024,128]{1,0:T(8,128)(2,1)S(1)}, bf16[1024,1024]{1,0:T(8,128)(2,1)S(1)}, bf16[8,96,1024]{2,1,0:T(8,128)(2,1)S(1)}) custom-call(bf16[8,6,96,1024]{3,2,1,0:T(8,128)(2,1)} %refs_1_.2, bf16[1024,1024]{1,0:T(8,128)(2,1)} %value_ref.1, f32[16,64]{1,0:T(8,128)S(1)} %copy-done.1, bf16[1024,1024]{1,0:T(8,128)(2,1)} %key_ref.1), custom_call_target="tpu_custom_call" | custom-call | tf_op jit(solution)/shard_map/pre/pallas_call | solution.py:431
  3.4 10.8 %lead.1 = (bf16[4,48,1152]{2,1,0:T(8,128)(2,1)S(1)}, bf16[4,48,1152]{2,1,0:T(8,128)(2,1)S(1)}, bf16[8,2,96,1024]{3,2,1,0:T(8,128)(2,1)S(1)}) custom-call(s32[1]{0:T(128)} %bitcast.refs_0_, bf16[8,6,96,1024]{3,2,1,0:T(8,128)(2,1)} %refs_1_.2, bf16[8,96,1024]{2,1,0:T(8,128)(2,1)S(1)} %get-tuple-element.47.refs_2_, ...), custom_call_target="tpu_custom_call" | custom-call | flops 9663676416 | bytes 6291456 | tf_op jit(solution)/shard_map/lead/pallas_call | solution.py:446
  14.3 0.5 collective-permute-start
  14.8 2.5 %pool.2 = (bf16[1,48,1152]{2,1,0:T(8,128)(2,1)S(1)}, bf16[1,48,1152]{2,1,0:T(8,128)(2,1)S(1)}) custom-call(s32[1]{0:T(128)} %bitcast.refs_0_, bf16[8,2,96,1024]{3,2,1,0:T(8,128)(2,1)S(1)} %get-tuple-element.60.refs_1_, bf16[1024,1024]{1,0:T(8,128)(2,1)S(1)} %get-tuple-element.48.refs_3_.refs_2_, bf16[1024,128]{1,0:T(8,128)(2,1)S(1)} %get-tuple-element.63.refs_4_.refs_3_), custom_call_target="tpu_custom_call" | custom-call | flops 2415919104 | bytes 1572864 | tf_op jit(solution)/shard_map/pool/pallas_call | solution.py:463
  17.2 0.1 collective-permute-start.2
  17.4 0.0 collective-permute-done.refs_1_
  17.4 0.7 %merge.6 = (bf16[4,24,1152]{2,1,0:T(8,128)(2,1)S(1)}, bf16[4,24,1152]{2,1,0:T(8,128)(2,1)S(1)}) custom-call(bf16[4,48,1152]{2,1,0:T(8,128)(2,1)S(1)} %get-tuple-element.50.refs_0_, bf16[4,48,1152]{2,1,0:T(8,128)(2,1)S(1)} %collective-permute-done.refs_1_), custom_call_target="tpu_custom_call" | custom-call | flops 100663296 | bytes 1572864 | tf_op jit(solution)/shard_map/merge/pallas_call | solution.py:282
  18.0 0.0 copy-start
  18.0 0.0 copy-start.2
  18.1 0.0 copy-start.3
  18.1 3.0 %collective-permute-start.1 = (bf16[4,24,1152]{2,1,0:T(8,128)(2,1)S(1)}, bf16[4,24,1152]{2,1,0:T(8,128)(2,1)S(1)}, u32[]{:S(2)}, u32[]{:S(2)}) collective-permute-start(bf16[4,24,1152]{2,1,0:T(8,128)(2,1)S(1)} %get-tuple-element.55), channel_id=1, source_target_pairs={{0,2},{1,3},{2,0},{3,1},{8,10},{9,11},{10,8},{11,9},{16,18},{17,19... | collective-permute-start | bytes 663560 | tf_op jit(solution)/shard_map/ppermute | solution.py:478
  21.1 2.5 %pool.3 = (bf16[1,48,1152]{2,1,0:T(8,128)(2,1)S(1)}, bf16[1,48,1152]{2,1,0:T(8,128)(2,1)S(1)}) custom-call(s32[1]{0:T(128)} %bitcast.refs_0_, bf16[8,2,96,1024]{3,2,1,0:T(8,128)(2,1)S(1)} %get-tuple-element.60.refs_1_, bf16[1024,1024]{1,0:T(8,128)(2,1)S(1)} %get-tuple-element.48.refs_3_.refs_2_, bf16[1024,128]{1,0:T(8,128)(2,1)S(1)} %get-tuple-element.63.refs_4_.refs_3_), custom_call_target="tpu_custom_call" | custom-call | flops 2415919104 | bytes 1572864 | tf_op jit(solution)/shard_map/pool/pallas_call | solution.py:463
  23.5 0.1 collective-permute-start.3
  23.6 0.0 collective-permute-done.2.refs_1_
  23.6 1.3 %collective-permute-done.3.refs_3_ = bf16[1,48,1152]{2,1,0:T(8,128)(2,1)S(1)} collective-permute-done((bf16[1,48,1152]{2,1,0:T(8,128)(2,1)S(1)}, bf16[1,48,1152]{2,1,0:T(8,128)(2,1)S(1)}, u32[]{:S(2)}, u32[]{:S(2)}) %collective-permute-start.3) | collective-permute-done | bytes 110624 | tf_op jit(solution)/shard_map/ppermute | solution.py:478
  24.9 0.5 merge.8
  25.4 1.3 %collective-permute-done.1.refs_1_ = bf16[4,24,1152]{2,1,0:T(8,128)(2,1)S(1)} collective-permute-done((bf16[4,24,1152]{2,1,0:T(8,128)(2,1)S(1)}, bf16[4,24,1152]{2,1,0:T(8,128)(2,1)S(1)}, u32[]{:S(2)}, u32[]{:S(2)}) %collective-permute-start.1) | collective-permute-done | bytes 221216 | tf_op jit(solution)/shard_map/ppermute | solution.py:478
  26.7 0.4 merge.7
  27.1 1.8 %collective-permute-start.7 = (bf16[2,24,1152]{2,1,0:T(8,128)(2,1)S(1)}, bf16[2,24,1152]{2,1,0:T(8,128)(2,1)S(1)}, u32[]{:S(2)}, u32[]{:S(2)}) collective-permute-start(bf16[2,24,1152]{2,1,0:T(8,128)(2,1)S(1)} %get-tuple-element.73), channel_id=1, source_target_pairs={{0,2},{1,3},{2,0},{3,1},{8,10},{9,11},{10,8},{11,9},{16,18},{17,19... | collective-permute-start | bytes 331784 | tf_op jit(solution)/shard_map/ppermute | solution.py:478
  28.9 1.6 %collective-permute-start.4 = (bf16[24,1152]{1,0:T(8,128)(2,1)S(1)}, bf16[24,1152]{1,0:T(8,128)(2,1)S(1)}, u32[]{:S(2)}, u32[]{:S(2)}) collective-permute-start(bf16[24,1152]{1,0:T(8,128)(2,1)S(1)} %get-tuple-element.69), channel_id=1, source_target_pairs={{0,8},{1,9},{2,10},{3,11},{8,16},{9,17},{10,18},{11,19},{16,24},{1... | collective-permute-start | bytes 165896 | tf_op jit(solution)/shard_map/ppermute | solution.py:478
  30.5 2.6 %collective-permute-start.5 = (bf16[24,1152]{1,0:T(8,128)(2,1)S(1)}, bf16[24,1152]{1,0:T(8,128)(2,1)S(1)}, u32[]{:S(2)}, u32[]{:S(2)}) collective-permute-start(bf16[24,1152]{1,0:T(8,128)(2,1)S(1)} %get-tuple-element.70), channel_id=1, source_target_pairs={{0,16},{1,17},{2,18},{3,19},{8,24},{9,25},{10,26},{11,27},{16,0},{... | collective-permute-start | bytes 165896 | tf_op jit(solution)/shard_map/ppermute | solution.py:478
  33.1 1.3 %collective-permute-start.6 = (bf16[24,1152]{1,0:T(8,128)(2,1)S(1)}, bf16[24,1152]{1,0:T(8,128)(2,1)S(1)}, u32[]{:S(2)}, u32[]{:S(2)}) collective-permute-start(bf16[24,1152]{1,0:T(8,128)(2,1)S(1)} %get-tuple-element.71), channel_id=1, source_target_pairs={{0,24},{1,25},{2,26},{3,27},{8,0},{9,1},{10,2},{11,3},{16,8},{17,9... | collective-permute-start | bytes 165896 | tf_op jit(solution)/shard_map/ppermute | solution.py:478
  34.5 0.0 collective-permute-done.7.refs_1_
  34.5 0.4 merge.9
  34.8 0.7 %collective-permute-start.8 = (bf16[12,1152]{1,0:T(8,128)(2,1)S(1)}, bf16[12,1152]{1,0:T(8,128)(2,1)S(1)}, u32[]{:S(2)}, u32[]{:S(2)}) collective-permute-start(bf16[12,1152]{1,0:T(8,128)(2,1)S(1)} %get-tuple-element.75), channel_id=1, source_target_pairs={{0,8},{1,9},{2,10},{3,11},{8,16},{9,17},{10,18},{11,19},{16,24},{1... | collective-permute-start | bytes 82952 | tf_op jit(solution)/shard_map/ppermute | solution.py:478
  35.6 1.2 %collective-permute-start.9 = (bf16[12,1152]{1,0:T(8,128)(2,1)S(1)}, bf16[12,1152]{1,0:T(8,128)(2,1)S(1)}, u32[]{:S(2)}, u32[]{:S(2)}) collective-permute-start(bf16[12,1152]{1,0:T(8,128)(2,1)S(1)} %get-tuple-element.76), channel_id=1, source_target_pairs={{0,16},{1,17},{2,18},{3,19},{8,24},{9,25},{10,26},{11,27},{16,0},{... | collective-permute-start | bytes 82952 | tf_op jit(solution)/shard_map/ppermute | solution.py:478
  36.8 0.0 collective-permute-done.4.refs_1_
  36.8 1.9 %collective-permute-start.10 = (bf16[12,1152]{1,0:T(8,128)(2,1)S(1)}, bf16[12,1152]{1,0:T(8,128)(2,1)S(1)}, u32[]{:S(2)}, u32[]{:S(2)}) collective-permute-start(bf16[12,1152]{1,0:T(8,128)(2,1)S(1)} %get-tuple-element.77), channel_id=1, source_target_pairs={{0,24},{1,25},{2,26},{3,27},{8,0},{9,1},{10,2},{11,3},{16,8},{17,9... | collective-permute-start | bytes 82952 | tf_op jit(solution)/shard_map/ppermute | solution.py:478
  38.7 0.1 pad_add_fusion.refs_0_
  38.8 0.0 collective-permute-done.5.refs_2_
  38.8 0.0 collective-permute-done.6.refs_3_
  38.8 0.4 merge.10
  39.2 1.5 %collective-permute-done.8.refs_1_ = bf16[12,1152]{1,0:T(8,128)(2,1)S(1)} collective-permute-done((bf16[12,1152]{1,0:T(8,128)(2,1)S(1)}, bf16[12,1152]{1,0:T(8,128)(2,1)S(1)}, u32[]{:S(2)}, u32[]{:S(2)}) %collective-permute-start.8) | collective-permute-done | bytes 27680 | tf_op jit(solution)/shard_map/ppermute | solution.py:478
  40.7 0.5 collective-permute-done.9.refs_2_
  41.3 0.0 collective-permute-done.10.refs_3_
  41.3 0.4 merge.11
  41.7 1.1 %collective-permute-start.15 = (bf16[36,1024]{1,0:T(8,128)(2,1)S(1)}, bf16[36,1024]{1,0:T(8,128)(2,1)S(1)}, u32[]{:S(2)}, u32[]{:S(2)}) collective-permute-start(bf16[36,1024]{1,0:T(8,128)(2,1)S(1)} %pad_maximum_fusion.refs_0_), channel_id=1, source_target_pairs={{5,0},{6,1},{7,2},{12,3},{1,4},{2,5},{3,6},{8,7},{13,8},{14,9},{15... | collective-permute-start | bytes 221192 | tf_op jit(solution)/shard_map/ppermute | solution.py:547
  42.8 3.8 %collective-permute-start.14 = (bf16[36,1024]{1,0:T(8,128)(2,1)S(1)}, bf16[36,1024]{1,0:T(8,128)(2,1)S(1)}, u32[]{:S(2)}, u32[]{:S(2)}) collective-permute-start(bf16[36,1024]{1,0:T(8,128)(2,1)S(1)} %pad_maximum_fusion.refs_0_), channel_id=1, source_target_pairs={{1,0},{2,1},{3,2},{8,3},{5,4},{6,5},{7,6},{12,7},{9,8},{10,9},{11,... | collective-permute-start | bytes 221192 | tf_op jit(solution)/shard_map/ppermute | solution.py:547
  46.5 0.0 collective-permute-start.13
  46.6 0.0 collective-permute-start.12
  46.6 0.5 collective-permute-start.11
  47.1 0.0 copy-done
  47.1 0.0 copy-done.2
  47.1 0.0 copy-done.3
  47.1 0.0 copy-start.4
  47.1 4.7 %stage.1 = (f32[16,48,216]{2,1,0:T(8,128)S(1)}, bf16[1024,1024]{1,0:T(8,128)(2,1)S(1)}, bf16[1024,1024]{1,0:T(8,128)(2,1)S(1)}, bf16[1024,1024]{1,0:T(8,128)(2,1...) custom-call(s32[2]{0:T(128)S(1)} %pad_add_fusion.refs_0_, s32[3,216]{1,0:T(4,128)S(1)} %copy-done.3, ...), custom_call_target="tpu_custom_call" | custom-call | flops 1000 | bytes 10485760 | tf_op jit(solution)/shard_map/stage/pallas_call | solution.py:551
  51.8 0.0 collective-permute-done.15.refs_5_
  51.8 0.0 collective-permute-done.14.refs_4_
  51.8 2.2 %collective-permute-done.13.refs_3_ = bf16[36,1024]{1,0:T(8,128)(2,1)S(1)} collective-permute-done((bf16[36,1024]{1,0:T(8,128)(2,1)S(1)}, bf16[36,1024]{1,0:T(8,128)(2,1)S(1)}, u32[]{:S(2)}, u32[]{:S(2)}) %collective-permute-start.13) | collective-permute-done | bytes 73760 | tf_op jit(solution)/shard_map/ppermute | solution.py:547
  54.0 0.0 collective-permute-done.12.refs_2_
  54.0 0.0 collective-permute-done.11.refs_1_
  54.0 0.0 copy-done.4
  54.0 3.8 %attend.1 = bf16[6,6,1024]{2,1,0:T(8,128)(2,1)} custom-call(bf16[36,1024]{1,0:T(8,128)(2,1)S(1)} %pad_maximum_fusion.refs_0_, bf16[36,1024]{1,0:T(8,128)(2,1)S(1)} %collective-permute-done.11.refs_1_, bf16[36,1024]{1,0:T(8,128)(2,1)S(1)} %collective-permute-done.12.refs_2_, bf16[36,1024]{1,0:T(8,128)(2,1)S(1)} %collective-permute-done.13.refs_3_, ...), custom_call_target="tpu_custom_call" | custom-call | tf_op jit(solution)/shard_map/attend/pallas_call | solution.py:565
  (1 shorter events, 0.0 us)
Async XLA Ops:
  0.0 0.7 %copy-start.1 = (f32[16,64]{1,0:T(8,128)S(1)}, f32[16,64]{1,0:T(8,128)}, u32[]{:S(2)}) copy-start(f32[16,64]{1,0:T(8,128)} %query_ref.1) | copy-start | bytes 12292
  14.3 3.1 %collective-permute-start = (bf16[4,48,1152]{2,1,0:T(8,128)(2,1)S(1)}, bf16[4,48,1152]{2,1,0:T(8,128)(2,1)S(1)}, u32[]{:S(2)}, u32[]{:S(2)}) collective-permute-start(bf16[4,48,1152]{2,1,0:T(8,128)(2,1)S(1)} %get-tuple-element.51), channel_id=1, source_target_pairs={{0,1},{1,0},{2,3},{3,2},{8,9},{9,8},{10,11},{11,10},{16,17},{17,16... | collective-permute-start | bytes 1327112 | tf_op jit(solution)/shard_map/ppermute | solution.py:478
  17.2 6.4 %collective-permute-start.2 = (bf16[1,48,1152]{2,1,0:T(8,128)(2,1)S(1)}, bf16[1,48,1152]{2,1,0:T(8,128)(2,1)S(1)}, u32[]{:S(2)}, u32[]{:S(2)}) collective-permute-start(bf16[1,48,1152]{2,1,0:T(8,128)(2,1)S(1)} %get-tuple-element.62), channel_id=1, source_target_pairs={{0,1},{1,0},{2,3},{3,2},{8,9},{9,8},{10,11},{11,10},{16,17},{17,16... | collective-permute-start | bytes 331784 | tf_op jit(solution)/shard_map/ppermute | solution.py:478
  18.0 29.0 %copy-start = (f32[16,13,13]{2,0,1:T(8,128)S(1)}, f32[16,13,13]{2,0,1:T(8,128)}, u32[]{:S(2)}) copy-start(f32[16,13,13]{2,0,1:T(8,128)} %param.23) | copy-start | bytes 32452
  18.0 29.0 %copy-start.2 = (s32[12,96]{1,0:T(8,128)S(1)}, s32[12,96]{1,0:T(8,128)}, u32[]{:S(2)}) copy-start(s32[12,96]{1,0:T(8,128)} %refs_2_.1) | copy-start | bytes 13828
  18.1 29.0 %copy-start.3 = (s32[3,216]{1,0:T(4,128)S(1)}, s32[3,216]{1,0:T(4,128)}, u32[]{:S(2)}) copy-start(s32[3,216]{1,0:T(4,128)} %constant.16.clone.refs_1_) | copy-start | bytes 7780
  18.1 8.6 %collective-permute-start.1 = (bf16[4,24,1152]{2,1,0:T(8,128)(2,1)S(1)}, bf16[4,24,1152]{2,1,0:T(8,128)(2,1)S(1)}, u32[]{:S(2)}, u32[]{:S(2)}) collective-permute-start(bf16[4,24,1152]{2,1,0:T(8,128)(2,1)S(1)} %get-tuple-element.55), channel_id=1, source_target_pairs={{0,2},{1,3},{2,0},{3,1},{8,10},{9,11},{10,8},{11,9},{16,18},{17,19... | collective-permute-start | bytes 663560 | tf_op jit(solution)/shard_map/ppermute | solution.py:478
  23.5 1.4 %collective-permute-start.3 = (bf16[1,48,1152]{2,1,0:T(8,128)(2,1)S(1)}, bf16[1,48,1152]{2,1,0:T(8,128)(2,1)S(1)}, u32[]{:S(2)}, u32[]{:S(2)}) collective-permute-start(bf16[1,48,1152]{2,1,0:T(8,128)(2,1)S(1)} %get-tuple-element.65), channel_id=1, source_target_pairs={{0,1},{1,0},{2,3},{3,2},{8,9},{9,8},{10,11},{11,10},{16,17},{17,16... | collective-permute-start | bytes 331784 | tf_op jit(solution)/shard_map/ppermute | solution.py:478
  27.1 7.3 %collective-permute-start.7 = (bf16[2,24,1152]{2,1,0:T(8,128)(2,1)S(1)}, bf16[2,24,1152]{2,1,0:T(8,128)(2,1)S(1)}, u32[]{:S(2)}, u32[]{:S(2)}) collective-permute-start(bf16[2,24,1152]{2,1,0:T(8,128)(2,1)S(1)} %get-tuple-element.73), channel_id=1, source_target_pairs={{0,2},{1,3},{2,0},{3,1},{8,10},{9,11},{10,8},{11,9},{16,18},{17,19... | collective-permute-start | bytes 331784 | tf_op jit(solution)/shard_map/ppermute | solution.py:478
  28.9 7.9 %collective-permute-start.4 = (bf16[24,1152]{1,0:T(8,128)(2,1)S(1)}, bf16[24,1152]{1,0:T(8,128)(2,1)S(1)}, u32[]{:S(2)}, u32[]{:S(2)}) collective-permute-start(bf16[24,1152]{1,0:T(8,128)(2,1)S(1)} %get-tuple-element.69), channel_id=1, source_target_pairs={{0,8},{1,9},{2,10},{3,11},{8,16},{9,17},{10,18},{11,19},{16,24},{1... | collective-permute-start | bytes 165896 | tf_op jit(solution)/shard_map/ppermute | solution.py:478
  30.5 8.3 %collective-permute-start.5 = (bf16[24,1152]{1,0:T(8,128)(2,1)S(1)}, bf16[24,1152]{1,0:T(8,128)(2,1)S(1)}, u32[]{:S(2)}, u32[]{:S(2)}) collective-permute-start(bf16[24,1152]{1,0:T(8,128)(2,1)S(1)} %get-tuple-element.70), channel_id=1, source_target_pairs={{0,16},{1,17},{2,18},{3,19},{8,24},{9,25},{10,26},{11,27},{16,0},{... | collective-permute-start | bytes 165896 | tf_op jit(solution)/shard_map/ppermute | solution.py:478
  33.1 5.7 %collective-permute-start.6 = (bf16[24,1152]{1,0:T(8,128)(2,1)S(1)}, bf16[24,1152]{1,0:T(8,128)(2,1)S(1)}, u32[]{:S(2)}, u32[]{:S(2)}) collective-permute-start(bf16[24,1152]{1,0:T(8,128)(2,1)S(1)} %get-tuple-element.71), channel_id=1, source_target_pairs={{0,24},{1,25},{2,26},{3,27},{8,0},{9,1},{10,2},{11,3},{16,8},{17,9... | collective-permute-start | bytes 165896 | tf_op jit(solution)/shard_map/ppermute | solution.py:478
  34.8 5.9 %collective-permute-start.8 = (bf16[12,1152]{1,0:T(8,128)(2,1)S(1)}, bf16[12,1152]{1,0:T(8,128)(2,1)S(1)}, u32[]{:S(2)}, u32[]{:S(2)}) collective-permute-start(bf16[12,1152]{1,0:T(8,128)(2,1)S(1)} %get-tuple-element.75), channel_id=1, source_target_pairs={{0,8},{1,9},{2,10},{3,11},{8,16},{9,17},{10,18},{11,19},{16,24},{1... | collective-permute-start | bytes 82952 | tf_op jit(solution)/shard_map/ppermute | solution.py:478
  35.6 5.7 %collective-permute-start.9 = (bf16[12,1152]{1,0:T(8,128)(2,1)S(1)}, bf16[12,1152]{1,0:T(8,128)(2,1)S(1)}, u32[]{:S(2)}, u32[]{:S(2)}) collective-permute-start(bf16[12,1152]{1,0:T(8,128)(2,1)S(1)} %get-tuple-element.76), channel_id=1, source_target_pairs={{0,16},{1,17},{2,18},{3,19},{8,24},{9,25},{10,26},{11,27},{16,0},{... | collective-permute-start | bytes 82952 | tf_op jit(solution)/shard_map/ppermute | solution.py:478
  36.8 4.5 %collective-permute-start.10 = (bf16[12,1152]{1,0:T(8,128)(2,1)S(1)}, bf16[12,1152]{1,0:T(8,128)(2,1)S(1)}, u32[]{:S(2)}, u32[]{:S(2)}) collective-permute-start(bf16[12,1152]{1,0:T(8,128)(2,1)S(1)} %get-tuple-element.77), channel_id=1, source_target_pairs={{0,24},{1,25},{2,26},{3,27},{8,0},{9,1},{10,2},{11,3},{16,8},{17,9... | collective-permute-start | bytes 82952 | tf_op jit(solution)/shard_map/ppermute | solution.py:478
  41.7 10.1 %collective-permute-start.15 = (bf16[36,1024]{1,0:T(8,128)(2,1)S(1)}, bf16[36,1024]{1,0:T(8,128)(2,1)S(1)}, u32[]{:S(2)}, u32[]{:S(2)}) collective-permute-start(bf16[36,1024]{1,0:T(8,128)(2,1)S(1)} %pad_maximum_fusion.refs_0_), channel_id=1, source_target_pairs={{5,0},{6,1},{7,2},{12,3},{1,4},{2,5},{3,6},{8,7},{13,8},{14,9},{15... | collective-permute-start | bytes 221192 | tf_op jit(solution)/shard_map/ppermute | solution.py:547
  42.8 9.0 %collective-permute-start.14 = (bf16[36,1024]{1,0:T(8,128)(2,1)S(1)}, bf16[36,1024]{1,0:T(8,128)(2,1)S(1)}, u32[]{:S(2)}, u32[]{:S(2)}) collective-permute-start(bf16[36,1024]{1,0:T(8,128)(2,1)S(1)} %pad_maximum_fusion.refs_0_), channel_id=1, source_target_pairs={{1,0},{2,1},{3,2},{8,3},{5,4},{6,5},{7,6},{12,7},{9,8},{10,9},{11,... | collective-permute-start | bytes 221192 | tf_op jit(solution)/shard_map/ppermute | solution.py:547
  46.5 7.5 %collective-permute-start.13 = (bf16[36,1024]{1,0:T(8,128)(2,1)S(1)}, bf16[36,1024]{1,0:T(8,128)(2,1)S(1)}, u32[]{:S(2)}, u32[]{:S(2)}) collective-permute-start(bf16[36,1024]{1,0:T(8,128)(2,1)S(1)} %pad_maximum_fusion.refs_0_), channel_id=1, source_target_pairs={{31,0},{4,1},{5,2},{6,3},{27,4},{0,5},{1,6},{2,7},{7,8},{12,9},{13... | collective-permute-start | bytes 221192 | tf_op jit(solution)/shard_map/ppermute | solution.py:547
  46.6 7.5 %collective-permute-start.12 = (bf16[36,1024]{1,0:T(8,128)(2,1)S(1)}, bf16[36,1024]{1,0:T(8,128)(2,1)S(1)}, u32[]{:S(2)}, u32[]{:S(2)}) collective-permute-start(bf16[36,1024]{1,0:T(8,128)(2,1)S(1)} %pad_maximum_fusion.refs_0_), channel_id=1, source_target_pairs={{27,0},{0,1},{1,2},{2,3},{31,4},{4,5},{5,6},{6,7},{3,8},{8,9},{9,1... | collective-permute-start | bytes 221192 | tf_op jit(solution)/shard_map/ppermute | solution.py:547
  46.6 7.5 %collective-permute-start.11 = (bf16[36,1024]{1,0:T(8,128)(2,1)S(1)}, bf16[36,1024]{1,0:T(8,128)(2,1)S(1)}, u32[]{:S(2)}, u32[]{:S(2)}) collective-permute-start(bf16[36,1024]{1,0:T(8,128)(2,1)S(1)} %pad_maximum_fusion.refs_0_), channel_id=1, source_target_pairs={{4,0},{5,1},{6,2},{7,3},{0,4},{1,5},{2,6},{3,7},{12,8},{13,9},{14,... | collective-permute-start | bytes 221192 | tf_op jit(solution)/shard_map/ppermute | solution.py:547
  47.1 6.9 %copy-start.4 = (f32[1024]{0:T(1024)S(1)}, f32[1024]{0:T(1024)}, u32[]{:S(2)}) copy-start(f32[1024]{0:T(1024)} %param.18) | copy-start | bytes 12292

commit v4 on v3

--- a/solution.py
+++ b/solution.py
@@ -20,7 +20,8 @@
 LEAD_VMEM = 40 * MIB
 POOL_VMEM = 30 * MIB
 MERGE_VMEM = 12 * MIB
-STAGE_VMEM = 42 * MIB
+STAGE_VMEM = 47 * MIB
+LOAD_VMEM = 42 * MIB
 F32 = jnp.float32
 BF16 = jnp.bfloat16
 
@@ -188,9 +189,8 @@
             (step // tiles) * tiles + (step % tiles + tiles - high) % tiles,
         )
 
+    fetch(2).start()
     work(0, first_ref[...])
-    fetch(2).start()
-    rest.start()
 
     def body(step, _):
         fetch(step).wait()
@@ -199,6 +199,10 @@
         @pl.when(step + 2 < steps)
         def _():
             fetch(step + 2).start()
+
+        @pl.when(step == 1)
+        def _():
+            rest.start()
 
         return 0
 
@@ -259,8 +263,10 @@
         flat = [part.reshape(-1, part.shape[-1]) for part in parts]
         merged.append(merge_body(flat, heads, width, last))
     if last:
-        for out, rows in zip(outs, merged):
-            out[...] = rows
+        at = 0
+        for rows in merged:
+            outs[0][at : at + rows.shape[0]] = rows
+            at += rows.shape[0]
         return
     size = math.prod(outs[0].shape[:-1]) // groups
     place = 0
@@ -309,7 +315,7 @@
     lat, block = where_ref[0], where_ref[1]
     side = rows - 2 * rows * lat
     row_at = meta_ref[0:1] + meta_ref[1:2] * side
-    column_at = meta_ref[2:3]
+    column_at = meta_ref[2:3] + meta_ref[3:4] * (1 - 2 * (block & 1))
 
     far = column_at + block * columns
     far = jnp.where(far < 0, far + n_columns, far)
@@ -335,6 +341,17 @@
             found = found[:heads] + found[heads : 2 * heads] + found[2 * heads :]
             kept = (inside & allowed) | (index == HALF * pitch + HALF)
             out_ref[:, row * columns + column, :] = jnp.where(kept, found, -jnp.inf)
+    for copy in copies:
+        copy.wait()
+
+
+def load_kernel(count, *refs):
+    sems = refs[2 * count]
+    copies = [
+        pltpu.make_async_copy(refs[at], refs[count + at], sems.at[at]) for at in range(count)
+    ]
+    for copy in copies:
+        copy.start()
     for copy in copies:
         copy.wait()
 
@@ -514,53 +531,76 @@
     keep_a = parts_a[0]
     keep_b = [[keep_b] + got_b, [keep_c] + got_c]
 
-    places = [(dl, dx) for dx in (0, -1, 1) for dl in (0, 1)]
+    places = [(0, 0), (1, 0), (0, 1), (1, 1), (0, -1), (1, -1)]
     patch = rows * columns
     dl = np.repeat([p[0] for p in places], patch)
     dx = np.repeat([p[1] for p in places], patch)
     row = np.tile(np.repeat(np.arange(rows), columns), len(places))
     column = np.tile(np.arange(columns), len(places) * rows)
-    meta = jnp.asarray(np.stack([row, dl, dx * columns + column]), jnp.int32)
+    meta = jnp.asarray(np.stack([row, dl, column, dx * columns]), jnp.int32)
     keys = len(places) * patch
     for number in range(1, len(stages)):
         split_b, split_a = split_before(stages, number - 1), split_before(stages, number)
         parts_b = next_split(keep_b, number - 1, 2 * tiles, half // split_b)
         if number > 1:
             got_a, _ = barrier((got_a, parts_b))
-        parts_a = next_split([[keep_a] + got_a], number, lead_rows * tiles, half // split_a)
-        if number == 1:
-            parts_a, parts_b = barrier((parts_a, parts_b))
+        group_a = [keep_a] + got_a
         if number + 1 < len(stages):
+            parts_a = next_split([group_a], number, lead_rows * tiles, half // split_a)
+            if number == 1:
+                parts_a, parts_b = barrier((parts_a, parts_b))
             keep_a, got_a = parts_a[0], swap(parts_a[1:], number + 1)
         keep_b = [[parts_b[0]] + swap(parts_b[1:], number)]
-    pooled_a = parts_a[0]
-    (pooled_b,) = next_split(keep_b, len(stages) - 1, 2 * tiles, columns)
-    pooled = jnp.concatenate([pooled_a, pooled_b], axis=0)
-
-    def neighbour(array, dl, dx):
-        pairs = []
-        for i in range(n_var * n_lat * n_lon):
-            v, l, o = i // (n_lat * n_lon), (i // n_lon) % n_lat, i % n_lon
-            b = (v * n_lon + o + dx) % devices
-            source = ((b // n_lon) * n_lat + (l + dl) % n_lat) * n_lon + b % n_lon
-            pairs.append((source, i))
-        return lax.ppermute(array, ("var", "lat", "lon"), pairs)
-
-    weights = (agg_out, nb_query, nb_key, nb_value, nb_out)
+    (pooled,) = next_split([group_a] + keep_b, len(stages) - 1, 0, columns)
+
+    staged = (agg_out, nb_query, nb_key)
     pooled, where = barrier((pooled, where))
-    bias, *weights = pl.pallas_call(
-        functools.partial(stage_kernel, rows, columns, len(weights)),
-        in_specs=[smem, vmem, vmem, vmem] + [hbm] * len(weights),
-        out_specs=[vmem] * (1 + len(weights)),
-        out_shape=[jax.ShapeDtypeStruct((heads, QROWS, keys), F32)] + [weight] * len(weights),
-        scratch_shapes=[pltpu.SemaphoreType.DMA((len(weights),))],
+    bias, *staged = pl.pallas_call(
+        functools.partial(stage_kernel, rows, columns, len(staged)),
+        in_specs=[smem, vmem, vmem, vmem] + [hbm] * len(staged),
+        out_specs=[vmem] * (1 + len(staged)),
+        out_shape=[jax.ShapeDtypeStruct((heads, QROWS, keys), F32)] + [weight] * len(staged),
+        scratch_shapes=[pltpu.SemaphoreType.DMA((len(staged),))],
         compiler_params=pltpu.CompilerParams(vmem_limit_bytes=STAGE_VMEM),
         cost_estimate=pl.CostEstimate(
             flops=1000, bytes_accessed=10 * width * width, transcendentals=0
         ),
         name="stage",
-    )(where, meta, valid, jnp.transpose(pos_bias, (1, 0, 2)), *weights)
-    window = [pooled] + [neighbour(pooled, dl, dx) for dl, dx in places[1:]]
+    )(where, meta, valid, jnp.transpose(pos_bias, (1, 0, 2)), *staged)
+
+    def partner(array, kind):
+        pairs = []
+        for i in range(n_var * n_lat * n_lon):
+            v, l, o = i // (n_lat * n_lon), (i // n_lon) % n_lat, i % n_lon
+            b = v * n_lon + o
+            if kind == "lat":
+                l = n_lat - 1 - l
+            elif kind == "core":
+                b ^= 1
+            else:
+                b = (b + 1 if b % 2 else b - 1) % devices
+            pairs.append((((b // n_lon) * n_lat + l) * n_lon + b % n_lon, i))
+        return lax.ppermute(array, ("var", "lat", "lon"), pairs)
+
+    across = partner(pooled, "lat")
+    near = partner(pooled, "core")
+    far = partner(pooled, "odd")
+    across, far, bias = barrier((across, far, bias))
+    window = [pooled, across, near, partner(across, "core"), far, partner(far, "lat")]
+    last = (nb_value, nb_out)
+    last, _ = barrier((last, across))
+    last = pl.pallas_call(
+        functools.partial(load_kernel, len(last)),
+        in_specs=[hbm] * len(last),
+        out_specs=[vmem] * len(last),
+        out_shape=[weight] * len(last),
+        scratch_shapes=[pltpu.SemaphoreType.DMA((len(last),))],
+        compiler_params=pltpu.CompilerParams(vmem_limit_bytes=LOAD_VMEM),
+        cost_estimate=pl.CostEstimate(
+            flops=1000, bytes_accessed=8 * width * width, transcendentals=0
+        ),
+        name="load",
+    )(*last)
 
     return pl.pallas_call(
         functools.partial(attend_kernel, heads, len(window)),
@@ -573,7 +613,7 @@
         ],
         compiler_params=pltpu.CompilerParams(vmem_limit_bytes=MERGE_VMEM),
         name="attend",
-    )(*window, norm_gain.reshape(1, width), bias, *weights)
+    )(*window, norm_gain.reshape(1, width), bias, *staged, *last)
 
 
 def solution(mesh):

time: 58.1 us -> 56.9 us (0.979)
  starting transfers between devices: 20.3 us -> 18.8 us
  waiting for transfers between devices: 6.87 us -> 8.18 us
  Pallas kernels: 29.7 us -> 28.7 us
    ppermute x5, starting transfers between devices: 5.34 us -> 3.9 us  [partner(): return lax.ppermute(array, ('var', 'lat', 'lon'), pairs)]
    ppermute x5, waiting for transfers between devices: 2.24 us -> 3.11 us  [partner(): return lax.ppermute(array, ('var', 'lat', 'lon'), pairs)]
    pallas_call x1 -> x2, Pallas kernels: 4.68 us -> 4.01 us  [the longest x1 3.7 us: on_device(): pl.pallas_call(functools.partial(stage_kernel, rows, columns, len(staged)...]
    pallas_call x6 -> x5, Pallas kernels: 2.79 us -> 2.47 us  [merge(): pl.pallas_call(functools.partial(merge_kernel, heads, width, [len(group)...]
  transfers between devices with their start and end apart: 16 -> 16, of which waited for: 5 -> 6; matrix products, arithmetic and copies ran while one was open for 0% -> 0% of each run, Pallas kernels for 20% -> 18%
where the time goes in v4:
time: 56.9 us; the launch traced here: 56.7 us
  Pallas kernels  28.7 us (50%)
  starting transfers between devices  18.8 us (33%)
  waiting for transfers between devices  8.18 us (14%)
  local copies, waits for them, and re-layouts  0.73 us (1%)
    ppermute x11, starting transfers between devices, exchange(): lax.ppermute(array, ('var', 'lon'), [(i, moved(i)) for i in range(devices)])  14.9 us
    pallas_call x1, Pallas kernels, lead_pool(): pl.pallas_call(functools.partial(lead_kernel, heads, head_dim, lead_rows,...  10.8 us
    ppermute x11, waiting for transfers between devices, exchange(): lax.ppermute(array, ('var', 'lon'), [(i, moved(i)) for i in range(devices)])  5.07 us
    pallas_call x2, Pallas kernels, pool(): pl.pallas_call(functools.partial(pool_kernel, heads, head_dim, row, tiles...  4.9 us
    ppermute x5, starting transfers between devices, partner(): return lax.ppermute(array, ('var', 'lat', 'lon'), pairs)  3.9 us
    pallas_call x1, Pallas kernels, on_device(): pl.pallas_call(functools.partial(attend_kernel, heads, len(window)), in_s...  3.78 us
    pallas_call x1, Pallas kernels, on_device(): pl.pallas_call(functools.partial(stage_kernel, rows, columns, len(staged)...  3.7 us
    ppermute x5, waiting for transfers between devices, partner(): return lax.ppermute(array, ('var', 'lat', 'lon'), pairs)  3.11 us
  transfers between devices with their start and end apart: 16, of which 6 were waited for; matrix products, arithmetic and copies ran while one was open for 0% of the time, Pallas kernels for 18%

profile of v4, /device:TPU:0, one launch (start us, length us, event | category | flops | bytes accessed | tf_op | source)
XLA Modules:
  0.0 56.7 jit_solution(7277273455813378299)
XLA Ops:
  0.0 0.0 copy-start.3
  0.0 0.7 %copy-done.3 = f32[16,64]{1,0:T(8,128)S(1)} copy-done((f32[16,64]{1,0:T(8,128)S(1)}, f32[16,64]{1,0:T(8,128)}, u32[]{:S(2)}) %copy-start.3) | copy-done | bytes 4120
  0.7 2.7 %pre.1 = (bf16[1024,128]{1,0:T(8,128)(2,1)S(1)}, bf16[1024,1024]{1,0:T(8,128)(2,1)S(1)}, bf16[8,96,1024]{2,1,0:T(8,128)(2,1)S(1)}) custom-call(bf16[8,6,96,1024]{3,2,1,0:T(8,128)(2,1)} %refs_1_.2, bf16[1024,1024]{1,0:T(8,128)(2,1)} %value_ref.1, f32[16,64]{1,0:T(8,128)S(1)} %copy-done.3, bf16[1024,1024]{1,0:T(8,128)(2,1)} %key_ref.1), custom_call_target="tpu_custom_call" | custom-call | tf_op jit(solution)/shard_map/pre/pallas_call | solution.py:448
  3.4 10.8 %lead.1 = (bf16[4,48,1152]{2,1,0:T(8,128)(2,1)S(1)}, bf16[4,48,1152]{2,1,0:T(8,128)(2,1)S(1)}, bf16[8,2,96,1024]{3,2,1,0:T(8,128)(2,1)S(1)}) custom-call(s32[1]{0:T(128)} %bitcast.refs_0_, bf16[8,6,96,1024]{3,2,1,0:T(8,128)(2,1)} %refs_1_.2, bf16[8,96,1024]{2,1,0:T(8,128)(2,1)S(1)} %get-tuple-element.52.refs_2_, ...), custom_call_target="tpu_custom_call" | custom-call | flops 9663676416 | bytes 6291456 | tf_op jit(solution)/shard_map/lead/pallas_call | solution.py:463
  14.3 0.5 collective-permute-start
  14.8 2.5 %pool.2 = (bf16[1,48,1152]{2,1,0:T(8,128)(2,1)S(1)}, bf16[1,48,1152]{2,1,0:T(8,128)(2,1)S(1)}) custom-call(s32[1]{0:T(128)} %bitcast.refs_0_, bf16[8,2,96,1024]{3,2,1,0:T(8,128)(2,1)S(1)} %get-tuple-element.65.refs_1_, bf16[1024,1024]{1,0:T(8,128)(2,1)S(1)} %get-tuple-element.53.refs_3_.refs_2_, bf16[1024,128]{1,0:T(8,128)(2,1)S(1)} %get-tuple-element.68.refs_4_.refs_3_), custom_call_target="tpu_custom_call" | custom-call | flops 2415919104 | bytes 1572864 | tf_op jit(solution)/shard_map/pool/pallas_call | solution.py:480
  17.2 0.1 collective-permute-start.2
  17.4 0.0 collective-permute-done.refs_1_
  17.4 0.7 %merge.5 = (bf16[4,24,1152]{2,1,0:T(8,128)(2,1)S(1)}, bf16[4,24,1152]{2,1,0:T(8,128)(2,1)S(1)}) custom-call(bf16[4,48,1152]{2,1,0:T(8,128)(2,1)S(1)} %get-tuple-element.55.refs_0_, bf16[4,48,1152]{2,1,0:T(8,128)(2,1)S(1)} %collective-permute-done.refs_1_), custom_call_target="tpu_custom_call" | custom-call | flops 100663296 | bytes 1572864 | tf_op jit(solution)/shard_map/merge/pallas_call | solution.py:288
  18.0 0.0 copy-start.2
  18.0 0.0 copy-start.4
  18.1 0.0 copy-start.6
  18.1 3.0 %collective-permute-start.1 = (bf16[4,24,1152]{2,1,0:T(8,128)(2,1)S(1)}, bf16[4,24,1152]{2,1,0:T(8,128)(2,1)S(1)}, u32[]{:S(2)}, u32[]{:S(2)}) collective-permute-start(bf16[4,24,1152]{2,1,0:T(8,128)(2,1)S(1)} %get-tuple-element.60), channel_id=1, source_target_pairs={{0,2},{1,3},{2,0},{3,1},{8,10},{9,11},{10,8},{11,9},{16,18},{17,19... | collective-permute-start | bytes 663560 | tf_op jit(solution)/shard_map/ppermute | solution.py:495
  21.1 2.5 %pool.3 = (bf16[1,48,1152]{2,1,0:T(8,128)(2,1)S(1)}, bf16[1,48,1152]{2,1,0:T(8,128)(2,1)S(1)}) custom-call(s32[1]{0:T(128)} %bitcast.refs_0_, bf16[8,2,96,1024]{3,2,1,0:T(8,128)(2,1)S(1)} %get-tuple-element.65.refs_1_, bf16[1024,1024]{1,0:T(8,128)(2,1)S(1)} %get-tuple-element.53.refs_3_.refs_2_, bf16[1024,128]{1,0:T(8,128)(2,1)S(1)} %get-tuple-element.68.refs_4_.refs_3_), custom_call_target="tpu_custom_call" | custom-call | flops 2415919104 | bytes 1572864 | tf_op jit(solution)/shard_map/pool/pallas_call | solution.py:480
  23.5 0.1 collective-permute-start.3
  23.6 0.0 collective-permute-done.2.refs_1_
  23.6 1.3 %collective-permute-done.3.refs_3_ = bf16[1,48,1152]{2,1,0:T(8,128)(2,1)S(1)} collective-permute-done((bf16[1,48,1152]{2,1,0:T(8,128)(2,1)S(1)}, bf16[1,48,1152]{2,1,0:T(8,128)(2,1)S(1)}, u32[]{:S(2)}, u32[]{:S(2)}) %collective-permute-start.3) | collective-permute-done | bytes 110624 | tf_op jit(solution)/shard_map/ppermute | solution.py:495
  24.9 0.5 merge.7
  25.4 1.3 %collective-permute-done.1.refs_1_ = bf16[4,24,1152]{2,1,0:T(8,128)(2,1)S(1)} collective-permute-done((bf16[4,24,1152]{2,1,0:T(8,128)(2,1)S(1)}, bf16[4,24,1152]{2,1,0:T(8,128)(2,1)S(1)}, u32[]{:S(2)}, u32[]{:S(2)}) %collective-permute-start.1) | collective-permute-done | bytes 221216 | tf_op jit(solution)/shard_map/ppermute | solution.py:495
  26.7 0.4 merge.6
  27.1 1.8 %collective-permute-start.7 = (bf16[2,24,1152]{2,1,0:T(8,128)(2,1)S(1)}, bf16[2,24,1152]{2,1,0:T(8,128)(2,1)S(1)}, u32[]{:S(2)}, u32[]{:S(2)}) collective-permute-start(bf16[2,24,1152]{2,1,0:T(8,128)(2,1)S(1)} %get-tuple-element.78), channel_id=1, source_target_pairs={{0,2},{1,3},{2,0},{3,1},{8,10},{9,11},{10,8},{11,9},{16,18},{17,19... | collective-permute-start | bytes 331784 | tf_op jit(solution)/shard_map/ppermute | solution.py:495
  28.9 1.6 %collective-permute-start.4 = (bf16[24,1152]{1,0:T(8,128)(2,1)S(1)}, bf16[24,1152]{1,0:T(8,128)(2,1)S(1)}, u32[]{:S(2)}, u32[]{:S(2)}) collective-permute-start(bf16[24,1152]{1,0:T(8,128)(2,1)S(1)} %get-tuple-element.74), channel_id=1, source_target_pairs={{0,8},{1,9},{2,10},{3,11},{8,16},{9,17},{10,18},{11,19},{16,24},{1... | collective-permute-start | bytes 165896 | tf_op jit(solution)/shard_map/ppermute | solution.py:495
  30.5 2.6 %collective-permute-start.5 = (bf16[24,1152]{1,0:T(8,128)(2,1)S(1)}, bf16[24,1152]{1,0:T(8,128)(2,1)S(1)}, u32[]{:S(2)}, u32[]{:S(2)}) collective-permute-start(bf16[24,1152]{1,0:T(8,128)(2,1)S(1)} %get-tuple-element.75), channel_id=1, source_target_pairs={{0,16},{1,17},{2,18},{3,19},{8,24},{9,25},{10,26},{11,27},{16,0},{... | collective-permute-start | bytes 165896 | tf_op jit(solution)/shard_map/ppermute | solution.py:495
  33.1 1.3 %collective-permute-start.6 = (bf16[24,1152]{1,0:T(8,128)(2,1)S(1)}, bf16[24,1152]{1,0:T(8,128)(2,1)S(1)}, u32[]{:S(2)}, u32[]{:S(2)}) collective-permute-start(bf16[24,1152]{1,0:T(8,128)(2,1)S(1)} %get-tuple-element.76), channel_id=1, source_target_pairs={{0,24},{1,25},{2,26},{3,27},{8,0},{9,1},{10,2},{11,3},{16,8},{17,9... | collective-permute-start | bytes 165896 | tf_op jit(solution)/shard_map/ppermute | solution.py:495
  34.5 0.0 collective-permute-done.7.refs_1_
  34.5 0.4 merge.8
  34.8 0.7 %collective-permute-start.8 = (bf16[12,1152]{1,0:T(8,128)(2,1)S(1)}, bf16[12,1152]{1,0:T(8,128)(2,1)S(1)}, u32[]{:S(2)}, u32[]{:S(2)}) collective-permute-start(bf16[12,1152]{1,0:T(8,128)(2,1)S(1)} %get-tuple-element.80), channel_id=1, source_target_pairs={{0,8},{1,9},{2,10},{3,11},{8,16},{9,17},{10,18},{11,19},{16,24},{1... | collective-permute-start | bytes 82952 | tf_op jit(solution)/shard_map/ppermute | solution.py:495
  35.6 1.2 %collective-permute-start.9 = (bf16[12,1152]{1,0:T(8,128)(2,1)S(1)}, bf16[12,1152]{1,0:T(8,128)(2,1)S(1)}, u32[]{:S(2)}, u32[]{:S(2)}) collective-permute-start(bf16[12,1152]{1,0:T(8,128)(2,1)S(1)} %get-tuple-element.81), channel_id=1, source_target_pairs={{0,16},{1,17},{2,18},{3,19},{8,24},{9,25},{10,26},{11,27},{16,0},{... | collective-permute-start | bytes 82952 | tf_op jit(solution)/shard_map/ppermute | solution.py:495
  36.8 0.0 collective-permute-done.4.refs_1_
  36.8 1.9 %collective-permute-start.10 = (bf16[12,1152]{1,0:T(8,128)(2,1)S(1)}, bf16[12,1152]{1,0:T(8,128)(2,1)S(1)}, u32[]{:S(2)}, u32[]{:S(2)}) collective-permute-start(bf16[12,1152]{1,0:T(8,128)(2,1)S(1)} %get-tuple-element.82), channel_id=1, source_target_pairs={{0,24},{1,25},{2,26},{3,27},{8,0},{9,1},{10,2},{11,3},{16,8},{17,9... | collective-permute-start | bytes 82952 | tf_op jit(solution)/shard_map/ppermute | solution.py:495
  38.7 0.1 pad_add_fusion.refs_0_
  38.8 0.0 collective-permute-done.5.refs_2_
  38.8 0.0 collective-permute-done.6.refs_3_
  38.8 1.9 %collective-permute-done.8.refs_5_ = bf16[12,1152]{1,0:T(8,128)(2,1)S(1)} collective-permute-done((bf16[12,1152]{1,0:T(8,128)(2,1)S(1)}, bf16[12,1152]{1,0:T(8,128)(2,1)S(1)}, u32[]{:S(2)}, u32[]{:S(2)}) %collective-permute-start.8) | collective-permute-done | bytes 27680 | tf_op jit(solution)/shard_map/ppermute | solution.py:495
  40.7 0.5 collective-permute-done.9.refs_6_
  41.3 0.0 collective-permute-done.10.refs_7_
  41.3 0.5 merge.9.refs_0_
  41.8 0.1 collective-permute-start.12
  41.9 1.6 %collective-permute-start.11 = (bf16[36,1024]{1,0:T(8,128)(2,1)S(1)}, bf16[36,1024]{1,0:T(8,128)(2,1)S(1)}, u32[]{:S(2)}, u32[]{:S(2)}) collective-permute-start(bf16[36,1024]{1,0:T(8,128)(2,1)S(1)} %merge.9.refs_0_), channel_id=1, source_target_pairs={{4,0},{5,1},{6,2},{7,3},{0,4},{1,5},{2,6},{3,7},{12,8},{13,9},{14,... | collective-permute-start | bytes 221192 | tf_op jit(solution)/shard_map/ppermute | solution.py:583
  43.5 0.7 %collective-permute-start.13 = (bf16[36,1024]{1,0:T(8,128)(2,1)S(1)}, bf16[36,1024]{1,0:T(8,128)(2,1)S(1)}, u32[]{:S(2)}, u32[]{:S(2)}) collective-permute-start(bf16[36,1024]{1,0:T(8,128)(2,1)S(1)} %merge.9.refs_0_), channel_id=1, source_target_pairs={{1,0},{0,1},{3,2},{2,3},{5,4},{4,5},{7,6},{6,7},{9,8},{8,9},{11,10... | collective-permute-start | bytes 221192 | tf_op jit(solution)/shard_map/ppermute | solution.py:583
  44.2 0.0 copy-done.2
  44.2 0.0 copy-done.4
  44.2 0.0 copy-done.6
  44.2 0.0 copy-start
  44.2 0.0 copy-start.1
  44.2 3.7 %stage.1 = (f32[16,48,216]{2,1,0:T(8,128)S(1)}, bf16[1024,1024]{1,0:T(8,128)(2,1)S(1)}, bf16[1024,1024]{1,0:T(8,128)(2,1)S(1)}, bf16[1024,1024]{1,0:T(8,128)(2,1)S(1)}) custom-call(s32[2]{0:T(128)S(1)} %pad_add_fusion.refs_0_, s32[4,216]{1,0:T(4,128)S(1)} %copy-done.6, s32[12,96]{1,0:T(8,128)S(1)} %copy-done.4, f32[13,16,13]{2,1,0:T(8,128)S(1)} %bitcast.4, ...), custom_call_target="tpu_custom_call" | custom-call | flops 1000 | bytes 10485760 | tf_op jit(solution)/shard_map/stage/pallas_call | solution.py:558
  47.9 0.5 collective-permute-done.12.refs_4_
  48.4 0.0 collective-permute-done.11.refs_1_
  48.4 0.0 copy-start.5
  48.4 1.5 %collective-permute-start.15 = (bf16[36,1024]{1,0:T(8,128)(2,1)S(1)}, bf16[36,1024]{1,0:T(8,128)(2,1)S(1)}, u32[]{:S(2)}, u32[]{:S(2)}) collective-permute-start(bf16[36,1024]{1,0:T(8,128)(2,1)S(1)} %collective-permute-done.12.refs_4_), channel_id=1, source_target_pairs={{4,0},{5,1},{6,2},{7,3},{0,4},{1,5},{2,6},{3,7},{12,8},{13,9},{14,... | collective-permute-start | bytes 221192 | tf_op jit(solution)/shard_map/ppermute | solution.py:583
  50.0 0.0 collective-permute-start.14
  50.0 0.0 copy-done
  50.0 0.0 copy-done.1
  50.0 0.3 load.1
  50.3 0.0 collective-permute-done.13.refs_2_
  50.3 2.6 %collective-permute-done.15.refs_5_ = bf16[36,1024]{1,0:T(8,128)(2,1)S(1)} collective-permute-done((bf16[36,1024]{1,0:T(8,128)(2,1)S(1)}, bf16[36,1024]{1,0:T(8,128)(2,1)S(1)}, u32[]{:S(2)}, u32[]{:S(2)}) %collective-permute-start.15) | collective-permute-done | bytes 73760 | tf_op jit(solution)/shard_map/ppermute | solution.py:583
  52.9 0.0 collective-permute-done.14.refs_3_
  52.9 0.0 copy-done.5
  52.9 3.8 %attend.1 = bf16[6,6,1024]{2,1,0:T(8,128)(2,1)} custom-call(bf16[36,1024]{1,0:T(8,128)(2,1)S(1)} %merge.9.refs_0_, bf16[36,1024]{1,0:T(8,128)(2,1)S(1)} %collective-permute-done.11.refs_1_, bf16[36,1024]{1,0:T(8,128)(2,1)S(1)} %collective-permute-done.13.refs_2_, bf16[36,1024]{1,0:T(8,128)(2,1)S(1)} %collective-permute-done.14.refs_3_, ...), custom_call_target="tpu_custom_call" | custom-call | tf_op jit(solution)/shard_map/attend/pallas_call | solution.py:605
Async XLA Ops:
  0.0 0.7 %copy-start.3 = (f32[16,64]{1,0:T(8,128)S(1)}, f32[16,64]{1,0:T(8,128)}, u32[]{:S(2)}) copy-start(f32[16,64]{1,0:T(8,128)} %query_ref.1) | copy-start | bytes 12292
  14.3 3.1 %collective-permute-start = (bf16[4,48,1152]{2,1,0:T(8,128)(2,1)S(1)}, bf16[4,48,1152]{2,1,0:T(8,128)(2,1)S(1)}, u32[]{:S(2)}, u32[]{:S(2)}) collective-permute-start(bf16[4,48,1152]{2,1,0:T(8,128)(2,1)S(1)} %get-tuple-element.56), channel_id=1, source_target_pairs={{0,1},{1,0},{2,3},{3,2},{8,9},{9,8},{10,11},{11,10},{16,17},{17,16... | collective-permute-start | bytes 1327112 | tf_op jit(solution)/shard_map/ppermute | solution.py:495
  17.2 6.4 %collective-permute-start.2 = (bf16[1,48,1152]{2,1,0:T(8,128)(2,1)S(1)}, bf16[1,48,1152]{2,1,0:T(8,128)(2,1)S(1)}, u32[]{:S(2)}, u32[]{:S(2)}) collective-permute-start(bf16[1,48,1152]{2,1,0:T(8,128)(2,1)S(1)} %get-tuple-element.67), channel_id=1, source_target_pairs={{0,1},{1,0},{2,3},{3,2},{8,9},{9,8},{10,11},{11,10},{16,17},{17,16... | collective-permute-start | bytes 331784 | tf_op jit(solution)/shard_map/ppermute | solution.py:495
  18.0 26.2 %copy-start.2 = (f32[16,13,13]{2,0,1:T(8,128)S(1)}, f32[16,13,13]{2,0,1:T(8,128)}, u32[]{:S(2)}) copy-start(f32[16,13,13]{2,0,1:T(8,128)} %param.23) | copy-start | bytes 32452
  18.0 26.2 %copy-start.4 = (s32[12,96]{1,0:T(8,128)S(1)}, s32[12,96]{1,0:T(8,128)}, u32[]{:S(2)}) copy-start(s32[12,96]{1,0:T(8,128)} %refs_2_.1) | copy-start | bytes 13828
  18.1 26.1 %copy-start.6 = (s32[4,216]{1,0:T(4,128)S(1)}, s32[4,216]{1,0:T(4,128)}, u32[]{:S(2)}) copy-start(s32[4,216]{1,0:T(4,128)} %constant.16.clone.refs_1_) | copy-start | bytes 10372
  18.1 8.6 %collective-permute-start.1 = (bf16[4,24,1152]{2,1,0:T(8,128)(2,1)S(1)}, bf16[4,24,1152]{2,1,0:T(8,128)(2,1)S(1)}, u32[]{:S(2)}, u32[]{:S(2)}) collective-permute-start(bf16[4,24,1152]{2,1,0:T(8,128)(2,1)S(1)} %get-tuple-element.60), channel_id=1, source_target_pairs={{0,2},{1,3},{2,0},{3,1},{8,10},{9,11},{10,8},{11,9},{16,18},{17,19... | collective-permute-start | bytes 663560 | tf_op jit(solution)/shard_map/ppermute | solution.py:495
  23.5 1.4 %collective-permute-start.3 = (bf16[1,48,1152]{2,1,0:T(8,128)(2,1)S(1)}, bf16[1,48,1152]{2,1,0:T(8,128)(2,1)S(1)}, u32[]{:S(2)}, u32[]{:S(2)}) collective-permute-start(bf16[1,48,1152]{2,1,0:T(8,128)(2,1)S(1)} %get-tuple-element.70), channel_id=1, source_target_pairs={{0,1},{1,0},{2,3},{3,2},{8,9},{9,8},{10,11},{11,10},{16,17},{17,16... | collective-permute-start | bytes 331784 | tf_op jit(solution)/shard_map/ppermute | solution.py:495
  27.1 7.3 %collective-permute-start.7 = (bf16[2,24,1152]{2,1,0:T(8,128)(2,1)S(1)}, bf16[2,24,1152]{2,1,0:T(8,128)(2,1)S(1)}, u32[]{:S(2)}, u32[]{:S(2)}) collective-permute-start(bf16[2,24,1152]{2,1,0:T(8,128)(2,1)S(1)} %get-tuple-element.78), channel_id=1, source_target_pairs={{0,2},{1,3},{2,0},{3,1},{8,10},{9,11},{10,8},{11,9},{16,18},{17,19... | collective-permute-start | bytes 331784 | tf_op jit(solution)/shard_map/ppermute | solution.py:495
  28.9 7.9 %collective-permute-start.4 = (bf16[24,1152]{1,0:T(8,128)(2,1)S(1)}, bf16[24,1152]{1,0:T(8,128)(2,1)S(1)}, u32[]{:S(2)}, u32[]{:S(2)}) collective-permute-start(bf16[24,1152]{1,0:T(8,128)(2,1)S(1)} %get-tuple-element.74), channel_id=1, source_target_pairs={{0,8},{1,9},{2,10},{3,11},{8,16},{9,17},{10,18},{11,19},{16,24},{1... | collective-permute-start | bytes 165896 | tf_op jit(solution)/shard_map/ppermute | solution.py:495
  30.5 8.3 %collective-permute-start.5 = (bf16[24,1152]{1,0:T(8,128)(2,1)S(1)}, bf16[24,1152]{1,0:T(8,128)(2,1)S(1)}, u32[]{:S(2)}, u32[]{:S(2)}) collective-permute-start(bf16[24,1152]{1,0:T(8,128)(2,1)S(1)} %get-tuple-element.75), channel_id=1, source_target_pairs={{0,16},{1,17},{2,18},{3,19},{8,24},{9,25},{10,26},{11,27},{16,0},{... | collective-permute-start | bytes 165896 | tf_op jit(solution)/shard_map/ppermute | solution.py:495
  33.1 5.7 %collective-permute-start.6 = (bf16[24,1152]{1,0:T(8,128)(2,1)S(1)}, bf16[24,1152]{1,0:T(8,128)(2,1)S(1)}, u32[]{:S(2)}, u32[]{:S(2)}) collective-permute-start(bf16[24,1152]{1,0:T(8,128)(2,1)S(1)} %get-tuple-element.76), channel_id=1, source_target_pairs={{0,24},{1,25},{2,26},{3,27},{8,0},{9,1},{10,2},{11,3},{16,8},{17,9... | collective-permute-start | bytes 165896 | tf_op jit(solution)/shard_map/ppermute | solution.py:495
  34.8 5.9 %collective-permute-start.8 = (bf16[12,1152]{1,0:T(8,128)(2,1)S(1)}, bf16[12,1152]{1,0:T(8,128)(2,1)S(1)}, u32[]{:S(2)}, u32[]{:S(2)}) collective-permute-start(bf16[12,1152]{1,0:T(8,128)(2,1)S(1)} %get-tuple-element.80), channel_id=1, source_target_pairs={{0,8},{1,9},{2,10},{3,11},{8,16},{9,17},{10,18},{11,19},{16,24},{1... | collective-permute-start | bytes 82952 | tf_op jit(solution)/shard_map/ppermute | solution.py:495
  35.6 5.7 %collective-permute-start.9 = (bf16[12,1152]{1,0:T(8,128)(2,1)S(1)}, bf16[12,1152]{1,0:T(8,128)(2,1)S(1)}, u32[]{:S(2)}, u32[]{:S(2)}) collective-permute-start(bf16[12,1152]{1,0:T(8,128)(2,1)S(1)} %get-tuple-element.81), channel_id=1, source_target_pairs={{0,16},{1,17},{2,18},{3,19},{8,24},{9,25},{10,26},{11,27},{16,0},{... | collective-permute-start | bytes 82952 | tf_op jit(solution)/shard_map/ppermute | solution.py:495
  36.8 4.5 %collective-permute-start.10 = (bf16[12,1152]{1,0:T(8,128)(2,1)S(1)}, bf16[12,1152]{1,0:T(8,128)(2,1)S(1)}, u32[]{:S(2)}, u32[]{:S(2)}) collective-permute-start(bf16[12,1152]{1,0:T(8,128)(2,1)S(1)} %get-tuple-element.82), channel_id=1, source_target_pairs={{0,24},{1,25},{2,26},{3,27},{8,0},{9,1},{10,2},{11,3},{16,8},{17,9... | collective-permute-start | bytes 82952 | tf_op jit(solution)/shard_map/ppermute | solution.py:495
  41.8 6.6 %collective-permute-start.12 = (bf16[36,1024]{1,0:T(8,128)(2,1)S(1)}, bf16[36,1024]{1,0:T(8,128)(2,1)S(1)}, u32[]{:S(2)}, u32[]{:S(2)}) collective-permute-start(bf16[36,1024]{1,0:T(8,128)(2,1)S(1)} %merge.9.refs_0_), channel_id=1, source_target_pairs={{27,0},{2,1},{1,2},{8,3},{31,4},{6,5},{5,6},{12,7},{3,8},{10,9},{9... | collective-permute-start | bytes 221192 | tf_op jit(solution)/shard_map/ppermute | solution.py:583
  41.9 6.5 %collective-permute-start.11 = (bf16[36,1024]{1,0:T(8,128)(2,1)S(1)}, bf16[36,1024]{1,0:T(8,128)(2,1)S(1)}, u32[]{:S(2)}, u32[]{:S(2)}) collective-permute-start(bf16[36,1024]{1,0:T(8,128)(2,1)S(1)} %merge.9.refs_0_), channel_id=1, source_target_pairs={{4,0},{5,1},{6,2},{7,3},{0,4},{1,5},{2,6},{3,7},{12,8},{13,9},{14,... | collective-permute-start | bytes 221192 | tf_op jit(solution)/shard_map/ppermute | solution.py:583
  43.5 6.8 %collective-permute-start.13 = (bf16[36,1024]{1,0:T(8,128)(2,1)S(1)}, bf16[36,1024]{1,0:T(8,128)(2,1)S(1)}, u32[]{:S(2)}, u32[]{:S(2)}) collective-permute-start(bf16[36,1024]{1,0:T(8,128)(2,1)S(1)} %merge.9.refs_0_), channel_id=1, source_target_pairs={{1,0},{0,1},{3,2},{2,3},{5,4},{4,5},{7,6},{6,7},{9,8},{8,9},{11,10... | collective-permute-start | bytes 221192 | tf_op jit(solution)/shard_map/ppermute | solution.py:583
  44.2 5.8 %copy-start = (bf16[1024,1024]{1,0:T(8,128)(2,1)S(1)}, bf16[1024,1024]{1,0:T(8,128)(2,1)}, u32[]{:S(2)}) copy-start(bf16[1024,1024]{1,0:T(8,128)(2,1)} %refs_0_) | copy-start | bytes 6291460
  44.2 5.8 %copy-start.1 = (bf16[1024,1024]{1,0:T(8,128)(2,1)S(1)}, bf16[1024,1024]{1,0:T(8,128)(2,1)}, u32[]{:S(2)}) copy-start(bf16[1024,1024]{1,0:T(8,128)(2,1)} %refs_1_.3) | copy-start | bytes 6291460
  48.4 4.5 %copy-start.5 = (f32[1024]{0:T(1024)S(1)}, f32[1024]{0:T(1024)}, u32[]{:S(2)}) copy-start(f32[1024]{0:T(1024)} %param.18) | copy-start | bytes 12292
  48.4 4.4 %collective-permute-start.15 = (bf16[36,1024]{1,0:T(8,128)(2,1)S(1)}, bf16[36,1024]{1,0:T(8,128)(2,1)S(1)}, u32[]{:S(2)}, u32[]{:S(2)}) collective-permute-start(bf16[36,1024]{1,0:T(8,128)(2,1)S(1)} %collective-permute-done.12.refs_4_), channel_id=1, source_target_pairs={{4,0},{5,1},{6,2},{7,3},{0,4},{1,5},{2,6},{3,7},{12,8},{13,9},{14,... | collective-permute-start | bytes 221192 | tf_op jit(solution)/shard_map/ppermute | solution.py:583
  50.0 2.9 %collective-permute-start.14 = (bf16[36,1024]{1,0:T(8,128)(2,1)S(1)}, bf16[36,1024]{1,0:T(8,128)(2,1)S(1)}, u32[]{:S(2)}, u32[]{:S(2)}) collective-permute-start(bf16[36,1024]{1,0:T(8,128)(2,1)S(1)} %collective-permute-done.11.refs_1_), channel_id=1, source_target_pairs={{1,0},{0,1},{3,2},{2,3},{5,4},{4,5},{7,6},{6,7},{9,8},{8,9},{11,10... | collective-permute-start | bytes 221192 | tf_op jit(solution)/shard_map/ppermute | solution.py:583

commit v5 on v4

--- a/solution.py
+++ b/solution.py
@@ -172,6 +172,7 @@
 
     later = rest_ref.shape[1]
     rest = pltpu.make_async_copy(token_ref.at[:, pl.ds(count, later)], rest_ref, sems.at[2])
+    pltpu.make_async_copy(first_ref, slots.at[0], sems.at[0]).start()
     fetch(1).start()
     order = column_order(block, tile, columns)
 
@@ -189,8 +190,6 @@
             (step // tiles) * tiles + (step % tiles + tiles - high) % tiles,
         )
 
-    fetch(2).start()
-    work(0, first_ref[...])
 
     def body(step, _):
         fetch(step).wait()
@@ -206,7 +205,7 @@
 
         return 0
 
-    lax.fori_loop(1, steps, body, 0)
+    lax.fori_loop(0, steps, body, 0)
     rest.wait()
 
 

time: 56.9 us -> 56.1 us (0.986)
  Pallas kernels: 28.7 us -> 27.9 us
    pallas_call x1, Pallas kernels: 10.8 us -> 9.99 us  [lead_pool(): pl.pallas_call(functools.partial(lead_kernel, heads, head_dim, lead_rows,...]
  transfers between devices with their start and end apart: 16 -> 16, of which waited for: 6 -> 6; matrix products, arithmetic and copies ran while one was open for 0% -> 0% of each run, Pallas kernels for 18% -> 19%
where the time goes in v5:
time: 56.1 us; the launch traced here: 55.9 us
  Pallas kernels  27.9 us (50%)
  starting transfers between devices  18.8 us (34%)
  waiting for transfers between devices  8.18 us (15%)
  local copies, waits for them, and re-layouts  0.73 us (1%)
    ppermute x11, starting transfers between devices, exchange(): lax.ppermute(array, ('var', 'lon'), [(i, moved(i)) for i in range(devices)])  14.9 us
    pallas_call x1, Pallas kernels, lead_pool(): pl.pallas_call(functools.partial(lead_kernel, heads, head_dim, lead_rows,...  9.99 us
    ppermute x11, waiting for transfers between devices, exchange(): lax.ppermute(array, ('var', 'lon'), [(i, moved(i)) for i in range(devices)])  5.07 us
    pallas_call x2, Pallas kernels, pool(): pl.pallas_call(functools.partial(pool_kernel, heads, head_dim, row, tiles...  4.91 us
    ppermute x5, starting transfers between devices, partner(): return lax.ppermute(array, ('var', 'lat', 'lon'), pairs)  3.89 us
    pallas_call x1, Pallas kernels, on_device(): pl.pallas_call(functools.partial(attend_kernel, heads, len(window)), in_s...  3.78 us
    pallas_call x1, Pallas kernels, on_device(): pl.pallas_call(functools.partial(stage_kernel, rows, columns, len(staged)...  3.7 us
    ppermute x5, waiting for transfers between devices, partner(): return lax.ppermute(array, ('var', 'lat', 'lon'), pairs)  3.12 us
  transfers between devices with their start and end apart: 16, of which 6 were waited for; matrix products, arithmetic and copies ran while one was open for 0% of the time, Pallas kernels for 19%

profile of v5, /device:TPU:0, one launch (start us, length us, event | category | flops | bytes accessed | tf_op | source)
XLA Modules:
  0.0 55.9 jit_solution(12057104220361716833)
XLA Ops:
  0.0 0.0 copy-start.3
  0.0 0.7 %copy-done.3 = f32[16,64]{1,0:T(8,128)S(1)} copy-done((f32[16,64]{1,0:T(8,128)S(1)}, f32[16,64]{1,0:T(8,128)}, u32[]{:S(2)}) %copy-start.3) | copy-done | bytes 4120
  0.7 2.7 %pre.1 = (bf16[1024,128]{1,0:T(8,128)(2,1)S(1)}, bf16[1024,1024]{1,0:T(8,128)(2,1)S(1)}, bf16[8,96,1024]{2,1,0:T(8,128)(2,1)S(1)}) custom-call(bf16[8,6,96,1024]{3,2,1,0:T(8,128)(2,1)} %refs_1_.2, bf16[1024,1024]{1,0:T(8,128)(2,1)} %value_ref.1, f32[16,64]{1,0:T(8,128)S(1)} %copy-done.3, bf16[1024,1024]{1,0:T(8,128)(2,1)} %key_ref.1), custom_call_target="tpu_custom_call" | custom-call | tf_op jit(solution)/shard_map/pre/pallas_call | solution.py:447
  3.4 10.0 %lead.1 = (bf16[4,48,1152]{2,1,0:T(8,128)(2,1)S(1)}, bf16[4,48,1152]{2,1,0:T(8,128)(2,1)S(1)}, bf16[8,2,96,1024]{3,2,1,0:T(8,128)(2,1)S(1)}) custom-call(s32[1]{0:T(128)} %bitcast.refs_0_, bf16[8,6,96,1024]{3,2,1,0:T(8,128)(2,1)} %refs_1_.2, bf16[8,96,1024]{2,1,0:T(8,128)(2,1)S(1)} %get-tuple-element.52.refs_2_, ...), custom_call_target="tpu_custom_call" | custom-call | flops 9663676416 | bytes 6291456 | tf_op jit(solution)/shard_map/lead/pallas_call | solution.py:462
  13.4 0.5 collective-permute-start
  14.0 2.5 %pool.2 = (bf16[1,48,1152]{2,1,0:T(8,128)(2,1)S(1)}, bf16[1,48,1152]{2,1,0:T(8,128)(2,1)S(1)}) custom-call(s32[1]{0:T(128)} %bitcast.refs_0_, bf16[8,2,96,1024]{3,2,1,0:T(8,128)(2,1)S(1)} %get-tuple-element.65.refs_1_, bf16[1024,1024]{1,0:T(8,128)(2,1)S(1)} %get-tuple-element.53.refs_3_.refs_2_, bf16[1024,128]{1,0:T(8,128)(2,1)S(1)} %get-tuple-element.68.refs_4_.refs_3_), custom_call_target="tpu_custom_call" | custom-call | flops 2415919104 | bytes 1572864 | tf_op jit(solution)/shard_map/pool/pallas_call | solution.py:479
  16.4 0.1 collective-permute-start.2
  16.5 0.0 collective-permute-done.refs_1_
  16.5 0.7 %merge.5 = (bf16[4,24,1152]{2,1,0:T(8,128)(2,1)S(1)}, bf16[4,24,1152]{2,1,0:T(8,128)(2,1)S(1)}) custom-call(bf16[4,48,1152]{2,1,0:T(8,128)(2,1)S(1)} %get-tuple-element.55.refs_0_, bf16[4,48,1152]{2,1,0:T(8,128)(2,1)S(1)} %collective-permute-done.refs_1_), custom_call_target="tpu_custom_call" | custom-call | flops 100663296 | bytes 1572864 | tf_op jit(solution)/shard_map/merge/pallas_call | solution.py:287
  17.2 0.0 copy-start.2
  17.2 0.0 copy-start.4
  17.2 0.0 copy-start.6
  17.2 3.0 %collective-permute-start.1 = (bf16[4,24,1152]{2,1,0:T(8,128)(2,1)S(1)}, bf16[4,24,1152]{2,1,0:T(8,128)(2,1)S(1)}, u32[]{:S(2)}, u32[]{:S(2)}) collective-permute-start(bf16[4,24,1152]{2,1,0:T(8,128)(2,1)S(1)} %get-tuple-element.60), channel_id=1, source_target_pairs={{0,2},{1,3},{2,0},{3,1},{8,10},{9,11},{10,8},{11,9},{16,18},{17,19... | collective-permute-start | bytes 663560 | tf_op jit(solution)/shard_map/ppermute | solution.py:494
  20.2 2.5 %pool.3 = (bf16[1,48,1152]{2,1,0:T(8,128)(2,1)S(1)}, bf16[1,48,1152]{2,1,0:T(8,128)(2,1)S(1)}) custom-call(s32[1]{0:T(128)} %bitcast.refs_0_, bf16[8,2,96,1024]{3,2,1,0:T(8,128)(2,1)S(1)} %get-tuple-element.65.refs_1_, bf16[1024,1024]{1,0:T(8,128)(2,1)S(1)} %get-tuple-element.53.refs_3_.refs_2_, bf16[1024,128]{1,0:T(8,128)(2,1)S(1)} %get-tuple-element.68.refs_4_.refs_3_), custom_call_target="tpu_custom_call" | custom-call | flops 2415919104 | bytes 1572864 | tf_op jit(solution)/shard_map/pool/pallas_call | solution.py:479
  22.7 0.1 collective-permute-start.3
  22.8 0.0 collective-permute-done.2.refs_1_
  22.8 1.3 %collective-permute-done.3.refs_3_ = bf16[1,48,1152]{2,1,0:T(8,128)(2,1)S(1)} collective-permute-done((bf16[1,48,1152]{2,1,0:T(8,128)(2,1)S(1)}, bf16[1,48,1152]{2,1,0:T(8,128)(2,1)S(1)}, u32[]{:S(2)}, u32[]{:S(2)}) %collective-permute-start.3) | collective-permute-done | bytes 110624 | tf_op jit(solution)/shard_map/ppermute | solution.py:494
  24.1 0.5 merge.7
  24.6 1.3 %collective-permute-done.1.refs_1_ = bf16[4,24,1152]{2,1,0:T(8,128)(2,1)S(1)} collective-permute-done((bf16[4,24,1152]{2,1,0:T(8,128)(2,1)S(1)}, bf16[4,24,1152]{2,1,0:T(8,128)(2,1)S(1)}, u32[]{:S(2)}, u32[]{:S(2)}) %collective-permute-start.1) | collective-permute-done | bytes 221216 | tf_op jit(solution)/shard_map/ppermute | solution.py:494
  25.9 0.4 merge.6
  26.3 1.8 %collective-permute-start.7 = (bf16[2,24,1152]{2,1,0:T(8,128)(2,1)S(1)}, bf16[2,24,1152]{2,1,0:T(8,128)(2,1)S(1)}, u32[]{:S(2)}, u32[]{:S(2)}) collective-permute-start(bf16[2,24,1152]{2,1,0:T(8,128)(2,1)S(1)} %get-tuple-element.78), channel_id=1, source_target_pairs={{0,2},{1,3},{2,0},{3,1},{8,10},{9,11},{10,8},{11,9},{16,18},{17,19... | collective-permute-start | bytes 331784 | tf_op jit(solution)/shard_map/ppermute | solution.py:494
  28.1 1.6 %collective-permute-start.4 = (bf16[24,1152]{1,0:T(8,128)(2,1)S(1)}, bf16[24,1152]{1,0:T(8,128)(2,1)S(1)}, u32[]{:S(2)}, u32[]{:S(2)}) collective-permute-start(bf16[24,1152]{1,0:T(8,128)(2,1)S(1)} %get-tuple-element.74), channel_id=1, source_target_pairs={{0,8},{1,9},{2,10},{3,11},{8,16},{9,17},{10,18},{11,19},{16,24},{1... | collective-permute-start | bytes 165896 | tf_op jit(solution)/shard_map/ppermute | solution.py:494
  29.7 2.6 %collective-permute-start.5 = (bf16[24,1152]{1,0:T(8,128)(2,1)S(1)}, bf16[24,1152]{1,0:T(8,128)(2,1)S(1)}, u32[]{:S(2)}, u32[]{:S(2)}) collective-permute-start(bf16[24,1152]{1,0:T(8,128)(2,1)S(1)} %get-tuple-element.75), channel_id=1, source_target_pairs={{0,16},{1,17},{2,18},{3,19},{8,24},{9,25},{10,26},{11,27},{16,0},{... | collective-permute-start | bytes 165896 | tf_op jit(solution)/shard_map/ppermute | solution.py:494
  32.3 1.3 %collective-permute-start.6 = (bf16[24,1152]{1,0:T(8,128)(2,1)S(1)}, bf16[24,1152]{1,0:T(8,128)(2,1)S(1)}, u32[]{:S(2)}, u32[]{:S(2)}) collective-permute-start(bf16[24,1152]{1,0:T(8,128)(2,1)S(1)} %get-tuple-element.76), channel_id=1, source_target_pairs={{0,24},{1,25},{2,26},{3,27},{8,0},{9,1},{10,2},{11,3},{16,8},{17,9... | collective-permute-start | bytes 165896 | tf_op jit(solution)/shard_map/ppermute | solution.py:494
  33.6 0.0 collective-permute-done.7.refs_1_
  33.6 0.4 merge.8
  34.0 0.7 %collective-permute-start.8 = (bf16[12,1152]{1,0:T(8,128)(2,1)S(1)}, bf16[12,1152]{1,0:T(8,128)(2,1)S(1)}, u32[]{:S(2)}, u32[]{:S(2)}) collective-permute-start(bf16[12,1152]{1,0:T(8,128)(2,1)S(1)} %get-tuple-element.80), channel_id=1, source_target_pairs={{0,8},{1,9},{2,10},{3,11},{8,16},{9,17},{10,18},{11,19},{16,24},{1... | collective-permute-start | bytes 82952 | tf_op jit(solution)/shard_map/ppermute | solution.py:494
  34.7 1.2 %collective-permute-start.9 = (bf16[12,1152]{1,0:T(8,128)(2,1)S(1)}, bf16[12,1152]{1,0:T(8,128)(2,1)S(1)}, u32[]{:S(2)}, u32[]{:S(2)}) collective-permute-start(bf16[12,1152]{1,0:T(8,128)(2,1)S(1)} %get-tuple-element.81), channel_id=1, source_target_pairs={{0,16},{1,17},{2,18},{3,19},{8,24},{9,25},{10,26},{11,27},{16,0},{... | collective-permute-start | bytes 82952 | tf_op jit(solution)/shard_map/ppermute | solution.py:494
  36.0 0.0 collective-permute-done.4.refs_1_
  36.0 1.9 %collective-permute-start.10 = (bf16[12,1152]{1,0:T(8,128)(2,1)S(1)}, bf16[12,1152]{1,0:T(8,128)(2,1)S(1)}, u32[]{:S(2)}, u32[]{:S(2)}) collective-permute-start(bf16[12,1152]{1,0:T(8,128)(2,1)S(1)} %get-tuple-element.82), channel_id=1, source_target_pairs={{0,24},{1,25},{2,26},{3,27},{8,0},{9,1},{10,2},{11,3},{16,8},{17,9... | collective-permute-start | bytes 82952 | tf_op jit(solution)/shard_map/ppermute | solution.py:494
  37.9 0.1 pad_add_fusion.refs_0_
  38.0 0.0 collective-permute-done.5.refs_2_
  38.0 0.0 collective-permute-done.6.refs_3_
  38.0 1.9 %collective-permute-done.8.refs_5_ = bf16[12,1152]{1,0:T(8,128)(2,1)S(1)} collective-permute-done((bf16[12,1152]{1,0:T(8,128)(2,1)S(1)}, bf16[12,1152]{1,0:T(8,128)(2,1)S(1)}, u32[]{:S(2)}, u32[]{:S(2)}) %collective-permute-start.8) | collective-permute-done | bytes 27680 | tf_op jit(solution)/shard_map/ppermute | solution.py:494
  39.9 0.5 collective-permute-done.9.refs_6_
  40.5 0.0 collective-permute-done.10.refs_7_
  40.5 0.5 merge.9.refs_0_
  41.0 0.1 collective-permute-start.12
  41.1 1.6 %collective-permute-start.11 = (bf16[36,1024]{1,0:T(8,128)(2,1)S(1)}, bf16[36,1024]{1,0:T(8,128)(2,1)S(1)}, u32[]{:S(2)}, u32[]{:S(2)}) collective-permute-start(bf16[36,1024]{1,0:T(8,128)(2,1)S(1)} %merge.9.refs_0_), channel_id=1, source_target_pairs={{4,0},{5,1},{6,2},{7,3},{0,4},{1,5},{2,6},{3,7},{12,8},{13,9},{14,... | collective-permute-start | bytes 221192 | tf_op jit(solution)/shard_map/ppermute | solution.py:582
  42.6 0.7 %collective-permute-start.13 = (bf16[36,1024]{1,0:T(8,128)(2,1)S(1)}, bf16[36,1024]{1,0:T(8,128)(2,1)S(1)}, u32[]{:S(2)}, u32[]{:S(2)}) collective-permute-start(bf16[36,1024]{1,0:T(8,128)(2,1)S(1)} %merge.9.refs_0_), channel_id=1, source_target_pairs={{1,0},{0,1},{3,2},{2,3},{5,4},{4,5},{7,6},{6,7},{9,8},{8,9},{11,10... | collective-permute-start | bytes 221192 | tf_op jit(solution)/shard_map/ppermute | solution.py:582
  43.4 0.0 copy-done.2
  43.4 0.0 copy-done.4
  43.4 0.0 copy-done.6
  43.4 0.0 copy-start
  43.4 0.0 copy-start.1
  43.4 3.7 %stage.1 = (f32[16,48,216]{2,1,0:T(8,128)S(1)}, bf16[1024,1024]{1,0:T(8,128)(2,1)S(1)}, bf16[1024,1024]{1,0:T(8,128)(2,1)S(1)}, bf16[1024,1024]{1,0:T(8,128)(2,1)S(1)}) custom-call(s32[2]{0:T(128)S(1)} %pad_add_fusion.refs_0_, s32[4,216]{1,0:T(4,128)S(1)} %copy-done.6, s32[12,96]{1,0:T(8,128)S(1)} %copy-done.4, f32[13,16,13]{2,1,0:T(8,128)S(1)} %bitcast.4, ...), custom_call_target="tpu_custom_call" | custom-call | flops 1000 | bytes 10485760 | tf_op jit(solution)/shard_map/stage/pallas_call | solution.py:557
  47.1 0.5 collective-permute-done.12.refs_4_
  47.6 0.0 collective-permute-done.11.refs_1_
  47.6 0.0 copy-start.5
  47.6 1.5 %collective-permute-start.15 = (bf16[36,1024]{1,0:T(8,128)(2,1)S(1)}, bf16[36,1024]{1,0:T(8,128)(2,1)S(1)}, u32[]{:S(2)}, u32[]{:S(2)}) collective-permute-start(bf16[36,1024]{1,0:T(8,128)(2,1)S(1)} %collective-permute-done.12.refs_4_), channel_id=1, source_target_pairs={{4,0},{5,1},{6,2},{7,3},{0,4},{1,5},{2,6},{3,7},{12,8},{13,9},{14,... | collective-permute-start | bytes 221192 | tf_op jit(solution)/shard_map/ppermute | solution.py:582
  49.1 0.0 collective-permute-start.14
  49.1 0.0 copy-done
  49.1 0.0 copy-done.1
  49.1 0.3 load.1
  49.5 0.0 collective-permute-done.13.refs_2_
  49.5 2.6 %collective-permute-done.15.refs_5_ = bf16[36,1024]{1,0:T(8,128)(2,1)S(1)} collective-permute-done((bf16[36,1024]{1,0:T(8,128)(2,1)S(1)}, bf16[36,1024]{1,0:T(8,128)(2,1)S(1)}, u32[]{:S(2)}, u32[]{:S(2)}) %collective-permute-start.15) | collective-permute-done | bytes 73760 | tf_op jit(solution)/shard_map/ppermute | solution.py:582
  52.1 0.0 collective-permute-done.14.refs_3_
  52.1 0.0 copy-done.5
  52.1 3.8 %attend.1 = bf16[6,6,1024]{2,1,0:T(8,128)(2,1)} custom-call(bf16[36,1024]{1,0:T(8,128)(2,1)S(1)} %merge.9.refs_0_, bf16[36,1024]{1,0:T(8,128)(2,1)S(1)} %collective-permute-done.11.refs_1_, bf16[36,1024]{1,0:T(8,128)(2,1)S(1)} %collective-permute-done.13.refs_2_, bf16[36,1024]{1,0:T(8,128)(2,1)S(1)} %collective-permute-done.14.refs_3_, ...), custom_call_target="tpu_custom_call" | custom-call | tf_op jit(solution)/shard_map/attend/pallas_call | solution.py:604
Async XLA Ops:
  0.0 0.7 %copy-start.3 = (f32[16,64]{1,0:T(8,128)S(1)}, f32[16,64]{1,0:T(8,128)}, u32[]{:S(2)}) copy-start(f32[16,64]{1,0:T(8,128)} %query_ref.1) | copy-start | bytes 12292
  13.4 3.1 %collective-permute-start = (bf16[4,48,1152]{2,1,0:T(8,128)(2,1)S(1)}, bf16[4,48,1152]{2,1,0:T(8,128)(2,1)S(1)}, u32[]{:S(2)}, u32[]{:S(2)}) collective-permute-start(bf16[4,48,1152]{2,1,0:T(8,128)(2,1)S(1)} %get-tuple-element.56), channel_id=1, source_target_pairs={{0,1},{1,0},{2,3},{3,2},{8,9},{9,8},{10,11},{11,10},{16,17},{17,16... | collective-permute-start | bytes 1327112 | tf_op jit(solution)/shard_map/ppermute | solution.py:494
  16.4 6.4 %collective-permute-start.2 = (bf16[1,48,1152]{2,1,0:T(8,128)(2,1)S(1)}, bf16[1,48,1152]{2,1,0:T(8,128)(2,1)S(1)}, u32[]{:S(2)}, u32[]{:S(2)}) collective-permute-start(bf16[1,48,1152]{2,1,0:T(8,128)(2,1)S(1)} %get-tuple-element.67), channel_id=1, source_target_pairs={{0,1},{1,0},{2,3},{3,2},{8,9},{9,8},{10,11},{11,10},{16,17},{17,16... | collective-permute-start | bytes 331784 | tf_op jit(solution)/shard_map/ppermute | solution.py:494
  17.2 26.2 %copy-start.2 = (f32[16,13,13]{2,0,1:T(8,128)S(1)}, f32[16,13,13]{2,0,1:T(8,128)}, u32[]{:S(2)}) copy-start(f32[16,13,13]{2,0,1:T(8,128)} %param.23) | copy-start | bytes 32452
  17.2 26.1 %copy-start.4 = (s32[12,96]{1,0:T(8,128)S(1)}, s32[12,96]{1,0:T(8,128)}, u32[]{:S(2)}) copy-start(s32[12,96]{1,0:T(8,128)} %refs_2_.1) | copy-start | bytes 13828
  17.2 26.1 %copy-start.6 = (s32[4,216]{1,0:T(4,128)S(1)}, s32[4,216]{1,0:T(4,128)}, u32[]{:S(2)}) copy-start(s32[4,216]{1,0:T(4,128)} %constant.16.clone.refs_1_) | copy-start | bytes 10372
  17.2 8.6 %collective-permute-start.1 = (bf16[4,24,1152]{2,1,0:T(8,128)(2,1)S(1)}, bf16[4,24,1152]{2,1,0:T(8,128)(2,1)S(1)}, u32[]{:S(2)}, u32[]{:S(2)}) collective-permute-start(bf16[4,24,1152]{2,1,0:T(8,128)(2,1)S(1)} %get-tuple-element.60), channel_id=1, source_target_pairs={{0,2},{1,3},{2,0},{3,1},{8,10},{9,11},{10,8},{11,9},{16,18},{17,19... | collective-permute-start | bytes 663560 | tf_op jit(solution)/shard_map/ppermute | solution.py:494
  22.7 1.4 %collective-permute-start.3 = (bf16[1,48,1152]{2,1,0:T(8,128)(2,1)S(1)}, bf16[1,48,1152]{2,1,0:T(8,128)(2,1)S(1)}, u32[]{:S(2)}, u32[]{:S(2)}) collective-permute-start(bf16[1,48,1152]{2,1,0:T(8,128)(2,1)S(1)} %get-tuple-element.70), channel_id=1, source_target_pairs={{0,1},{1,0},{2,3},{3,2},{8,9},{9,8},{10,11},{11,10},{16,17},{17,16... | collective-permute-start | bytes 331784 | tf_op jit(solution)/shard_map/ppermute | solution.py:494
  26.3 7.3 %collective-permute-start.7 = (bf16[2,24,1152]{2,1,0:T(8,128)(2,1)S(1)}, bf16[2,24,1152]{2,1,0:T(8,128)(2,1)S(1)}, u32[]{:S(2)}, u32[]{:S(2)}) collective-permute-start(bf16[2,24,1152]{2,1,0:T(8,128)(2,1)S(1)} %get-tuple-element.78), channel_id=1, source_target_pairs={{0,2},{1,3},{2,0},{3,1},{8,10},{9,11},{10,8},{11,9},{16,18},{17,19... | collective-permute-start | bytes 331784 | tf_op jit(solution)/shard_map/ppermute | solution.py:494
  28.1 7.9 %collective-permute-start.4 = (bf16[24,1152]{1,0:T(8,128)(2,1)S(1)}, bf16[24,1152]{1,0:T(8,128)(2,1)S(1)}, u32[]{:S(2)}, u32[]{:S(2)}) collective-permute-start(bf16[24,1152]{1,0:T(8,128)(2,1)S(1)} %get-tuple-element.74), channel_id=1, source_target_pairs={{0,8},{1,9},{2,10},{3,11},{8,16},{9,17},{10,18},{11,19},{16,24},{1... | collective-permute-start | bytes 165896 | tf_op jit(solution)/shard_map/ppermute | solution.py:494
  29.7 8.3 %collective-permute-start.5 = (bf16[24,1152]{1,0:T(8,128)(2,1)S(1)}, bf16[24,1152]{1,0:T(8,128)(2,1)S(1)}, u32[]{:S(2)}, u32[]{:S(2)}) collective-permute-start(bf16[24,1152]{1,0:T(8,128)(2,1)S(1)} %get-tuple-element.75), channel_id=1, source_target_pairs={{0,16},{1,17},{2,18},{3,19},{8,24},{9,25},{10,26},{11,27},{16,0},{... | collective-permute-start | bytes 165896 | tf_op jit(solution)/shard_map/ppermute | solution.py:494
  32.3 5.7 %collective-permute-start.6 = (bf16[24,1152]{1,0:T(8,128)(2,1)S(1)}, bf16[24,1152]{1,0:T(8,128)(2,1)S(1)}, u32[]{:S(2)}, u32[]{:S(2)}) collective-permute-start(bf16[24,1152]{1,0:T(8,128)(2,1)S(1)} %get-tuple-element.76), channel_id=1, source_target_pairs={{0,24},{1,25},{2,26},{3,27},{8,0},{9,1},{10,2},{11,3},{16,8},{17,9... | collective-permute-start | bytes 165896 | tf_op jit(solution)/shard_map/ppermute | solution.py:494
  34.0 5.9 %collective-permute-start.8 = (bf16[12,1152]{1,0:T(8,128)(2,1)S(1)}, bf16[12,1152]{1,0:T(8,128)(2,1)S(1)}, u32[]{:S(2)}, u32[]{:S(2)}) collective-permute-start(bf16[12,1152]{1,0:T(8,128)(2,1)S(1)} %get-tuple-element.80), channel_id=1, source_target_pairs={{0,8},{1,9},{2,10},{3,11},{8,16},{9,17},{10,18},{11,19},{16,24},{1... | collective-permute-start | bytes 82952 | tf_op jit(solution)/shard_map/ppermute | solution.py:494
  34.7 5.7 %collective-permute-start.9 = (bf16[12,1152]{1,0:T(8,128)(2,1)S(1)}, bf16[12,1152]{1,0:T(8,128)(2,1)S(1)}, u32[]{:S(2)}, u32[]{:S(2)}) collective-permute-start(bf16[12,1152]{1,0:T(8,128)(2,1)S(1)} %get-tuple-element.81), channel_id=1, source_target_pairs={{0,16},{1,17},{2,18},{3,19},{8,24},{9,25},{10,26},{11,27},{16,0},{... | collective-permute-start | bytes 82952 | tf_op jit(solution)/shard_map/ppermute | solution.py:494
  36.0 4.5 %collective-permute-start.10 = (bf16[12,1152]{1,0:T(8,128)(2,1)S(1)}, bf16[12,1152]{1,0:T(8,128)(2,1)S(1)}, u32[]{:S(2)}, u32[]{:S(2)}) collective-permute-start(bf16[12,1152]{1,0:T(8,128)(2,1)S(1)} %get-tuple-element.82), channel_id=1, source_target_pairs={{0,24},{1,25},{2,26},{3,27},{8,0},{9,1},{10,2},{11,3},{16,8},{17,9... | collective-permute-start | bytes 82952 | tf_op jit(solution)/shard_map/ppermute | solution.py:494
  41.0 6.6 %collective-permute-start.12 = (bf16[36,1024]{1,0:T(8,128)(2,1)S(1)}, bf16[36,1024]{1,0:T(8,128)(2,1)S(1)}, u32[]{:S(2)}, u32[]{:S(2)}) collective-permute-start(bf16[36,1024]{1,0:T(8,128)(2,1)S(1)} %merge.9.refs_0_), channel_id=1, source_target_pairs={{27,0},{2,1},{1,2},{8,3},{31,4},{6,5},{5,6},{12,7},{3,8},{10,9},{9... | collective-permute-start | bytes 221192 | tf_op jit(solution)/shard_map/ppermute | solution.py:582
  41.1 6.5 %collective-permute-start.11 = (bf16[36,1024]{1,0:T(8,128)(2,1)S(1)}, bf16[36,1024]{1,0:T(8,128)(2,1)S(1)}, u32[]{:S(2)}, u32[]{:S(2)}) collective-permute-start(bf16[36,1024]{1,0:T(8,128)(2,1)S(1)} %merge.9.refs_0_), channel_id=1, source_target_pairs={{4,0},{5,1},{6,2},{7,3},{0,4},{1,5},{2,6},{3,7},{12,8},{13,9},{14,... | collective-permute-start | bytes 221192 | tf_op jit(solution)/shard_map/ppermute | solution.py:582
  42.6 6.8 %collective-permute-start.13 = (bf16[36,1024]{1,0:T(8,128)(2,1)S(1)}, bf16[36,1024]{1,0:T(8,128)(2,1)S(1)}, u32[]{:S(2)}, u32[]{:S(2)}) collective-permute-start(bf16[36,1024]{1,0:T(8,128)(2,1)S(1)} %merge.9.refs_0_), channel_id=1, source_target_pairs={{1,0},{0,1},{3,2},{2,3},{5,4},{4,5},{7,6},{6,7},{9,8},{8,9},{11,10... | collective-permute-start | bytes 221192 | tf_op jit(solution)/shard_map/ppermute | solution.py:582
  43.4 5.8 %copy-start = (bf16[1024,1024]{1,0:T(8,128)(2,1)S(1)}, bf16[1024,1024]{1,0:T(8,128)(2,1)}, u32[]{:S(2)}) copy-start(bf16[1024,1024]{1,0:T(8,128)(2,1)} %refs_0_) | copy-start | bytes 6291460
  43.4 5.8 %copy-start.1 = (bf16[1024,1024]{1,0:T(8,128)(2,1)S(1)}, bf16[1024,1024]{1,0:T(8,128)(2,1)}, u32[]{:S(2)}) copy-start(bf16[1024,1024]{1,0:T(8,128)(2,1)} %refs_1_.3) | copy-start | bytes 6291460
  47.6 4.5 %copy-start.5 = (f32[1024]{0:T(1024)S(1)}, f32[1024]{0:T(1024)}, u32[]{:S(2)}) copy-start(f32[1024]{0:T(1024)} %param.18) | copy-start | bytes 12292
  47.6 4.4 %collective-permute-start.15 = (bf16[36,1024]{1,0:T(8,128)(2,1)S(1)}, bf16[36,1024]{1,0:T(8,128)(2,1)S(1)}, u32[]{:S(2)}, u32[]{:S(2)}) collective-permute-start(bf16[36,1024]{1,0:T(8,128)(2,1)S(1)} %collective-permute-done.12.refs_4_), channel_id=1, source_target_pairs={{4,0},{5,1},{6,2},{7,3},{0,4},{1,5},{2,6},{3,7},{12,8},{13,9},{14,... | collective-permute-start | bytes 221192 | tf_op jit(solution)/shard_map/ppermute | solution.py:582
  49.1 2.9 %collective-permute-start.14 = (bf16[36,1024]{1,0:T(8,128)(2,1)S(1)}, bf16[36,1024]{1,0:T(8,128)(2,1)S(1)}, u32[]{:S(2)}, u32[]{:S(2)}) collective-permute-start(bf16[36,1024]{1,0:T(8,128)(2,1)S(1)} %collective-permute-done.11.refs_1_), channel_id=1, source_target_pairs={{1,0},{0,1},{3,2},{2,3},{5,4},{4,5},{7,6},{6,7},{9,8},{8,9},{11,10... | collective-permute-start | bytes 221192 | tf_op jit(solution)/shard_map/ppermute | solution.py:582

commit v6 on v5

--- a/solution.py
+++ b/solution.py
@@ -90,7 +90,7 @@
     return parts.T.astype(BF16)
 
 
-def column_order(block, tile, columns):
+def column_order(block, tile, columns, turned=False):
     shape = (tile, tile)
     target = lax.broadcasted_iota(jnp.int32, shape, 0)
     source = lax.broadcasted_iota(jnp.int32, shape, 1)
@@ -102,7 +102,10 @@
     for radix in RADICES:
         weight //= radix
         bits, low = weight.bit_length() - 1, stride.bit_length() - 1
-        digit = ((group >> bits) + (block >> low)) & (radix - 1)
+        place = (group >> bits) & (radix - 1)
+        if turned and radix == 4:
+            place = jnp.where(place == 0, 0, jnp.where(place == 3, 1, place + 1))
+        digit = (place + (block >> low)) & (radix - 1)
         wanted = wanted + digit * stride
         stride *= radix
     wanted = wanted * columns + target - group * columns
@@ -214,7 +217,7 @@
     block = block_ref[0]
     high = block // TILE_BLOCKS
     tile = rest_ref.shape[2] // tiles
-    order = column_order(block, tile, columns)
+    order = column_order(block, tile, columns, turned=True)
     for step in range(tiles):
         pool_rows(
             heads,
@@ -355,43 +358,67 @@
         copy.wait()
 
 
-def attend_kernel(heads, count, *refs):
-    blocks = refs[:count]
-    gain_ref, bias_ref, w_agg, w_query, w_key, w_value, w_out, out_ref = refs[count : count + 8]
-    window, mix = refs[count + 8 :]
-    width = window.shape[1]
-    scale = 1.0 / math.sqrt(width // heads)
+def project(window, gain_ref, w_agg, w_key, w_value):
+    tokens = dot(window, w_agg[...]).astype(BF16)
+    values = tokens.astype(F32)
+    center = values - jnp.mean(values, axis=-1, keepdims=True)
+    variance = jnp.mean(center * center, axis=-1, keepdims=True)
+    normed = (center * lax.rsqrt(variance + EPS) * gain_ref[...]).astype(BF16)
+    keys = dot(normed, w_key[...]).astype(BF16)
+    values = dot(normed, w_value[...]).astype(BF16)
+    return tokens, normed, keys, values
+
+
+def gather_blocks(blocks, window):
     at = 0
     for block in blocks:
         size = block.shape[0]
         window[at : at + size] = block[...]
         at += size
-    tokens = dot(window[...], w_agg[...]).astype(BF16)
-    values = tokens.astype(F32)
-    center = values - jnp.mean(values, axis=-1, keepdims=True)
-    variance = jnp.mean(center * center, axis=-1, keepdims=True)
-    normed = (center * lax.rsqrt(variance + EPS) * gain_ref[...]).astype(BF16)
-    queries = dot(normed[:QROWS], w_query[...]).astype(BF16)
-    keys = dot(normed, w_key[...]).astype(BF16)
+
+
+def project_kernel(count, *refs):
+    gain_ref, w_agg, w_query, w_key, w_value = refs[count : count + 5]
+    token_ref, query_ref, near_key, near_value, window = refs[count + 5 :]
+    gather_blocks(refs[:count], window)
+    tokens, normed, keys, values = project(window[...], gain_ref, w_agg, w_key, w_value)
+    token_ref[...] = tokens[:QROWS]
+    query_ref[...] = dot(normed[:QROWS], w_query[...]).astype(BF16)
+    near_key[...] = keys
+    near_value[...] = values
+
+
+def attend_kernel(heads, count, *refs):
+    gain_ref, w_agg, w_key, w_value, w_out, bias_ref = refs[count : count + 6]
+    token_ref, query_ref, near_key, near_value, out_ref = refs[count + 6 : count + 11]
+    window, key_ref, value_ref, mix = refs[count + 11 :]
+    width = window.shape[1]
+    scale = 1.0 / math.sqrt(width // heads)
+    near = near_key.shape[0]
+    gather_blocks(refs[:count], window)
+    _, _, keys, values = project(window[...], gain_ref, w_agg, w_key, w_value)
+    key_ref[:near] = near_key[...]
+    key_ref[near:] = keys
+    value_ref[:near] = near_value[...]
+    value_ref[near:] = values
     left = lane_iota((QROWS, LANES)) < LANES // 2
     pairs = [slice(at, at + LANES) for at in range(0, width, LANES)]
     logits = []
     for at in pairs:
-        query = queries[:, at]
+        query = query_ref[:, at]
         zero = jnp.zeros_like(query)
         both = jnp.concatenate([jnp.where(left, query, zero), jnp.where(left, zero, query)], axis=0)
-        logits.append(dot_nt(both, keys[:, at]))
-    values = dot(normed, w_value[...]).astype(BF16)
+        logits.append(dot_nt(both, key_ref[:, at]))
     shares = []
     for pair, logit in enumerate(logits):
         bias = bias_ref[2 * pair : 2 * pair + 2]
         logit = logit * scale + bias.reshape(2 * QROWS, bias.shape[-1])
         raised = jnp.exp(logit - jnp.max(logit, axis=-1, keepdims=True))
         shares.append((raised / jnp.sum(raised, axis=-1, keepdims=True)).astype(BF16))
-    mixed = [dot(share, values[:, at]) for share, at in zip(shares, pairs)]
+    mixed = [dot(share, value_ref[:, at]) for share, at in zip(shares, pairs)]
     for at, rows in zip(pairs, mixed):
         mix[:, at] = jnp.where(left, rows[:QROWS], rows[QROWS:]).astype(BF16)
-    result = tokens[:QROWS].astype(F32) + dot(mix[...], w_out[...])
+    result = token_ref[...].astype(F32) + dot(mix[...], w_out[...])
     rows, columns, _ = out_ref.shape
     for row in range(rows):
         out_ref[row] = result[row * columns : (row + 1) * columns].astype(BF16)
@@ -500,9 +527,12 @@
     if tiles > 1:
         stages.append((TILE_BLOCKS, tiles))
 
-    def swap(sends, number):
+    def swap(sends, number, turned=False):
         stride, radix = stages[number]
-        return [exchange(send, k + 1, stride, radix) for k, send in enumerate(sends)]
+        shifts = range(1, radix)
+        if turned and number < len(RADICES) and radix == 4:
+            shifts = (2, 3, 1)
+        return [exchange(send, shift, stride, radix) for send, shift in zip(sends, shifts)]
 
     def next_split(groups, number, places, size):
         if number + 1 == len(stages):
@@ -530,7 +560,7 @@
     keep_a = parts_a[0]
     keep_b = [[keep_b] + got_b, [keep_c] + got_c]
 
-    places = [(0, 0), (1, 0), (0, 1), (1, 1), (0, -1), (1, -1)]
+    places = [(0, 0), (0, -1), (0, 1), (1, 0), (1, -1), (1, 1)]
     patch = rows * columns
     dl = np.repeat([p[0] for p in places], patch)
     dx = np.repeat([p[1] for p in places], patch)
@@ -549,7 +579,7 @@
             if number == 1:
                 parts_a, parts_b = barrier((parts_a, parts_b))
             keep_a, got_a = parts_a[0], swap(parts_a[1:], number + 1)
-        keep_b = [[parts_b[0]] + swap(parts_b[1:], number)]
+        keep_b = [[parts_b[0]] + swap(parts_b[1:], number, True)]
     (pooled,) = next_split([group_a] + keep_b, len(stages) - 1, 0, columns)
 
     staged = (agg_out, nb_query, nb_key)
@@ -581,13 +611,14 @@
             pairs.append((((b // n_lon) * n_lat + l) * n_lon + b % n_lon, i))
         return lax.ppermute(array, ("var", "lat", "lon"), pairs)
 
+    far = partner(pooled, "odd")
     across = partner(pooled, "lat")
     near = partner(pooled, "core")
-    far = partner(pooled, "odd")
-    across, far, bias = barrier((across, far, bias))
-    window = [pooled, across, near, partner(across, "core"), far, partner(far, "lat")]
+    far, across, bias = barrier((far, across, bias))
+    window = [pooled, far, near, across]
+    far_late = partner(far, "lat")
     last = (nb_value, nb_out)
-    last, _ = barrier((last, across))
+    last, _ = barrier((last, far))
     last = pl.pallas_call(
         functools.partial(load_kernel, len(last)),
         in_specs=[hbm] * len(last),
@@ -601,18 +632,40 @@
         name="load",
     )(*last)
 
+    gain = norm_gain.reshape(1, width)
+    w_agg, w_query, w_key = staged
+    across, last = barrier((across, last))
+    w_value, w_out = last
+    late = [far_late, partner(across, "core")]
+    early = len(window) * patch
+    tall = jax.ShapeDtypeStruct((QROWS, width), BF16)
+    side = jax.ShapeDtypeStruct((early, width), BF16)
+    projected = pl.pallas_call(
+        functools.partial(project_kernel, len(window)),
+        in_specs=[vmem] * (len(window) + 5),
+        out_specs=[vmem] * 4,
+        out_shape=[tall, tall, side, side],
+        scratch_shapes=[pltpu.VMEM((early, width), BF16)],
+        compiler_params=pltpu.CompilerParams(vmem_limit_bytes=MERGE_VMEM),
+        cost_estimate=pl.CostEstimate(
+            flops=6 * early * width * width, bytes_accessed=8 * width * width, transcendentals=0
+        ),
+        name="project",
+    )(*window, gain, w_agg, w_query, w_key, w_value)
     return pl.pallas_call(
-        functools.partial(attend_kernel, heads, len(window)),
-        in_specs=[vmem] * (len(window) + 7),
+        functools.partial(attend_kernel, heads, len(late)),
+        in_specs=[vmem] * (len(late) + 10),
         out_specs=vmem,
         out_shape=jax.ShapeDtypeStruct((rows, columns, width), BF16),
         scratch_shapes=[
+            pltpu.VMEM((keys - early, width), BF16),
+            pltpu.VMEM((keys, width), BF16),
             pltpu.VMEM((keys, width), BF16),
             pltpu.VMEM((QROWS, width), BF16),
         ],
         compiler_params=pltpu.CompilerParams(vmem_limit_bytes=MERGE_VMEM),
         name="attend",
-    )(*window, norm_gain.reshape(1, width), bias, *staged, *last)
+    )(*late, gain, w_agg, w_key, w_value, w_out, bias, *projected)
 
 
 def solution(mesh):

time: 56.1 us -> 55.3 us (0.986)
  waiting for transfers between devices: 8.18 us -> 6.33 us
  Pallas kernels: 27.9 us -> 28.9 us
    ppermute x5, waiting for transfers between devices: 3.12 us -> 1.26 us  [partner(): return lax.ppermute(array, ('var', 'lat', 'lon'), pairs)]
    pallas_call x1 -> x2, Pallas kernels: 3.78 us -> 4.8 us  [the longest x1 3.05 us: on_device(): pl.pallas_call(functools.partial(attend_kernel, heads, len(late)), in_spe...]
  transfers between devices with their start and end apart: 16 -> 16, of which waited for: 6 -> 6; matrix products, arithmetic and copies ran while one was open for 0% -> 0% of each run, Pallas kernels for 19% -> 22%
where the time goes in v6:
time: 55.3 us; the launch traced here: 55.1 us
  Pallas kernels  28.9 us (52%)
  starting transfers between devices  18.9 us (34%)
  waiting for transfers between devices  6.33 us (11%)
  local copies, waits for them, and re-layouts  0.73 us (1%)
    ppermute x11, starting transfers between devices, exchange(): lax.ppermute(array, ('var', 'lon'), [(i, moved(i)) for i in range(devices)])  14.9 us
    pallas_call x1, Pallas kernels, lead_pool(): pl.pallas_call(functools.partial(lead_kernel, heads, head_dim, lead_rows,...  10 us
    ppermute x11, waiting for transfers between devices, exchange(): lax.ppermute(array, ('var', 'lon'), [(i, moved(i)) for i in range(devices)])  5.07 us
    pallas_call x2, Pallas kernels, pool(): pl.pallas_call(functools.partial(pool_kernel, heads, head_dim, row, tiles...  4.91 us
    ppermute x5, starting transfers between devices, partner(): return lax.ppermute(array, ('var', 'lat', 'lon'), pairs)  3.97 us
    pallas_call x1, Pallas kernels, on_device(): pl.pallas_call(functools.partial(stage_kernel, rows, columns, len(staged)...  3.7 us
    pallas_call x1, Pallas kernels, on_device(): pl.pallas_call(functools.partial(attend_kernel, heads, len(late)), in_spe...  3.05 us
    pallas_call x1, Pallas kernels, lead_pool(): pl.pallas_call(functools.partial(pre_kernel, heads, head_dim), in_specs=[...  2.74 us
  transfers between devices with their start and end apart: 16, of which 6 were waited for; matrix products, arithmetic and copies ran while one was open for 0% of the time, Pallas kernels for 22%

profile of v6, /device:TPU:0, one launch (start us, length us, event | category | flops | bytes accessed | tf_op | source)
XLA Modules:
  0.0 55.1 jit_solution(12702038665261983866)
XLA Ops:
  0.0 0.0 copy-start.4
  0.0 0.7 %copy-done.4 = f32[16,64]{1,0:T(8,128)S(1)} copy-done((f32[16,64]{1,0:T(8,128)S(1)}, f32[16,64]{1,0:T(8,128)}, u32[]{:S(2)}) %copy-start.4) | copy-done | bytes 4120
  0.7 2.7 %pre.1 = (bf16[1024,128]{1,0:T(8,128)(2,1)S(1)}, bf16[1024,1024]{1,0:T(8,128)(2,1)S(1)}, bf16[8,96,1024]{2,1,0:T(8,128)(2,1)S(1)}) custom-call(bf16[8,6,96,1024]{3,2,1,0:T(8,128)(2,1)} %refs_1_.2, bf16[1024,1024]{1,0:T(8,128)(2,1)} %value_ref.1, f32[16,64]{1,0:T(8,128)S(1)} %copy-done.4, bf16[1024,1024]{1,0:T(8,128)(2,1)} %key_ref.1), custom_call_target="tpu_custom_call" | custom-call | tf_op jit(solution)/shard_map/pre/pallas_call | solution.py:474
  3.4 10.0 %lead.1 = (bf16[4,48,1152]{2,1,0:T(8,128)(2,1)S(1)}, bf16[4,48,1152]{2,1,0:T(8,128)(2,1)S(1)}, bf16[8,2,96,1024]{3,2,1,0:T(8,128)(2,1)S(1)}) custom-call(s32[1]{0:T(128)} %bitcast.refs_0_, bf16[8,6,96,1024]{3,2,1,0:T(8,128)(2,1)} %refs_1_.2, bf16[8,96,1024]{2,1,0:T(8,128)(2,1)S(1)} %get-tuple-element.59.refs_2_, ...), custom_call_target="tpu_custom_call" | custom-call | flops 9663676416 | bytes 6291456 | tf_op jit(solution)/shard_map/lead/pallas_call | solution.py:489
  13.4 0.5 collective-permute-start
  14.0 2.5 %pool.2 = (bf16[1,48,1152]{2,1,0:T(8,128)(2,1)S(1)}, bf16[1,48,1152]{2,1,0:T(8,128)(2,1)S(1)}) custom-call(s32[1]{0:T(128)} %bitcast.refs_0_, bf16[8,2,96,1024]{3,2,1,0:T(8,128)(2,1)S(1)} %get-tuple-element.72.refs_1_, bf16[1024,1024]{1,0:T(8,128)(2,1)S(1)} %get-tuple-element.60.refs_3_.refs_2_, bf16[1024,128]{1,0:T(8,128)(2,1)S(1)} %get-tuple-element.75.refs_4_.refs_3_), custom_call_target="tpu_custom_call" | custom-call | flops 2415919104 | bytes 1572864 | tf_op jit(solution)/shard_map/pool/pallas_call | solution.py:506
  16.4 0.1 collective-permute-start.2
  16.6 0.0 collective-permute-done.refs_1_
  16.6 0.7 %merge.5 = (bf16[4,24,1152]{2,1,0:T(8,128)(2,1)S(1)}, bf16[4,24,1152]{2,1,0:T(8,128)(2,1)S(1)}) custom-call(bf16[4,48,1152]{2,1,0:T(8,128)(2,1)S(1)} %get-tuple-element.62.refs_0_, bf16[4,48,1152]{2,1,0:T(8,128)(2,1)S(1)} %collective-permute-done.refs_1_), custom_call_target="tpu_custom_call" | custom-call | flops 100663296 | bytes 1572864 | tf_op jit(solution)/shard_map/merge/pallas_call | solution.py:290
  17.2 0.0 copy-start.2
  17.2 0.0 copy-start.5
  17.2 0.0 copy-start.6
  17.2 3.0 %collective-permute-start.1 = (bf16[4,24,1152]{2,1,0:T(8,128)(2,1)S(1)}, bf16[4,24,1152]{2,1,0:T(8,128)(2,1)S(1)}, u32[]{:S(2)}, u32[]{:S(2)}) collective-permute-start(bf16[4,24,1152]{2,1,0:T(8,128)(2,1)S(1)} %get-tuple-element.67), channel_id=1, source_target_pairs={{0,2},{1,3},{2,0},{3,1},{8,10},{9,11},{10,8},{11,9},{16,18},{17,19... | collective-permute-start | bytes 663560 | tf_op jit(solution)/shard_map/ppermute | solution.py:521
  20.3 2.5 %pool.3 = (bf16[1,48,1152]{2,1,0:T(8,128)(2,1)S(1)}, bf16[1,48,1152]{2,1,0:T(8,128)(2,1)S(1)}) custom-call(s32[1]{0:T(128)} %bitcast.refs_0_, bf16[8,2,96,1024]{3,2,1,0:T(8,128)(2,1)S(1)} %get-tuple-element.72.refs_1_, bf16[1024,1024]{1,0:T(8,128)(2,1)S(1)} %get-tuple-element.60.refs_3_.refs_2_, bf16[1024,128]{1,0:T(8,128)(2,1)S(1)} %get-tuple-element.75.refs_4_.refs_3_), custom_call_target="tpu_custom_call" | custom-call | flops 2415919104 | bytes 1572864 | tf_op jit(solution)/shard_map/pool/pallas_call | solution.py:506
  22.7 0.1 collective-permute-start.3
  22.8 0.0 collective-permute-done.2.refs_1_
  22.8 1.3 %collective-permute-done.3.refs_3_ = bf16[1,48,1152]{2,1,0:T(8,128)(2,1)S(1)} collective-permute-done((bf16[1,48,1152]{2,1,0:T(8,128)(2,1)S(1)}, bf16[1,48,1152]{2,1,0:T(8,128)(2,1)S(1)}, u32[]{:S(2)}, u32[]{:S(2)}) %collective-permute-start.3) | collective-permute-done | bytes 110624 | tf_op jit(solution)/shard_map/ppermute | solution.py:521
  24.1 0.5 merge.7
  24.6 1.3 %collective-permute-done.1.refs_1_ = bf16[4,24,1152]{2,1,0:T(8,128)(2,1)S(1)} collective-permute-done((bf16[4,24,1152]{2,1,0:T(8,128)(2,1)S(1)}, bf16[4,24,1152]{2,1,0:T(8,128)(2,1)S(1)}, u32[]{:S(2)}, u32[]{:S(2)}) %collective-permute-start.1) | collective-permute-done | bytes 221216 | tf_op jit(solution)/shard_map/ppermute | solution.py:521
  25.9 0.4 merge.6
  26.3 1.8 %collective-permute-start.7 = (bf16[2,24,1152]{2,1,0:T(8,128)(2,1)S(1)}, bf16[2,24,1152]{2,1,0:T(8,128)(2,1)S(1)}, u32[]{:S(2)}, u32[]{:S(2)}) collective-permute-start(bf16[2,24,1152]{2,1,0:T(8,128)(2,1)S(1)} %get-tuple-element.85), channel_id=1, source_target_pairs={{0,2},{1,3},{2,0},{3,1},{8,10},{9,11},{10,8},{11,9},{16,18},{17,19... | collective-permute-start | bytes 331784 | tf_op jit(solution)/shard_map/ppermute | solution.py:521
  28.1 1.6 %collective-permute-start.4 = (bf16[24,1152]{1,0:T(8,128)(2,1)S(1)}, bf16[24,1152]{1,0:T(8,128)(2,1)S(1)}, u32[]{:S(2)}, u32[]{:S(2)}) collective-permute-start(bf16[24,1152]{1,0:T(8,128)(2,1)S(1)} %get-tuple-element.81), channel_id=1, source_target_pairs={{0,8},{1,9},{2,10},{3,11},{8,16},{9,17},{10,18},{11,19},{16,24},{1... | collective-permute-start | bytes 165896 | tf_op jit(solution)/shard_map/ppermute | solution.py:521
  29.7 2.6 %collective-permute-start.5 = (bf16[24,1152]{1,0:T(8,128)(2,1)S(1)}, bf16[24,1152]{1,0:T(8,128)(2,1)S(1)}, u32[]{:S(2)}, u32[]{:S(2)}) collective-permute-start(bf16[24,1152]{1,0:T(8,128)(2,1)S(1)} %get-tuple-element.82), channel_id=1, source_target_pairs={{0,16},{1,17},{2,18},{3,19},{8,24},{9,25},{10,26},{11,27},{16,0},{... | collective-permute-start | bytes 165896 | tf_op jit(solution)/shard_map/ppermute | solution.py:521
  32.3 1.3 %collective-permute-start.6 = (bf16[24,1152]{1,0:T(8,128)(2,1)S(1)}, bf16[24,1152]{1,0:T(8,128)(2,1)S(1)}, u32[]{:S(2)}, u32[]{:S(2)}) collective-permute-start(bf16[24,1152]{1,0:T(8,128)(2,1)S(1)} %get-tuple-element.83), channel_id=1, source_target_pairs={{0,24},{1,25},{2,26},{3,27},{8,0},{9,1},{10,2},{11,3},{16,8},{17,9... | collective-permute-start | bytes 165896 | tf_op jit(solution)/shard_map/ppermute | solution.py:521
  33.6 0.0 collective-permute-done.7.refs_1_
  33.6 0.4 merge.8
  34.0 0.7 %collective-permute-start.10 = (bf16[12,1152]{1,0:T(8,128)(2,1)S(1)}, bf16[12,1152]{1,0:T(8,128)(2,1)S(1)}, u32[]{:S(2)}, u32[]{:S(2)}) collective-permute-start(bf16[12,1152]{1,0:T(8,128)(2,1)S(1)} %get-tuple-element.89), channel_id=1, source_target_pairs={{0,8},{1,9},{2,10},{3,11},{8,16},{9,17},{10,18},{11,19},{16,24},{1... | collective-permute-start | bytes 82952 | tf_op jit(solution)/shard_map/ppermute | solution.py:521
  34.7 1.2 %collective-permute-start.8 = (bf16[12,1152]{1,0:T(8,128)(2,1)S(1)}, bf16[12,1152]{1,0:T(8,128)(2,1)S(1)}, u32[]{:S(2)}, u32[]{:S(2)}) collective-permute-start(bf16[12,1152]{1,0:T(8,128)(2,1)S(1)} %get-tuple-element.87), channel_id=1, source_target_pairs={{0,16},{1,17},{2,18},{3,19},{8,24},{9,25},{10,26},{11,27},{16,0},{... | collective-permute-start | bytes 82952 | tf_op jit(solution)/shard_map/ppermute | solution.py:521
  36.0 0.0 collective-permute-done.4.refs_1_
  36.0 1.9 %collective-permute-start.9 = (bf16[12,1152]{1,0:T(8,128)(2,1)S(1)}, bf16[12,1152]{1,0:T(8,128)(2,1)S(1)}, u32[]{:S(2)}, u32[]{:S(2)}) collective-permute-start(bf16[12,1152]{1,0:T(8,128)(2,1)S(1)} %get-tuple-element.88), channel_id=1, source_target_pairs={{0,24},{1,25},{2,26},{3,27},{8,0},{9,1},{10,2},{11,3},{16,8},{17,9... | collective-permute-start | bytes 82952 | tf_op jit(solution)/shard_map/ppermute | solution.py:521
  37.9 0.1 pad_add_fusion.refs_0_
  38.0 0.0 collective-permute-done.5.refs_2_
  38.0 0.0 collective-permute-done.6.refs_3_
  38.0 1.9 %collective-permute-done.10.refs_7_ = bf16[12,1152]{1,0:T(8,128)(2,1)S(1)} collective-permute-done((bf16[12,1152]{1,0:T(8,128)(2,1)S(1)}, bf16[12,1152]{1,0:T(8,128)(2,1)S(1)}, u32[]{:S(2)}, u32[]{:S(2)}) %collective-permute-start.10) | collective-permute-done | bytes 27680 | tf_op jit(solution)/shard_map/ppermute | solution.py:521
  39.9 0.5 collective-permute-done.8.refs_5_
  40.5 0.0 collective-permute-done.9.refs_6_
  40.5 0.5 merge.9.refs_0_
  41.0 0.1 collective-permute-start.11
  41.1 1.6 %collective-permute-start.12 = (bf16[36,1024]{1,0:T(8,128)(2,1)S(1)}, bf16[36,1024]{1,0:T(8,128)(2,1)S(1)}, u32[]{:S(2)}, u32[]{:S(2)}) collective-permute-start(bf16[36,1024]{1,0:T(8,128)(2,1)S(1)} %merge.9.refs_0_), channel_id=1, source_target_pairs={{4,0},{5,1},{6,2},{7,3},{0,4},{1,5},{2,6},{3,7},{12,8},{13,9},{14,... | collective-permute-start | bytes 221192 | tf_op jit(solution)/shard_map/ppermute | solution.py:612
  42.7 0.7 %collective-permute-start.15 = (bf16[36,1024]{1,0:T(8,128)(2,1)S(1)}, bf16[36,1024]{1,0:T(8,128)(2,1)S(1)}, u32[]{:S(2)}, u32[]{:S(2)}) collective-permute-start(bf16[36,1024]{1,0:T(8,128)(2,1)S(1)} %merge.9.refs_0_), channel_id=1, source_target_pairs={{1,0},{0,1},{3,2},{2,3},{5,4},{4,5},{7,6},{6,7},{9,8},{8,9},{11,10... | collective-permute-start | bytes 221192 | tf_op jit(solution)/shard_map/ppermute | solution.py:612
  43.4 0.0 copy-done.2
  43.4 0.0 copy-done.5
  43.4 0.0 copy-done.6
  43.4 0.0 copy-start
  43.4 0.0 copy-start.1
  43.4 3.7 %stage.1 = (f32[16,48,216]{2,1,0:T(8,128)S(1)}, bf16[1024,1024]{1,0:T(8,128)(2,1)S(1)}, bf16[1024,1024]{1,0:T(8,128)(2,1)S(1)}, bf16[1024,1024]{1,0:T(8,128)(2,1)S(1)}) custom-call(s32[2]{0:T(128)S(1)} %pad_add_fusion.refs_0_, s32[4,216]{1,0:T(4,128)S(1)} %copy-done.6, s32[12,96]{1,0:T(8,128)S(1)} %copy-done.5, f32[13,16,13]{2,1,0:T(8,128)S(1)} %bitcast.4, ...), custom_call_target="tpu_custom_call" | custom-call | flops 1000 | bytes 10485760 | tf_op jit(solution)/shard_map/stage/pallas_call | solution.py:587
  47.1 0.5 collective-permute-done.11.refs_1_
  47.6 0.0 collective-permute-done.12.refs_3_
  47.6 0.0 copy-start.3
  47.6 1.5 %collective-permute-start.13 = (bf16[36,1024]{1,0:T(8,128)(2,1)S(1)}, bf16[36,1024]{1,0:T(8,128)(2,1)S(1)}, u32[]{:S(2)}, u32[]{:S(2)}) collective-permute-start(bf16[36,1024]{1,0:T(8,128)(2,1)S(1)} %collective-permute-done.11.refs_1_), channel_id=1, source_target_pairs={{4,0},{5,1},{6,2},{7,3},{0,4},{1,5},{2,6},{3,7},{12,8},{13,9},{14,... | collective-permute-start | bytes 221192 | tf_op jit(solution)/shard_map/ppermute | solution.py:612
  49.1 0.0 copy-done
  49.1 0.0 copy-done.1
  49.2 0.3 load.1
  49.5 0.1 collective-permute-start.14
  49.5 0.0 collective-permute-done.15.refs_2_
  49.6 0.0 copy-done.3
  49.6 1.7 %project.1 = (bf16[48,1024]{1,0:T(8,128)(2,1)S(1)}, bf16[48,1024]{1,0:T(8,128)(2,1)S(1)}, bf16[144,1024]{1,0:T(8,128)(2,1)S(1)}, bf16[144,1024]{1,0:T(8,128)(2,1)S(1)}) custom-call(bf16[36,1024]{1,0:T(8,128)(2,1)S(1)} %merge.9.refs_0_, bf16[36,1024]{1,0:T(8,128)(2,1)S(1)} %collective-permute-done.11.refs_1_, ...), custom_call_target="tpu_custom_call" | custom-call | flops 905969664 | bytes 8388608 | tf_op jit(solution)/shard_map/project/pallas_call | solution.py:643
  51.3 0.0 collective-permute-done.14.refs_1_
  51.3 0.7 %collective-permute-done.13.refs_0_ = bf16[36,1024]{1,0:T(8,128)(2,1)S(1)} collective-permute-done((bf16[36,1024]{1,0:T(8,128)(2,1)S(1)}, bf16[36,1024]{1,0:T(8,128)(2,1)S(1)}, u32[]{:S(2)}, u32[]{:S(2)}) %collective-permute-start.13) | collective-permute-done | bytes 73760 | tf_op jit(solution)/shard_map/ppermute | solution.py:612
  52.1 3.1 %attend.1 = bf16[6,6,1024]{2,1,0:T(8,128)(2,1)} custom-call(bf16[36,1024]{1,0:T(8,128)(2,1)S(1)} %collective-permute-done.13.refs_0_, bf16[36,1024]{1,0:T(8,128)(2,1)S(1)} %collective-permute-done.14.refs_1_, f32[1,1024]{1,0:T(1,128)S(1)} %bitcast.6, bf16[1024,1024]{1,0:T(8,128)(2,1)S(1)} %get-tuple-element.103.refs_5_.refs_3_, ...), custom_call_target="tpu_custom_call" | custom-call | tf_op jit(solution)/shard_map/attend/pallas_call | solution.py:655
Async XLA Ops:
  0.0 0.7 %copy-start.4 = (f32[16,64]{1,0:T(8,128)S(1)}, f32[16,64]{1,0:T(8,128)}, u32[]{:S(2)}) copy-start(f32[16,64]{1,0:T(8,128)} %query_ref.1) | copy-start | bytes 12292
  13.4 3.1 %collective-permute-start = (bf16[4,48,1152]{2,1,0:T(8,128)(2,1)S(1)}, bf16[4,48,1152]{2,1,0:T(8,128)(2,1)S(1)}, u32[]{:S(2)}, u32[]{:S(2)}) collective-permute-start(bf16[4,48,1152]{2,1,0:T(8,128)(2,1)S(1)} %get-tuple-element.63), channel_id=1, source_target_pairs={{0,1},{1,0},{2,3},{3,2},{8,9},{9,8},{10,11},{11,10},{16,17},{17,16... | collective-permute-start | bytes 1327112 | tf_op jit(solution)/shard_map/ppermute | solution.py:521
  16.4 6.4 %collective-permute-start.2 = (bf16[1,48,1152]{2,1,0:T(8,128)(2,1)S(1)}, bf16[1,48,1152]{2,1,0:T(8,128)(2,1)S(1)}, u32[]{:S(2)}, u32[]{:S(2)}) collective-permute-start(bf16[1,48,1152]{2,1,0:T(8,128)(2,1)S(1)} %get-tuple-element.74), channel_id=1, source_target_pairs={{0,1},{1,0},{2,3},{3,2},{8,9},{9,8},{10,11},{11,10},{16,17},{17,16... | collective-permute-start | bytes 331784 | tf_op jit(solution)/shard_map/ppermute | solution.py:521
  17.2 26.2 %copy-start.2 = (f32[16,13,13]{2,0,1:T(8,128)S(1)}, f32[16,13,13]{2,0,1:T(8,128)}, u32[]{:S(2)}) copy-start(f32[16,13,13]{2,0,1:T(8,128)} %param.23) | copy-start | bytes 32452
  17.2 26.2 %copy-start.5 = (s32[12,96]{1,0:T(8,128)S(1)}, s32[12,96]{1,0:T(8,128)}, u32[]{:S(2)}) copy-start(s32[12,96]{1,0:T(8,128)} %refs_2_.1) | copy-start | bytes 13828
  17.2 26.1 %copy-start.6 = (s32[4,216]{1,0:T(4,128)S(1)}, s32[4,216]{1,0:T(4,128)}, u32[]{:S(2)}) copy-start(s32[4,216]{1,0:T(4,128)} %constant.16.clone.refs_1_) | copy-start | bytes 10372
  17.2 8.6 %collective-permute-start.1 = (bf16[4,24,1152]{2,1,0:T(8,128)(2,1)S(1)}, bf16[4,24,1152]{2,1,0:T(8,128)(2,1)S(1)}, u32[]{:S(2)}, u32[]{:S(2)}) collective-permute-start(bf16[4,24,1152]{2,1,0:T(8,128)(2,1)S(1)} %get-tuple-element.67), channel_id=1, source_target_pairs={{0,2},{1,3},{2,0},{3,1},{8,10},{9,11},{10,8},{11,9},{16,18},{17,19... | collective-permute-start | bytes 663560 | tf_op jit(solution)/shard_map/ppermute | solution.py:521
  22.7 1.4 %collective-permute-start.3 = (bf16[1,48,1152]{2,1,0:T(8,128)(2,1)S(1)}, bf16[1,48,1152]{2,1,0:T(8,128)(2,1)S(1)}, u32[]{:S(2)}, u32[]{:S(2)}) collective-permute-start(bf16[1,48,1152]{2,1,0:T(8,128)(2,1)S(1)} %get-tuple-element.77), channel_id=1, source_target_pairs={{0,1},{1,0},{2,3},{3,2},{8,9},{9,8},{10,11},{11,10},{16,17},{17,16... | collective-permute-start | bytes 331784 | tf_op jit(solution)/shard_map/ppermute | solution.py:521
  26.3 7.3 %collective-permute-start.7 = (bf16[2,24,1152]{2,1,0:T(8,128)(2,1)S(1)}, bf16[2,24,1152]{2,1,0:T(8,128)(2,1)S(1)}, u32[]{:S(2)}, u32[]{:S(2)}) collective-permute-start(bf16[2,24,1152]{2,1,0:T(8,128)(2,1)S(1)} %get-tuple-element.85), channel_id=1, source_target_pairs={{0,2},{1,3},{2,0},{3,1},{8,10},{9,11},{10,8},{11,9},{16,18},{17,19... | collective-permute-start | bytes 331784 | tf_op jit(solution)/shard_map/ppermute | solution.py:521
  28.1 7.9 %collective-permute-start.4 = (bf16[24,1152]{1,0:T(8,128)(2,1)S(1)}, bf16[24,1152]{1,0:T(8,128)(2,1)S(1)}, u32[]{:S(2)}, u32[]{:S(2)}) collective-permute-start(bf16[24,1152]{1,0:T(8,128)(2,1)S(1)} %get-tuple-element.81), channel_id=1, source_target_pairs={{0,8},{1,9},{2,10},{3,11},{8,16},{9,17},{10,18},{11,19},{16,24},{1... | collective-permute-start | bytes 165896 | tf_op jit(solution)/shard_map/ppermute | solution.py:521
  29.7 8.3 %collective-permute-start.5 = (bf16[24,1152]{1,0:T(8,128)(2,1)S(1)}, bf16[24,1152]{1,0:T(8,128)(2,1)S(1)}, u32[]{:S(2)}, u32[]{:S(2)}) collective-permute-start(bf16[24,1152]{1,0:T(8,128)(2,1)S(1)} %get-tuple-element.82), channel_id=1, source_target_pairs={{0,16},{1,17},{2,18},{3,19},{8,24},{9,25},{10,26},{11,27},{16,0},{... | collective-permute-start | bytes 165896 | tf_op jit(solution)/shard_map/ppermute | solution.py:521
  32.3 5.7 %collective-permute-start.6 = (bf16[24,1152]{1,0:T(8,128)(2,1)S(1)}, bf16[24,1152]{1,0:T(8,128)(2,1)S(1)}, u32[]{:S(2)}, u32[]{:S(2)}) collective-permute-start(bf16[24,1152]{1,0:T(8,128)(2,1)S(1)} %get-tuple-element.83), channel_id=1, source_target_pairs={{0,24},{1,25},{2,26},{3,27},{8,0},{9,1},{10,2},{11,3},{16,8},{17,9... | collective-permute-start | bytes 165896 | tf_op jit(solution)/shard_map/ppermute | solution.py:521
  34.0 5.9 %collective-permute-start.10 = (bf16[12,1152]{1,0:T(8,128)(2,1)S(1)}, bf16[12,1152]{1,0:T(8,128)(2,1)S(1)}, u32[]{:S(2)}, u32[]{:S(2)}) collective-permute-start(bf16[12,1152]{1,0:T(8,128)(2,1)S(1)} %get-tuple-element.89), channel_id=1, source_target_pairs={{0,8},{1,9},{2,10},{3,11},{8,16},{9,17},{10,18},{11,19},{16,24},{1... | collective-permute-start | bytes 82952 | tf_op jit(solution)/shard_map/ppermute | solution.py:521
  34.7 5.7 %collective-permute-start.8 = (bf16[12,1152]{1,0:T(8,128)(2,1)S(1)}, bf16[12,1152]{1,0:T(8,128)(2,1)S(1)}, u32[]{:S(2)}, u32[]{:S(2)}) collective-permute-start(bf16[12,1152]{1,0:T(8,128)(2,1)S(1)} %get-tuple-element.87), channel_id=1, source_target_pairs={{0,16},{1,17},{2,18},{3,19},{8,24},{9,25},{10,26},{11,27},{16,0},{... | collective-permute-start | bytes 82952 | tf_op jit(solution)/shard_map/ppermute | solution.py:521
  36.0 4.5 %collective-permute-start.9 = (bf16[12,1152]{1,0:T(8,128)(2,1)S(1)}, bf16[12,1152]{1,0:T(8,128)(2,1)S(1)}, u32[]{:S(2)}, u32[]{:S(2)}) collective-permute-start(bf16[12,1152]{1,0:T(8,128)(2,1)S(1)} %get-tuple-element.88), channel_id=1, source_target_pairs={{0,24},{1,25},{2,26},{3,27},{8,0},{9,1},{10,2},{11,3},{16,8},{17,9... | collective-permute-start | bytes 82952 | tf_op jit(solution)/shard_map/ppermute | solution.py:521
  41.0 6.6 %collective-permute-start.11 = (bf16[36,1024]{1,0:T(8,128)(2,1)S(1)}, bf16[36,1024]{1,0:T(8,128)(2,1)S(1)}, u32[]{:S(2)}, u32[]{:S(2)}) collective-permute-start(bf16[36,1024]{1,0:T(8,128)(2,1)S(1)} %merge.9.refs_0_), channel_id=1, source_target_pairs={{27,0},{2,1},{1,2},{8,3},{31,4},{6,5},{5,6},{12,7},{3,8},{10,9},{9... | collective-permute-start | bytes 221192 | tf_op jit(solution)/shard_map/ppermute | solution.py:612
  41.1 6.5 %collective-permute-start.12 = (bf16[36,1024]{1,0:T(8,128)(2,1)S(1)}, bf16[36,1024]{1,0:T(8,128)(2,1)S(1)}, u32[]{:S(2)}, u32[]{:S(2)}) collective-permute-start(bf16[36,1024]{1,0:T(8,128)(2,1)S(1)} %merge.9.refs_0_), channel_id=1, source_target_pairs={{4,0},{5,1},{6,2},{7,3},{0,4},{1,5},{2,6},{3,7},{12,8},{13,9},{14,... | collective-permute-start | bytes 221192 | tf_op jit(solution)/shard_map/ppermute | solution.py:612
  42.7 6.9 %collective-permute-start.15 = (bf16[36,1024]{1,0:T(8,128)(2,1)S(1)}, bf16[36,1024]{1,0:T(8,128)(2,1)S(1)}, u32[]{:S(2)}, u32[]{:S(2)}) collective-permute-start(bf16[36,1024]{1,0:T(8,128)(2,1)S(1)} %merge.9.refs_0_), channel_id=1, source_target_pairs={{1,0},{0,1},{3,2},{2,3},{5,4},{4,5},{7,6},{6,7},{9,8},{8,9},{11,10... | collective-permute-start | bytes 221192 | tf_op jit(solution)/shard_map/ppermute | solution.py:612
  43.4 5.8 %copy-start = (bf16[1024,1024]{1,0:T(8,128)(2,1)S(1)}, bf16[1024,1024]{1,0:T(8,128)(2,1)}, u32[]{:S(2)}) copy-start(bf16[1024,1024]{1,0:T(8,128)(2,1)} %refs_0_) | copy-start | bytes 6291460
  43.4 5.8 %copy-start.1 = (bf16[1024,1024]{1,0:T(8,128)(2,1)S(1)}, bf16[1024,1024]{1,0:T(8,128)(2,1)}, u32[]{:S(2)}) copy-start(bf16[1024,1024]{1,0:T(8,128)(2,1)} %refs_1_.3) | copy-start | bytes 6291460
  47.6 1.9 %copy-start.3 = (f32[1024]{0:T(1024)S(1)}, f32[1024]{0:T(1024)}, u32[]{:S(2)}) copy-start(f32[1024]{0:T(1024)} %param.18) | copy-start | bytes 12292
  47.6 4.4 %collective-permute-start.13 = (bf16[36,1024]{1,0:T(8,128)(2,1)S(1)}, bf16[36,1024]{1,0:T(8,128)(2,1)S(1)}, u32[]{:S(2)}, u32[]{:S(2)}) collective-permute-start(bf16[36,1024]{1,0:T(8,128)(2,1)S(1)} %collective-permute-done.11.refs_1_), channel_id=1, source_target_pairs={{4,0},{5,1},{6,2},{7,3},{0,4},{1,5},{2,6},{3,7},{12,8},{13,9},{14,... | collective-permute-start | bytes 221192 | tf_op jit(solution)/shard_map/ppermute | solution.py:612
  49.5 1.9 %collective-permute-start.14 = (bf16[36,1024]{1,0:T(8,128)(2,1)S(1)}, bf16[36,1024]{1,0:T(8,128)(2,1)S(1)}, u32[]{:S(2)}, u32[]{:S(2)}) collective-permute-start(bf16[36,1024]{1,0:T(8,128)(2,1)S(1)} %collective-permute-done.12.refs_3_), channel_id=1, source_target_pairs={{1,0},{0,1},{3,2},{2,3},{5,4},{4,5},{7,6},{6,7},{9,8},{8,9},{11,10... | collective-permute-start | bytes 221192 | tf_op jit(solution)/shard_map/ppermute | solution.py:612

commit v7 on v6

--- a/solution.py
+++ b/solution.py
@@ -20,8 +20,8 @@
 LEAD_VMEM = 40 * MIB
 POOL_VMEM = 30 * MIB
 MERGE_VMEM = 12 * MIB
-STAGE_VMEM = 47 * MIB
-LOAD_VMEM = 42 * MIB
+STAGE_VMEM = 49 * MIB
+LOAD_VMEM = 36 * MIB
 F32 = jnp.float32
 BF16 = jnp.bfloat16
 
@@ -582,7 +582,7 @@
         keep_b = [[parts_b[0]] + swap(parts_b[1:], number, True)]
     (pooled,) = next_split([group_a] + keep_b, len(stages) - 1, 0, columns)
 
-    staged = (agg_out, nb_query, nb_key)
+    staged = (agg_out, nb_query)
     pooled, where = barrier((pooled, where))
     bias, *staged = pl.pallas_call(
         functools.partial(stage_kernel, rows, columns, len(staged)),
@@ -617,7 +617,7 @@
     far, across, bias = barrier((far, across, bias))
     window = [pooled, far, near, across]
     far_late = partner(far, "lat")
-    last = (nb_value, nb_out)
+    last = (nb_key, nb_value, nb_out)
     last, _ = barrier((last, far))
     last = pl.pallas_call(
         functools.partial(load_kernel, len(last)),
@@ -633,9 +633,9 @@
     )(*last)
 
     gain = norm_gain.reshape(1, width)
-    w_agg, w_query, w_key = staged
+    w_agg, w_query = staged
     across, last = barrier((across, last))
-    w_value, w_out = last
+    w_key, w_value, w_out = last
     late = [far_late, partner(across, "core")]
     early = len(window) * patch
     tall = jax.ShapeDtypeStruct((QROWS, width), BF16)

time: 55.3 us -> 55.3 us (level)
    pallas_call x1, Pallas kernels: 3.7 us -> 3.06 us  [on_device(): pl.pallas_call(functools.partial(stage_kernel, rows, columns, len(staged)...]
  transfers between devices with their start and end apart: 16 -> 16, of which waited for: 6 -> 6; matrix products, arithmetic and copies ran while one was open for 0% -> 0% of each run, Pallas kernels for 22% -> 21%
where the time goes in v7:
time: 55.3 us; the launch traced here: 55.1 us
  Pallas kernels  28.4 us (51%)
  starting transfers between devices  18.9 us (34%)
  waiting for transfers between devices  6.83 us (12%)
  local copies, waits for them, and re-layouts  0.73 us (1%)
    ppermute x11, starting transfers between devices, exchange(): lax.ppermute(array, ('var', 'lon'), [(i, moved(i)) for i in range(devices)])  14.9 us
    pallas_call x1, Pallas kernels, lead_pool(): pl.pallas_call(functools.partial(lead_kernel, heads, head_dim, lead_rows,...  10 us
    ppermute x11, waiting for transfers between devices, exchange(): lax.ppermute(array, ('var', 'lon'), [(i, moved(i)) for i in range(devices)])  5.07 us
    pallas_call x2, Pallas kernels, pool(): pl.pallas_call(functools.partial(pool_kernel, heads, head_dim, row, tiles...  4.91 us
    ppermute x5, starting transfers between devices, partner(): return lax.ppermute(array, ('var', 'lat', 'lon'), pairs)  3.97 us
    pallas_call x1, Pallas kernels, on_device(): pl.pallas_call(functools.partial(stage_kernel, rows, columns, len(staged)...  3.06 us
    pallas_call x1, Pallas kernels, on_device(): pl.pallas_call(functools.partial(attend_kernel, heads, len(late)), in_spe...  3.06 us
    pallas_call x1, Pallas kernels, lead_pool(): pl.pallas_call(functools.partial(pre_kernel, heads, head_dim), in_specs=[...  2.74 us
  transfers between devices with their start and end apart: 16, of which 6 were waited for; matrix products, arithmetic and copies ran while one was open for 0% of the time, Pallas kernels for 21%

profile of v7, /device:TPU:0, one launch (start us, length us, event | category | flops | bytes accessed | tf_op | source)
XLA Modules:
  0.0 55.1 jit_solution(888434070044716637)
XLA Ops:
  0.0 0.0 copy-start.5
  0.0 0.7 %copy-done.5 = f32[16,64]{1,0:T(8,128)S(1)} copy-done((f32[16,64]{1,0:T(8,128)S(1)}, f32[16,64]{1,0:T(8,128)}, u32[]{:S(2)}) %copy-start.5) | copy-done | bytes 4120
  0.7 2.7 %pre.1 = (bf16[1024,128]{1,0:T(8,128)(2,1)S(1)}, bf16[1024,1024]{1,0:T(8,128)(2,1)S(1)}, bf16[8,96,1024]{2,1,0:T(8,128)(2,1)S(1)}) custom-call(bf16[8,6,96,1024]{3,2,1,0:T(8,128)(2,1)} %refs_1_.2, bf16[1024,1024]{1,0:T(8,128)(2,1)} %value_ref.1, f32[16,64]{1,0:T(8,128)S(1)} %copy-done.5, bf16[1024,1024]{1,0:T(8,128)(2,1)} %key_ref.1), custom_call_target="tpu_custom_call" | custom-call | tf_op jit(solution)/shard_map/pre/pallas_call | solution.py:474
  3.4 10.0 %lead.1 = (bf16[4,48,1152]{2,1,0:T(8,128)(2,1)S(1)}, bf16[4,48,1152]{2,1,0:T(8,128)(2,1)S(1)}, bf16[8,2,96,1024]{3,2,1,0:T(8,128)(2,1)S(1)}) custom-call(s32[1]{0:T(128)} %bitcast.refs_0_, bf16[8,6,96,1024]{3,2,1,0:T(8,128)(2,1)} %refs_1_.2, bf16[8,96,1024]{2,1,0:T(8,128)(2,1)S(1)} %get-tuple-element.61.refs_2_, ...), custom_call_target="tpu_custom_call" | custom-call | flops 9663676416 | bytes 6291456 | tf_op jit(solution)/shard_map/lead/pallas_call | solution.py:489
  13.4 0.5 collective-permute-start
  14.0 2.5 %pool.2 = (bf16[1,48,1152]{2,1,0:T(8,128)(2,1)S(1)}, bf16[1,48,1152]{2,1,0:T(8,128)(2,1)S(1)}) custom-call(s32[1]{0:T(128)} %bitcast.refs_0_, bf16[8,2,96,1024]{3,2,1,0:T(8,128)(2,1)S(1)} %get-tuple-element.74.refs_1_, bf16[1024,1024]{1,0:T(8,128)(2,1)S(1)} %get-tuple-element.62.refs_3_.refs_2_, bf16[1024,128]{1,0:T(8,128)(2,1)S(1)} %get-tuple-element.77.refs_4_.refs_3_), custom_call_target="tpu_custom_call" | custom-call | flops 2415919104 | bytes 1572864 | tf_op jit(solution)/shard_map/pool/pallas_call | solution.py:506
  16.4 0.1 collective-permute-start.2
  16.6 0.0 collective-permute-done.refs_1_
  16.6 0.7 %merge.5 = (bf16[4,24,1152]{2,1,0:T(8,128)(2,1)S(1)}, bf16[4,24,1152]{2,1,0:T(8,128)(2,1)S(1)}) custom-call(bf16[4,48,1152]{2,1,0:T(8,128)(2,1)S(1)} %get-tuple-element.64.refs_0_, bf16[4,48,1152]{2,1,0:T(8,128)(2,1)S(1)} %collective-permute-done.refs_1_), custom_call_target="tpu_custom_call" | custom-call | flops 100663296 | bytes 1572864 | tf_op jit(solution)/shard_map/merge/pallas_call | solution.py:290
  17.2 0.0 copy-start.3
  17.2 0.0 copy-start.6
  17.2 0.0 copy-start.7
  17.2 3.0 %collective-permute-start.1 = (bf16[4,24,1152]{2,1,0:T(8,128)(2,1)S(1)}, bf16[4,24,1152]{2,1,0:T(8,128)(2,1)S(1)}, u32[]{:S(2)}, u32[]{:S(2)}) collective-permute-start(bf16[4,24,1152]{2,1,0:T(8,128)(2,1)S(1)} %get-tuple-element.69), channel_id=1, source_target_pairs={{0,2},{1,3},{2,0},{3,1},{8,10},{9,11},{10,8},{11,9},{16,18},{17,19... | collective-permute-start | bytes 663560 | tf_op jit(solution)/shard_map/ppermute | solution.py:521
  20.3 0.0 copy-start.2
  20.3 2.5 %pool.3 = (bf16[1,48,1152]{2,1,0:T(8,128)(2,1)S(1)}, bf16[1,48,1152]{2,1,0:T(8,128)(2,1)S(1)}) custom-call(s32[1]{0:T(128)} %bitcast.refs_0_, bf16[8,2,96,1024]{3,2,1,0:T(8,128)(2,1)S(1)} %get-tuple-element.74.refs_1_, bf16[1024,1024]{1,0:T(8,128)(2,1)S(1)} %get-tuple-element.62.refs_3_.refs_2_, bf16[1024,128]{1,0:T(8,128)(2,1)S(1)} %get-tuple-element.77.refs_4_.refs_3_), custom_call_target="tpu_custom_call" | custom-call | flops 2415919104 | bytes 1572864 | tf_op jit(solution)/shard_map/pool/pallas_call | solution.py:506
  22.7 0.1 collective-permute-start.3
  22.8 0.0 collective-permute-done.2.refs_1_
  22.8 1.3 %collective-permute-done.3.refs_3_ = bf16[1,48,1152]{2,1,0:T(8,128)(2,1)S(1)} collective-permute-done((bf16[1,48,1152]{2,1,0:T(8,128)(2,1)S(1)}, bf16[1,48,1152]{2,1,0:T(8,128)(2,1)S(1)}, u32[]{:S(2)}, u32[]{:S(2)}) %collective-permute-start.3) | collective-permute-done | bytes 110624 | tf_op jit(solution)/shard_map/ppermute | solution.py:521
  24.1 0.5 merge.7
  24.6 1.3 %collective-permute-done.1.refs_1_ = bf16[4,24,1152]{2,1,0:T(8,128)(2,1)S(1)} collective-permute-done((bf16[4,24,1152]{2,1,0:T(8,128)(2,1)S(1)}, bf16[4,24,1152]{2,1,0:T(8,128)(2,1)S(1)}, u32[]{:S(2)}, u32[]{:S(2)}) %collective-permute-start.1) | collective-permute-done | bytes 221216 | tf_op jit(solution)/shard_map/ppermute | solution.py:521
  25.9 0.4 merge.6
  26.3 1.8 %collective-permute-start.7 = (bf16[2,24,1152]{2,1,0:T(8,128)(2,1)S(1)}, bf16[2,24,1152]{2,1,0:T(8,128)(2,1)S(1)}, u32[]{:S(2)}, u32[]{:S(2)}) collective-permute-start(bf16[2,24,1152]{2,1,0:T(8,128)(2,1)S(1)} %get-tuple-element.87), channel_id=1, source_target_pairs={{0,2},{1,3},{2,0},{3,1},{8,10},{9,11},{10,8},{11,9},{16,18},{17,19... | collective-permute-start | bytes 331784 | tf_op jit(solution)/shard_map/ppermute | solution.py:521
  28.1 1.6 %collective-permute-start.4 = (bf16[24,1152]{1,0:T(8,128)(2,1)S(1)}, bf16[24,1152]{1,0:T(8,128)(2,1)S(1)}, u32[]{:S(2)}, u32[]{:S(2)}) collective-permute-start(bf16[24,1152]{1,0:T(8,128)(2,1)S(1)} %get-tuple-element.83), channel_id=1, source_target_pairs={{0,8},{1,9},{2,10},{3,11},{8,16},{9,17},{10,18},{11,19},{16,24},{1... | collective-permute-start | bytes 165896 | tf_op jit(solution)/shard_map/ppermute | solution.py:521
  29.7 2.6 %collective-permute-start.5 = (bf16[24,1152]{1,0:T(8,128)(2,1)S(1)}, bf16[24,1152]{1,0:T(8,128)(2,1)S(1)}, u32[]{:S(2)}, u32[]{:S(2)}) collective-permute-start(bf16[24,1152]{1,0:T(8,128)(2,1)S(1)} %get-tuple-element.84), channel_id=1, source_target_pairs={{0,16},{1,17},{2,18},{3,19},{8,24},{9,25},{10,26},{11,27},{16,0},{... | collective-permute-start | bytes 165896 | tf_op jit(solution)/shard_map/ppermute | solution.py:521
  32.3 1.3 %collective-permute-start.6 = (bf16[24,1152]{1,0:T(8,128)(2,1)S(1)}, bf16[24,1152]{1,0:T(8,128)(2,1)S(1)}, u32[]{:S(2)}, u32[]{:S(2)}) collective-permute-start(bf16[24,1152]{1,0:T(8,128)(2,1)S(1)} %get-tuple-element.85), channel_id=1, source_target_pairs={{0,24},{1,25},{2,26},{3,27},{8,0},{9,1},{10,2},{11,3},{16,8},{17,9... | collective-permute-start | bytes 165896 | tf_op jit(solution)/shard_map/ppermute | solution.py:521
  33.6 0.0 collective-permute-done.7.refs_1_
  33.6 0.4 merge.8
  34.0 0.7 %collective-permute-start.10 = (bf16[12,1152]{1,0:T(8,128)(2,1)S(1)}, bf16[12,1152]{1,0:T(8,128)(2,1)S(1)}, u32[]{:S(2)}, u32[]{:S(2)}) collective-permute-start(bf16[12,1152]{1,0:T(8,128)(2,1)S(1)} %get-tuple-element.91), channel_id=1, source_target_pairs={{0,8},{1,9},{2,10},{3,11},{8,16},{9,17},{10,18},{11,19},{16,24},{1... | collective-permute-start | bytes 82952 | tf_op jit(solution)/shard_map/ppermute | solution.py:521
  34.7 1.2 %collective-permute-start.8 = (bf16[12,1152]{1,0:T(8,128)(2,1)S(1)}, bf16[12,1152]{1,0:T(8,128)(2,1)S(1)}, u32[]{:S(2)}, u32[]{:S(2)}) collective-permute-start(bf16[12,1152]{1,0:T(8,128)(2,1)S(1)} %get-tuple-element.89), channel_id=1, source_target_pairs={{0,16},{1,17},{2,18},{3,19},{8,24},{9,25},{10,26},{11,27},{16,0},{... | collective-permute-start | bytes 82952 | tf_op jit(solution)/shard_map/ppermute | solution.py:521
  36.0 0.0 collective-permute-done.4.refs_1_
  36.0 1.9 %collective-permute-start.9 = (bf16[12,1152]{1,0:T(8,128)(2,1)S(1)}, bf16[12,1152]{1,0:T(8,128)(2,1)S(1)}, u32[]{:S(2)}, u32[]{:S(2)}) collective-permute-start(bf16[12,1152]{1,0:T(8,128)(2,1)S(1)} %get-tuple-element.90), channel_id=1, source_target_pairs={{0,24},{1,25},{2,26},{3,27},{8,0},{9,1},{10,2},{11,3},{16,8},{17,9... | collective-permute-start | bytes 82952 | tf_op jit(solution)/shard_map/ppermute | solution.py:521
  37.9 0.1 pad_add_fusion.refs_0_
  38.0 0.0 collective-permute-done.5.refs_2_
  38.0 0.0 collective-permute-done.6.refs_3_
  38.0 1.9 %collective-permute-done.10.refs_7_ = bf16[12,1152]{1,0:T(8,128)(2,1)S(1)} collective-permute-done((bf16[12,1152]{1,0:T(8,128)(2,1)S(1)}, bf16[12,1152]{1,0:T(8,128)(2,1)S(1)}, u32[]{:S(2)}, u32[]{:S(2)}) %collective-permute-start.10) | collective-permute-done | bytes 27680 | tf_op jit(solution)/shard_map/ppermute | solution.py:521
  39.9 0.5 collective-permute-done.8.refs_5_
  40.5 0.0 collective-permute-done.9.refs_6_
  40.5 0.5 merge.9.refs_0_
  41.0 0.1 collective-permute-start.11
  41.1 1.6 %collective-permute-start.12 = (bf16[36,1024]{1,0:T(8,128)(2,1)S(1)}, bf16[36,1024]{1,0:T(8,128)(2,1)S(1)}, u32[]{:S(2)}, u32[]{:S(2)}) collective-permute-start(bf16[36,1024]{1,0:T(8,128)(2,1)S(1)} %merge.9.refs_0_), channel_id=1, source_target_pairs={{4,0},{5,1},{6,2},{7,3},{0,4},{1,5},{2,6},{3,7},{12,8},{13,9},{14,... | collective-permute-start | bytes 221192 | tf_op jit(solution)/shard_map/ppermute | solution.py:612
  42.7 0.7 %collective-permute-start.15 = (bf16[36,1024]{1,0:T(8,128)(2,1)S(1)}, bf16[36,1024]{1,0:T(8,128)(2,1)S(1)}, u32[]{:S(2)}, u32[]{:S(2)}) collective-permute-start(bf16[36,1024]{1,0:T(8,128)(2,1)S(1)} %merge.9.refs_0_), channel_id=1, source_target_pairs={{1,0},{0,1},{3,2},{2,3},{5,4},{4,5},{7,6},{6,7},{9,8},{8,9},{11,10... | collective-permute-start | bytes 221192 | tf_op jit(solution)/shard_map/ppermute | solution.py:612
  43.4 0.0 copy-done.3
  43.4 0.0 copy-done.6
  43.4 0.0 copy-done.7
  43.4 0.0 copy-start
  43.4 0.0 copy-start.1
  43.4 3.1 %stage.1 = (f32[16,48,216]{2,1,0:T(8,128)S(1)}, bf16[1024,1024]{1,0:T(8,128)(2,1)S(1)}, bf16[1024,1024]{1,0:T(8,128)(2,1)S(1)}) custom-call(s32[2]{0:T(128)S(1)} %pad_add_fusion.refs_0_, s32[4,216]{1,0:T(4,128)S(1)} %copy-done.7, s32[12,96]{1,0:T(8,128)S(1)} %copy-done.6, f32[13,16,13]{2,1,0:T(8,128)S(1)} %bitcast.4, bf16[1024,1024]{1,0:T(8,128)(2,1)} %refs_4_.1, ...), custom_call_target="tpu_custom_call" | custom-call | flops 1000 | bytes 10485760 | tf_op jit(solution)/shard_map/stage/pallas_call | solution.py:587
  46.5 1.2 %collective-permute-done.11.refs_1_ = bf16[36,1024]{1,0:T(8,128)(2,1)S(1)} collective-permute-done((bf16[36,1024]{1,0:T(8,128)(2,1)S(1)}, bf16[36,1024]{1,0:T(8,128)(2,1)S(1)}, u32[]{:S(2)}, u32[]{:S(2)}) %collective-permute-start.11) | collective-permute-done | bytes 73760 | tf_op jit(solution)/shard_map/ppermute | solution.py:612
  47.6 0.0 collective-permute-done.12.refs_3_
  47.6 0.0 copy-start.4
  47.6 1.5 %collective-permute-start.13 = (bf16[36,1024]{1,0:T(8,128)(2,1)S(1)}, bf16[36,1024]{1,0:T(8,128)(2,1)S(1)}, u32[]{:S(2)}, u32[]{:S(2)}) collective-permute-start(bf16[36,1024]{1,0:T(8,128)(2,1)S(1)} %collective-permute-done.11.refs_1_), channel_id=1, source_target_pairs={{4,0},{5,1},{6,2},{7,3},{0,4},{1,5},{2,6},{3,7},{12,8},{13,9},{14,... | collective-permute-start | bytes 221192 | tf_op jit(solution)/shard_map/ppermute | solution.py:612
  49.1 0.0 copy-done.2
  49.1 0.0 copy-done
  49.2 0.0 copy-done.1
  49.2 0.5 load.1
  49.6 0.1 collective-permute-start.14
  49.7 0.0 collective-permute-done.15.refs_2_
  49.7 0.0 copy-done.4
  49.7 1.7 %project.1 = (bf16[48,1024]{1,0:T(8,128)(2,1)S(1)}, bf16[48,1024]{1,0:T(8,128)(2,1)S(1)}, bf16[144,1024]{1,0:T(8,128)(2,1)S(1)}, bf16[144,1024]{1,0:T(8,128)(2,1)S(1)}) custom-call(bf16[36,1024]{1,0:T(8,128)(2,1)S(1)} %merge.9.refs_0_, bf16[36,1024]{1,0:T(8,128)(2,1)S(1)} %collective-permute-done.11.refs_1_, ...), custom_call_target="tpu_custom_call" | custom-call | flops 905969664 | bytes 8388608 | tf_op jit(solution)/shard_map/project/pallas_call | solution.py:643
  51.5 0.0 collective-permute-done.14.refs_1_
  51.5 0.6 %collective-permute-done.13.refs_0_ = bf16[36,1024]{1,0:T(8,128)(2,1)S(1)} collective-permute-done((bf16[36,1024]{1,0:T(8,128)(2,1)S(1)}, bf16[36,1024]{1,0:T(8,128)(2,1)S(1)}, u32[]{:S(2)}, u32[]{:S(2)}) %collective-permute-start.13) | collective-permute-done | bytes 73760 | tf_op jit(solution)/shard_map/ppermute | solution.py:612
  52.1 3.1 %attend.1 = bf16[6,6,1024]{2,1,0:T(8,128)(2,1)} custom-call(bf16[36,1024]{1,0:T(8,128)(2,1)S(1)} %collective-permute-done.13.refs_0_, bf16[36,1024]{1,0:T(8,128)(2,1)S(1)} %collective-permute-done.14.refs_1_, f32[1,1024]{1,0:T(1,128)S(1)} %bitcast.6, bf16[1024,1024]{1,0:T(8,128)(2,1)S(1)} %get-tuple-element.107.refs_5_.refs_3_, ...), custom_call_target="tpu_custom_call" | custom-call | tf_op jit(solution)/shard_map/attend/pallas_call | solution.py:655
Async XLA Ops:
  0.0 0.7 %copy-start.5 = (f32[16,64]{1,0:T(8,128)S(1)}, f32[16,64]{1,0:T(8,128)}, u32[]{:S(2)}) copy-start(f32[16,64]{1,0:T(8,128)} %query_ref.1) | copy-start | bytes 12292
  13.4 3.1 %collective-permute-start = (bf16[4,48,1152]{2,1,0:T(8,128)(2,1)S(1)}, bf16[4,48,1152]{2,1,0:T(8,128)(2,1)S(1)}, u32[]{:S(2)}, u32[]{:S(2)}) collective-permute-start(bf16[4,48,1152]{2,1,0:T(8,128)(2,1)S(1)} %get-tuple-element.65), channel_id=1, source_target_pairs={{0,1},{1,0},{2,3},{3,2},{8,9},{9,8},{10,11},{11,10},{16,17},{17,16... | collective-permute-start | bytes 1327112 | tf_op jit(solution)/shard_map/ppermute | solution.py:521
  16.4 6.4 %collective-permute-start.2 = (bf16[1,48,1152]{2,1,0:T(8,128)(2,1)S(1)}, bf16[1,48,1152]{2,1,0:T(8,128)(2,1)S(1)}, u32[]{:S(2)}, u32[]{:S(2)}) collective-permute-start(bf16[1,48,1152]{2,1,0:T(8,128)(2,1)S(1)} %get-tuple-element.76), channel_id=1, source_target_pairs={{0,1},{1,0},{2,3},{3,2},{8,9},{9,8},{10,11},{11,10},{16,17},{17,16... | collective-permute-start | bytes 331784 | tf_op jit(solution)/shard_map/ppermute | solution.py:521
  17.2 26.2 %copy-start.3 = (f32[16,13,13]{2,0,1:T(8,128)S(1)}, f32[16,13,13]{2,0,1:T(8,128)}, u32[]{:S(2)}) copy-start(f32[16,13,13]{2,0,1:T(8,128)} %param.23) | copy-start | bytes 32452
  17.2 26.2 %copy-start.6 = (s32[12,96]{1,0:T(8,128)S(1)}, s32[12,96]{1,0:T(8,128)}, u32[]{:S(2)}) copy-start(s32[12,96]{1,0:T(8,128)} %refs_2_.1) | copy-start | bytes 13828
  17.2 26.1 %copy-start.7 = (s32[4,216]{1,0:T(4,128)S(1)}, s32[4,216]{1,0:T(4,128)}, u32[]{:S(2)}) copy-start(s32[4,216]{1,0:T(4,128)} %constant.16.clone.refs_1_) | copy-start | bytes 10372
  17.2 8.6 %collective-permute-start.1 = (bf16[4,24,1152]{2,1,0:T(8,128)(2,1)S(1)}, bf16[4,24,1152]{2,1,0:T(8,128)(2,1)S(1)}, u32[]{:S(2)}, u32[]{:S(2)}) collective-permute-start(bf16[4,24,1152]{2,1,0:T(8,128)(2,1)S(1)} %get-tuple-element.69), channel_id=1, source_target_pairs={{0,2},{1,3},{2,0},{3,1},{8,10},{9,11},{10,8},{11,9},{16,18},{17,19... | collective-permute-start | bytes 663560 | tf_op jit(solution)/shard_map/ppermute | solution.py:521
  20.3 28.9 %copy-start.2 = (bf16[1024,1024]{1,0:T(8,128)(2,1)S(1)}, bf16[1024,1024]{1,0:T(8,128)(2,1)}, u32[]{:S(2)}) copy-start(bf16[1024,1024]{1,0:T(8,128)(2,1)} %refs_2_.2) | copy-start | bytes 6291460
  22.7 1.4 %collective-permute-start.3 = (bf16[1,48,1152]{2,1,0:T(8,128)(2,1)S(1)}, bf16[1,48,1152]{2,1,0:T(8,128)(2,1)S(1)}, u32[]{:S(2)}, u32[]{:S(2)}) collective-permute-start(bf16[1,48,1152]{2,1,0:T(8,128)(2,1)S(1)} %get-tuple-element.79), channel_id=1, source_target_pairs={{0,1},{1,0},{2,3},{3,2},{8,9},{9,8},{10,11},{11,10},{16,17},{17,16... | collective-permute-start | bytes 331784 | tf_op jit(solution)/shard_map/ppermute | solution.py:521
  26.3 7.3 %collective-permute-start.7 = (bf16[2,24,1152]{2,1,0:T(8,128)(2,1)S(1)}, bf16[2,24,1152]{2,1,0:T(8,128)(2,1)S(1)}, u32[]{:S(2)}, u32[]{:S(2)}) collective-permute-start(bf16[2,24,1152]{2,1,0:T(8,128)(2,1)S(1)} %get-tuple-element.87), channel_id=1, source_target_pairs={{0,2},{1,3},{2,0},{3,1},{8,10},{9,11},{10,8},{11,9},{16,18},{17,19... | collective-permute-start | bytes 331784 | tf_op jit(solution)/shard_map/ppermute | solution.py:521
  28.1 7.9 %collective-permute-start.4 = (bf16[24,1152]{1,0:T(8,128)(2,1)S(1)}, bf16[24,1152]{1,0:T(8,128)(2,1)S(1)}, u32[]{:S(2)}, u32[]{:S(2)}) collective-permute-start(bf16[24,1152]{1,0:T(8,128)(2,1)S(1)} %get-tuple-element.83), channel_id=1, source_target_pairs={{0,8},{1,9},{2,10},{3,11},{8,16},{9,17},{10,18},{11,19},{16,24},{1... | collective-permute-start | bytes 165896 | tf_op jit(solution)/shard_map/ppermute | solution.py:521
  29.7 8.3 %collective-permute-start.5 = (bf16[24,1152]{1,0:T(8,128)(2,1)S(1)}, bf16[24,1152]{1,0:T(8,128)(2,1)S(1)}, u32[]{:S(2)}, u32[]{:S(2)}) collective-permute-start(bf16[24,1152]{1,0:T(8,128)(2,1)S(1)} %get-tuple-element.84), channel_id=1, source_target_pairs={{0,16},{1,17},{2,18},{3,19},{8,24},{9,25},{10,26},{11,27},{16,0},{... | collective-permute-start | bytes 165896 | tf_op jit(solution)/shard_map/ppermute | solution.py:521
  32.3 5.7 %collective-permute-start.6 = (bf16[24,1152]{1,0:T(8,128)(2,1)S(1)}, bf16[24,1152]{1,0:T(8,128)(2,1)S(1)}, u32[]{:S(2)}, u32[]{:S(2)}) collective-permute-start(bf16[24,1152]{1,0:T(8,128)(2,1)S(1)} %get-tuple-element.85), channel_id=1, source_target_pairs={{0,24},{1,25},{2,26},{3,27},{8,0},{9,1},{10,2},{11,3},{16,8},{17,9... | collective-permute-start | bytes 165896 | tf_op jit(solution)/shard_map/ppermute | solution.py:521
  34.0 5.9 %collective-permute-start.10 = (bf16[12,1152]{1,0:T(8,128)(2,1)S(1)}, bf16[12,1152]{1,0:T(8,128)(2,1)S(1)}, u32[]{:S(2)}, u32[]{:S(2)}) collective-permute-start(bf16[12,1152]{1,0:T(8,128)(2,1)S(1)} %get-tuple-element.91), channel_id=1, source_target_pairs={{0,8},{1,9},{2,10},{3,11},{8,16},{9,17},{10,18},{11,19},{16,24},{1... | collective-permute-start | bytes 82952 | tf_op jit(solution)/shard_map/ppermute | solution.py:521
  34.7 5.7 %collective-permute-start.8 = (bf16[12,1152]{1,0:T(8,128)(2,1)S(1)}, bf16[12,1152]{1,0:T(8,128)(2,1)S(1)}, u32[]{:S(2)}, u32[]{:S(2)}) collective-permute-start(bf16[12,1152]{1,0:T(8,128)(2,1)S(1)} %get-tuple-element.89), channel_id=1, source_target_pairs={{0,16},{1,17},{2,18},{3,19},{8,24},{9,25},{10,26},{11,27},{16,0},{... | collective-permute-start | bytes 82952 | tf_op jit(solution)/shard_map/ppermute | solution.py:521
  36.0 4.5 %collective-permute-start.9 = (bf16[12,1152]{1,0:T(8,128)(2,1)S(1)}, bf16[12,1152]{1,0:T(8,128)(2,1)S(1)}, u32[]{:S(2)}, u32[]{:S(2)}) collective-permute-start(bf16[12,1152]{1,0:T(8,128)(2,1)S(1)} %get-tuple-element.90), channel_id=1, source_target_pairs={{0,24},{1,25},{2,26},{3,27},{8,0},{9,1},{10,2},{11,3},{16,8},{17,9... | collective-permute-start | bytes 82952 | tf_op jit(solution)/shard_map/ppermute | solution.py:521
  41.0 6.6 %collective-permute-start.11 = (bf16[36,1024]{1,0:T(8,128)(2,1)S(1)}, bf16[36,1024]{1,0:T(8,128)(2,1)S(1)}, u32[]{:S(2)}, u32[]{:S(2)}) collective-permute-start(bf16[36,1024]{1,0:T(8,128)(2,1)S(1)} %merge.9.refs_0_), channel_id=1, source_target_pairs={{27,0},{2,1},{1,2},{8,3},{31,4},{6,5},{5,6},{12,7},{3,8},{10,9},{9... | collective-permute-start | bytes 221192 | tf_op jit(solution)/shard_map/ppermute | solution.py:612
  41.1 6.5 %collective-permute-start.12 = (bf16[36,1024]{1,0:T(8,128)(2,1)S(1)}, bf16[36,1024]{1,0:T(8,128)(2,1)S(1)}, u32[]{:S(2)}, u32[]{:S(2)}) collective-permute-start(bf16[36,1024]{1,0:T(8,128)(2,1)S(1)} %merge.9.refs_0_), channel_id=1, source_target_pairs={{4,0},{5,1},{6,2},{7,3},{0,4},{1,5},{2,6},{3,7},{12,8},{13,9},{14,... | collective-permute-start | bytes 221192 | tf_op jit(solution)/shard_map/ppermute | solution.py:612
  42.7 7.0 %collective-permute-start.15 = (bf16[36,1024]{1,0:T(8,128)(2,1)S(1)}, bf16[36,1024]{1,0:T(8,128)(2,1)S(1)}, u32[]{:S(2)}, u32[]{:S(2)}) collective-permute-start(bf16[36,1024]{1,0:T(8,128)(2,1)S(1)} %merge.9.refs_0_), channel_id=1, source_target_pairs={{1,0},{0,1},{3,2},{2,3},{5,4},{4,5},{7,6},{6,7},{9,8},{8,9},{11,10... | collective-permute-start | bytes 221192 | tf_op jit(solution)/shard_map/ppermute | solution.py:612
  43.4 5.8 %copy-start = (bf16[1024,1024]{1,0:T(8,128)(2,1)S(1)}, bf16[1024,1024]{1,0:T(8,128)(2,1)}, u32[]{:S(2)}) copy-start(bf16[1024,1024]{1,0:T(8,128)(2,1)} %refs_0_) | copy-start | bytes 6291460
  43.4 5.8 %copy-start.1 = (bf16[1024,1024]{1,0:T(8,128)(2,1)S(1)}, bf16[1024,1024]{1,0:T(8,128)(2,1)}, u32[]{:S(2)}) copy-start(bf16[1024,1024]{1,0:T(8,128)(2,1)} %refs_1_.3) | copy-start | bytes 6291460
  47.6 2.1 %copy-start.4 = (f32[1024]{0:T(1024)S(1)}, f32[1024]{0:T(1024)}, u32[]{:S(2)}) copy-start(f32[1024]{0:T(1024)} %param.18) | copy-start | bytes 12292
  47.6 4.4 %collective-permute-start.13 = (bf16[36,1024]{1,0:T(8,128)(2,1)S(1)}, bf16[36,1024]{1,0:T(8,128)(2,1)S(1)}, u32[]{:S(2)}, u32[]{:S(2)}) collective-permute-start(bf16[36,1024]{1,0:T(8,128)(2,1)S(1)} %collective-permute-done.11.refs_1_), channel_id=1, source_target_pairs={{4,0},{5,1},{6,2},{7,3},{0,4},{1,5},{2,6},{3,7},{12,8},{13,9},{14,... | collective-permute-start | bytes 221192 | tf_op jit(solution)/shard_map/ppermute | solution.py:612
  49.6 1.8 %collective-permute-start.14 = (bf16[36,1024]{1,0:T(8,128)(2,1)S(1)}, bf16[36,1024]{1,0:T(8,128)(2,1)S(1)}, u32[]{:S(2)}, u32[]{:S(2)}) collective-permute-start(bf16[36,1024]{1,0:T(8,128)(2,1)S(1)} %collective-permute-done.12.refs_3_), channel_id=1, source_target_pairs={{1,0},{0,1},{3,2},{2,3},{5,4},{4,5},{7,6},{6,7},{9,8},{8,9},{11,10... | collective-permute-start | bytes 221192 | tf_op jit(solution)/shard_map/ppermute | solution.py:612
